TPU v7x, 32 devices: a whole 2x2x4 slice. The times are simulated.
32 devices in a mesh: fsdp: 8 (over y, x, core), tensor: 4 (over z).
Axes of the slice: x: 2, y: 2, z: 4, core: 2. Of those that a mesh axis runs over, the one named last changes fastest.
Arguments:
- tokens: bfloat16 [24, 729, 1152], P('fsdp'), may hold values from -6 to 6
- slot_valid: int32 [24], P('fsdp'), may hold values 0 or 1
- ln1_gain: bfloat16 [1152], P('tensor'), may hold values from 0.5 to 1.5
- ln1_bias: bfloat16 [1152], P('tensor'), may hold values from -1.5 to 1.5
- w_qkv: bfloat16 [3, 1152, 1152], P(None, 'fsdp', 'tensor'), may hold values from -0.1875 to 0.1875
- b_query: bfloat16 [1152], P('tensor'), may hold values from -1.5 to 1.5
- b_value: bfloat16 [1152], P('tensor'), may hold values from -0.25 to 0.25
- w_out: bfloat16 [1152, 1152], P('tensor', 'fsdp'), may hold values from -3 to 3
- b_out: bfloat16 [1152], P('tensor'), may hold values from -1.5 to 1.5
- ln2_gain: bfloat16 [1152], P('tensor'), may hold values from 0.5 to 1.5
- ln2_bias: bfloat16 [1152], P('tensor'), may hold values from -1.5 to 1.5
- w_up: bfloat16 [1152, 4304], P('fsdp', 'tensor'), may hold values from -0.1875 to 0.1875
- b_up: bfloat16 [4304], P('tensor'), may hold values from -1.5 to 1.5
- w_down: bfloat16 [4304, 1152], P('tensor', 'fsdp'), may hold values from -0.09375 to 0.09375
- b_down: bfloat16 [1152], P('tensor'), may hold values from -1.5 to 1.5
- grad_out: bfloat16 [24, 729, 1152], P('fsdp'), may hold values from -6 to 6
Outputs:
- layer_out: bfloat16 [24, 729, 1152], P('fsdp')
- grad_tokens: float32 [24, 729, 1152], P('fsdp')
- grad_ln1_gain: float32 [1152], P('tensor')
- grad_ln1_bias: float32 [1152], P('tensor')
- grad_qkv: float32 [3, 1152, 1152], P(None, 'fsdp', 'tensor')
- grad_b_query: float32 [1152], P('tensor')
- grad_b_value: float32 [1152], P('tensor')
- grad_w_out: float32 [1152, 1152], P('tensor', 'fsdp')
- grad_b_out: float32 [1152], P('tensor')
- grad_ln2_gain: float32 [1152], P('tensor')
- grad_ln2_bias: float32 [1152], P('tensor')
- grad_w_up: float32 [1152, 4304], P('fsdp', 'tensor')
- grad_b_up: float32 [4304], P('tensor')
- grad_w_down: float32 [4304, 1152], P('tensor', 'fsdp')
- grad_b_down: float32 [1152], P('tensor')
- head_max: float32 [16], P('tensor')
- clipped_qk: float32 [2, 1152, 1152], P(None, 'fsdp', 'tensor')
- clipped_b_query: float32 [1152], P('tensor')
Inputs may be any that keep to these rules, and one draw needn't show every extreme that they name: `slot_valid`: 1 marks a slot that holds an image, 0 an empty slot.
All inputs are finite; a program needn't handle non-finite values. No bound on the sum of `slot_valid` on one device may be relied on, other than what follows from the above.
Results may differ from a plain program's by a relative error of at most 0.02.
Values may be sent and summed in bfloat16 or wider, within the bound.
A program may use at most 192 MiB of HBM per device.

v0:
```python
from functools import partial

import jax
import jax.numpy as jnp
from jax import lax
from jax.sharding import PartitionSpec as P

HD = 72
CLIP = 4


epsilon = 1e-06


def across(first_term, second_term):
    return lax.psum((first_term, second_term), "tensor")


def full_rows(part_rows):
    return lax.all_gather(part_rows, "tensor", axis=1, tiled=True)


def own_columns(whole_rows):
    return lax.psum_scatter(
        whole_rows.astype(jnp.bfloat16), "tensor", scatter_dimension=1, tiled=True
    ).astype(jnp.float32)


def norm_shard(row_block, gain_vec, shift_vec, full_width):
    totals, squares = across(jnp.sum(row_block, axis=1), jnp.sum(row_block * row_block, axis=1))
    centre = totals / full_width
    inverse = lax.rsqrt(squares / full_width - centre * centre + epsilon)
    normed = (row_block - centre[:, None]) * inverse[:, None]
    return (normed, inverse, normed * gain_vec + shift_vec)


def norm_back(upstream, normed, inverse, gain_vec, full_width):
    scaled = upstream * gain_vec
    first_sum, second_sum = across(jnp.sum(scaled, axis=1), jnp.sum(scaled * normed, axis=1))
    return (
        scaled - first_sum[:, None] / full_width - normed * (second_sum[:, None] / full_width)
    ) * inverse[:, None]


def on_device(
    tokens,
    slot_valid,
    ln1_gain,
    ln1_bias,
    w_qkv,
    b_query,
    b_value,
    w_out,
    b_out,
    ln2_gain,
    ln2_bias,
    w_up,
    b_up,
    w_down,
    b_down,
    grad_out,
):
    full_width = tokens.shape[2]
    own_width = ln1_gain.shape[0]
    own_start = lax.axis_index("tensor") * own_width
    length = tokens.shape[1]
    inner_local = b_query.shape[0]
    heads_local = inner_local // HD
    units_local = b_up.shape[0]
    score_scale = HD ** (-0.5)
    gain_one = ln1_gain.astype(jnp.float32)
    bias_one = ln1_bias.astype(jnp.float32)
    gain_two = ln2_gain.astype(jnp.float32)
    bias_two = ln2_bias.astype(jnp.float32)
    bias_out = b_out.astype(jnp.float32)
    bias_up = b_up.astype(jnp.float32)
    bias_down = b_down.astype(jnp.float32)
    qkv_bias = jnp.stack([b_query, jnp.zeros_like(b_query), b_value]).astype(jnp.float32)

    def micro_step(state_carry, inputs):
        big_grads, small_sums, head_peak = state_carry
        image_whole, upstream_whole, valid_flag = inputs
        keep_mask = valid_flag.astype(jnp.float32)
        qkv_full, out_full, up_full, down_full = (
            lax.all_gather(w_qkv, "fsdp", axis=1, tiled=True),
            lax.all_gather(w_out, "fsdp", axis=1, tiled=True),
            lax.all_gather(w_up, "fsdp", axis=0, tiled=True),
            lax.all_gather(w_down, "fsdp", axis=1, tiled=True),
        )
        image_float = lax.dynamic_slice_in_dim(image_whole, own_start, own_width, 1).astype(
            jnp.float32
        )
        normed_one, inverse_one, shifted_one = norm_shard(
            image_float, gain_one, bias_one, full_width
        )
        rows_one = full_rows(shifted_one.astype(jnp.bfloat16))
        projected = (
            jnp.einsum("sd,cdi->csi", rows_one, qkv_full, preferred_element_type=jnp.float32)
            + qkv_bias[:, None, :]
        )
        qkv_rows = projected.astype(jnp.bfloat16)
        query_rows = qkv_rows[0].reshape(length, heads_local, HD)
        key_rows = qkv_rows[1].reshape(length, heads_local, HD)
        value_rows = qkv_rows[2].reshape(length, heads_local, HD)
        scores = (
            jnp.einsum("qhd,khd->hqk", query_rows, key_rows, preferred_element_type=jnp.float32)
            * score_scale
        )
        head_peak = jnp.maximum(
            head_peak, jnp.where(valid_flag > 0, jnp.max(scores, axis=(1, 2)), -1e30)
        )
        row_peak = jnp.max(scores, axis=2, keepdims=True)
        exp_scores = jnp.exp(scores - row_peak)
        row_totals = jnp.sum(exp_scores, axis=2, keepdims=True)
        attn_probs = exp_scores / row_totals
        log_total = row_peak + jnp.log(row_totals)
        mixed_rows = jnp.einsum(
            "hqk,khd->qhd",
            attn_probs.astype(jnp.bfloat16),
            value_rows,
            preferred_element_type=jnp.float32,
        )
        heads_out = mixed_rows.reshape(length, inner_local).astype(jnp.bfloat16)
        attn_part = jnp.dot(heads_out, out_full, preferred_element_type=jnp.float32)
        residual = image_float + own_columns(attn_part) + bias_out
        normed_two, inverse_two, shifted_two = norm_shard(residual, gain_two, bias_two, full_width)
        rows_two = full_rows(shifted_two.astype(jnp.bfloat16))
        pre_act = jnp.dot(rows_two, up_full, preferred_element_type=jnp.float32) + bias_up
        activated = jax.nn.gelu(pre_act, approximate=True).astype(jnp.bfloat16)
        mlp_part = jnp.dot(activated, down_full, preferred_element_type=jnp.float32)
        layer_own = ((residual + own_columns(mlp_part) + bias_down) * keep_mask).astype(
            jnp.bfloat16
        )
        rows_upstream = upstream_whole * keep_mask.astype(jnp.bfloat16)
        upstream = lax.dynamic_slice_in_dim(rows_upstream, own_start, own_width, 1).astype(
            jnp.float32
        )
        grad_down = jnp.einsum(
            "sf,sd->fd", activated, rows_upstream, preferred_element_type=jnp.float32
        )
        grad_act = jnp.einsum(
            "sd,fd->sf", rows_upstream, down_full, preferred_element_type=jnp.float32
        )
        gelu_pull = jax.vjp(partial(jax.nn.gelu, approximate=True), pre_act)[1]
        grad_pre = gelu_pull(grad_act)[0].astype(jnp.bfloat16)
        grad_up = jnp.einsum("sd,sf->df", rows_two, grad_pre, preferred_element_type=jnp.float32)
        grad_two = own_columns(
            jnp.einsum("sf,df->sd", grad_pre, up_full, preferred_element_type=jnp.float32)
        )
        grad_resid = upstream + norm_back(grad_two, normed_two, inverse_two, gain_two, full_width)
        grad_attn = grad_resid.astype(jnp.bfloat16)
        rows_back = full_rows(grad_attn)
        grad_out_w = jnp.einsum(
            "si,sd->id", heads_out, rows_back, preferred_element_type=jnp.float32
        )
        grad_heads = (
            jnp.einsum("sd,id->si", rows_back, out_full, preferred_element_type=jnp.float32)
            .astype(jnp.bfloat16)
            .reshape(length, heads_local, HD)
        )
        scores_again = (
            jnp.einsum("qhd,khd->hqk", query_rows, key_rows, preferred_element_type=jnp.float32)
            * score_scale
        )
        probs_again = jnp.exp(scores_again - log_total)
        grad_probs = jnp.einsum(
            "qhd,khd->hqk", grad_heads, value_rows, preferred_element_type=jnp.float32
        )
        grad_value = jnp.einsum(
            "hqk,qhd->khd",
            probs_again.astype(jnp.bfloat16),
            grad_heads,
            preferred_element_type=jnp.float32,
        )
        row_dots = jnp.sum(probs_again * grad_probs, axis=2, keepdims=True)
        grad_scores = (probs_again * (grad_probs - row_dots) * score_scale).astype(jnp.bfloat16)
        grad_query = jnp.einsum(
            "hqk,khd->qhd", grad_scores, key_rows, preferred_element_type=jnp.float32
        )
        grad_key = jnp.einsum(
            "hqk,qhd->khd", grad_scores, query_rows, preferred_element_type=jnp.float32
        )
        grad_qkv_rows = jnp.stack(
            [
                grad_query.reshape(length, inner_local),
                grad_key.reshape(length, inner_local),
                grad_value.reshape(length, inner_local),
            ]
        ).astype(jnp.bfloat16)
        grad_qkv = jnp.einsum(
            "sd,csi->cdi", rows_one, grad_qkv_rows, preferred_element_type=jnp.float32
        )
        grad_one = own_columns(
            jnp.einsum("csi,cdi->sd", grad_qkv_rows, qkv_full, preferred_element_type=jnp.float32)
        )
        grad_image = grad_resid + norm_back(grad_one, normed_one, inverse_one, gain_one, full_width)
        layer_rows = lax.all_gather(layer_own, "tensor", axis=1, tiled=True)
        grad_rows = lax.all_gather(
            grad_image.astype(jnp.bfloat16), "tensor", axis=1, tiled=True
        ).astype(grad_image.dtype)
        step_grads = (grad_qkv, grad_out_w, grad_up, grad_down)
        big_grads = jax.tree.map(jnp.add, big_grads, step_grads)
        qkv_float = grad_qkv_rows.astype(jnp.float32)
        step_small = (
            jnp.sum(grad_one * normed_one, axis=0),
            jnp.sum(grad_one, axis=0),
            jnp.sum(grad_two * normed_two, axis=0),
            jnp.sum(grad_two, axis=0),
            jnp.sum(grad_attn.astype(jnp.float32), axis=0),
            jnp.sum(upstream, axis=0),
            jnp.sum(qkv_float[0], axis=0),
            jnp.sum(qkv_float[2], axis=0),
            jnp.sum(grad_pre.astype(jnp.float32), axis=0),
        )
        small_sums = jax.tree.map(jnp.add, small_sums, step_small)
        return ((big_grads, small_sums, head_peak), (layer_rows, grad_rows))

    rows_width = w_qkv.shape[1] * lax.axis_size("fsdp")
    big_start = (
        jnp.zeros((3, rows_width, inner_local), jnp.float32),
        jnp.zeros((inner_local, rows_width), jnp.float32),
        jnp.zeros((rows_width, units_local), jnp.float32),
        jnp.zeros((units_local, rows_width), jnp.float32),
    )
    feature_zero = jnp.zeros((own_width,), jnp.float32)
    inner_zero = jnp.zeros((inner_local,), jnp.float32)
    small_start = (
        feature_zero,
        feature_zero,
        feature_zero,
        feature_zero,
        feature_zero,
        feature_zero,
        inner_zero,
        inner_zero,
        jnp.zeros((units_local,), jnp.float32),
    )
    peak_start = jnp.full((heads_local,), -1e30, jnp.float32)
    final_carry, outputs = lax.scan(
        micro_step, (big_start, small_start, peak_start), (tokens, grad_out, slot_valid)
    )
    big_grads, small_sums, head_peak = final_carry
    layer_out, grad_tokens = outputs
    acc_qkv, acc_out, acc_up, acc_down = big_grads
    acc_qkv, acc_out, acc_up, acc_down = (
        lax.psum_scatter(
            acc_qkv.astype(jnp.bfloat16), "fsdp", scatter_dimension=1, tiled=True
        ).astype(jnp.float32),
        lax.psum_scatter(
            acc_out.astype(jnp.bfloat16), "fsdp", scatter_dimension=1, tiled=True
        ).astype(jnp.float32),
        lax.psum_scatter(
            acc_up.astype(jnp.bfloat16), "fsdp", scatter_dimension=0, tiled=True
        ).astype(jnp.float32),
        lax.psum_scatter(
            acc_down.astype(jnp.bfloat16), "fsdp", scatter_dimension=1, tiled=True
        ).astype(jnp.float32),
    )
    (
        sum_gain_one,
        sum_bias_one,
        sum_gain_two,
        sum_bias_two,
        sum_bias_out,
        sum_bias_down,
        sum_query,
        sum_value,
        sum_bias_up,
    ) = small_sums
    totals_small = lax.psum(
        (
            sum_gain_one,
            sum_bias_one,
            sum_gain_two,
            sum_bias_two,
            sum_bias_out,
            sum_bias_down,
            sum_query,
            sum_value,
            sum_bias_up,
        ),
        "fsdp",
    )
    head_top = lax.pmax(head_peak, "fsdp")
    factor = jnp.repeat(jnp.sqrt(CLIP / jnp.maximum(head_top, CLIP * 1.0)), HD)
    clipped = jnp.stack(
        [w_qkv[0].astype(jnp.float32) * factor, w_qkv[1].astype(jnp.float32) * factor]
    )
    return (
        layer_out,
        grad_tokens,
        totals_small[0],
        totals_small[1],
        acc_qkv,
        totals_small[6],
        totals_small[7],
        acc_out,
        totals_small[4],
        totals_small[2],
        totals_small[3],
        acc_up,
        totals_small[8],
        acc_down,
        totals_small[5],
        head_top,
        clipped,
        b_query.astype(jnp.float32) * factor,
    )


def solution(mesh):
    placed = (
        P("fsdp", None, None),
        P("fsdp"),
        P("tensor"),
        P("tensor"),
        P(None, "fsdp", "tensor"),
        P("tensor"),
        P("tensor"),
        P("tensor", "fsdp"),
        P("tensor"),
        P("tensor"),
        P("tensor"),
        P("fsdp", "tensor"),
        P("tensor"),
        P("tensor", "fsdp"),
        P("tensor"),
        P("fsdp", None, None),
    )
    return jax.shard_map(
        on_device,
        mesh=mesh,
        in_specs=placed,
        out_specs=(
            P("fsdp", None, None),
            P("fsdp", None, None),
            P("tensor"),
            P("tensor"),
            P(None, "fsdp", "tensor"),
            P("tensor"),
            P("tensor"),
            P("tensor", "fsdp"),
            P("tensor"),
            P("tensor"),
            P("tensor"),
            P("fsdp", "tensor"),
            P("tensor"),
            P("tensor", "fsdp"),
            P("tensor"),
            P("tensor"),
            P(None, "fsdp", "tensor"),
            P("tensor"),
        ),
        check_vma=False,
    )
```

profile of v0, /device:TPU:10, one launch (start us, length us, event | category | flops | bytes accessed | tf_op | source)
XLA Modules:
  0.0 1911.6 jit_solution(1927895957674716447)
XLA Ops:
  24.2 1703.2 %while.44 = (s32[]{:T(128)}, f32[3,1152,288]{1,2,0:T(8,128)}, f32[288,1152]{1,0:T(8,128)}, f32[1152,1076]{0,1:T(8,128)}, f32[1076,1152]{1,0:T(8,128)}, /*index=5...) while((s32[]{:T(128)}, f32[3,1152,288]{1,2,0:T(8,128)}, ...), condition=%wide.region_34.35_spmd.clone, body=%wide.region_0.34_spmd.clone.sunk | while | flops 18623879168 | bytes 442372352 | solution.py:239
  50.4 29.0 %all-gather.9.cloned.1.call-done = bf16[729,1152]{0,1:T(8,128)(2,1)} async-done(((bf16[729,288]{0,1:T(8,128)(2,1)}), bf16[729,1152]{0,1:T(8,128)(2,1)}) %all-gather.9.cloned.1.call-update) | async-done | bytes 1679632 | tf_op jit(solution)/shard_map/while/body/eval_jaxpr/all_gather | solution.py:20
  79.4 31.9 %all-gather.11.cloned.1.call-done = bf16[3,1152,288]{2,1,0:T(8,128)(2,1)} async-done(((bf16[3,144,288]{2,1,0:T(8,128)(2,1)}), bf16[3,1152,288]{2,1,0:T(8,128)(2,1)}) %all-gather.11.cloned.1.call-update) | async-done | bytes 1990672 | tf_op jit(solution)/shard_map/while/body/eval_jaxpr/all_gather | solution.py:85
  126.6 36.9 %reduce-scatter.25.cloned.1.call-done = bf16[729,288]{0,1:T(8,128)(2,1)} async-done(((bf16[729,1152]{0,1:T(8,128)(2,1)}), bf16[729,288]{0,1:T(8,128)(2,1)}) %reduce-scatter.25.cloned.1.call-update) | async-done | bytes 419920 | tf_op jit(solution)/shard_map/while/body/eval_jaxpr/reduce_scatter | solution.py:24
  195.5 41.2 %all-gather.13.cloned.1.call-done = bf16[729,1152]{0,1:T(8,128)(2,1)} async-done(((bf16[729,288]{0,1:T(8,128)(2,1)}), bf16[729,1152]{0,1:T(8,128)(2,1)}) %all-gather.13.cloned.1.call-update) | async-done | bytes 1679632 | tf_op jit(solution)/shard_map/while/body/eval_jaxpr/all_gather | solution.py:20
  243.0 25.5 %all-gather.17.cloned.1.call-done = bf16[1076,1152]{0,1:T(8,128)(2,1)} async-done(((bf16[1076,144]{0,1:T(8,128)(2,1)}), bf16[1076,1152]{0,1:T(8,128)(2,1)}) %all-gather.17.cloned.1.call-update) | async-done | bytes 2479120 | tf_op jit(solution)/shard_map/while/body/eval_jaxpr/all_gather | solution.py:88
  287.4 30.6 %reduce-scatter.27.cloned.1.call-done = bf16[729,288]{0,1:T(8,128)(2,1)} async-done(((bf16[729,1152]{0,1:T(8,128)(2,1)}), bf16[729,288]{0,1:T(8,128)(2,1)}) %reduce-scatter.27.cloned.1.call-update) | async-done | bytes 419920 | tf_op jit(solution)/shard_map/while/body/eval_jaxpr/reduce_scatter | solution.py:24
  318.0 39.8 %reduce-scatter.29.cloned.1.call-done = bf16[729,288]{0,1:T(8,128)(2,1)} async-done(((bf16[729,1152]{0,1:T(8,128)(2,1)}), bf16[729,288]{0,1:T(8,128)(2,1)}) %reduce-scatter.29.cloned.1.call-update) | async-done | bytes 419920 | tf_op jit(solution)/shard_map/while/body/eval_jaxpr/reduce_scatter | solution.py:24
  376.4 37.1 %all-gather.19.cloned.1.call-done = bf16[729,1152]{0,1:T(8,128)(2,1)} async-done(((bf16[729,288]{0,1:T(8,128)(2,1)}), bf16[729,1152]{0,1:T(8,128)(2,1)}) %all-gather.19.cloned.1.call-update) | async-done | bytes 1679632 | tf_op jit(solution)/shard_map/while/body/eval_jaxpr/all_gather | solution.py:20
  475.3 24.6 %reduce-scatter.31.cloned.1.call-done = bf16[729,288]{0,1:T(8,128)(2,1)} async-done(((bf16[729,1152]{0,1:T(8,128)(2,1)}), bf16[729,288]{0,1:T(8,128)(2,1)}) %reduce-scatter.31.cloned.1.call-update) | async-done | bytes 419920 | tf_op jit(solution)/shard_map/while/body/eval_jaxpr/reduce_scatter | solution.py:24
  554.1 28.3 %all-gather.23.cloned.1.call-done = bf16[729,1152]{0,1:T(8,128)(2,1)} async-done(((bf16[729,288]{0,1:T(8,128)(2,1)}), bf16[729,1152]{0,1:T(8,128)(2,1)}) %all-gather.23.cloned.1.call-update) | async-done | bytes 1679632 | tf_op jit(solution)/shard_map/while/body/eval_jaxpr/all_gather | solution.py:198
  618.2 27.2 %all-gather.9.cloned.1.call-done = bf16[729,1152]{0,1:T(8,128)(2,1)} async-done(((bf16[729,288]{0,1:T(8,128)(2,1)}), bf16[729,1152]{0,1:T(8,128)(2,1)}) %all-gather.9.cloned.1.call-update) | async-done | bytes 1679632 | tf_op jit(solution)/shard_map/while/body/eval_jaxpr/all_gather | solution.py:20
  645.4 31.8 %all-gather.11.cloned.1.call-done = bf16[3,1152,288]{2,1,0:T(8,128)(2,1)} async-done(((bf16[3,144,288]{2,1,0:T(8,128)(2,1)}), bf16[3,1152,288]{2,1,0:T(8,128)(2,1)}) %all-gather.11.cloned.1.call-update) | async-done | bytes 1990672 | tf_op jit(solution)/shard_map/while/body/eval_jaxpr/all_gather | solution.py:85
  692.4 36.9 %reduce-scatter.25.cloned.1.call-done = bf16[729,288]{0,1:T(8,128)(2,1)} async-done(((bf16[729,1152]{0,1:T(8,128)(2,1)}), bf16[729,288]{0,1:T(8,128)(2,1)}) %reduce-scatter.25.cloned.1.call-update) | async-done | bytes 419920 | tf_op jit(solution)/shard_map/while/body/eval_jaxpr/reduce_scatter | solution.py:24
  761.3 41.2 %all-gather.13.cloned.1.call-done = bf16[729,1152]{0,1:T(8,128)(2,1)} async-done(((bf16[729,288]{0,1:T(8,128)(2,1)}), bf16[729,1152]{0,1:T(8,128)(2,1)}) %all-gather.13.cloned.1.call-update) | async-done | bytes 1679632 | tf_op jit(solution)/shard_map/while/body/eval_jaxpr/all_gather | solution.py:20
  808.8 25.5 %all-gather.17.cloned.1.call-done = bf16[1076,1152]{0,1:T(8,128)(2,1)} async-done(((bf16[1076,144]{0,1:T(8,128)(2,1)}), bf16[1076,1152]{0,1:T(8,128)(2,1)}) %all-gather.17.cloned.1.call-update) | async-done | bytes 2479120 | tf_op jit(solution)/shard_map/while/body/eval_jaxpr/all_gather | solution.py:88
  853.3 30.5 %reduce-scatter.27.cloned.1.call-done = bf16[729,288]{0,1:T(8,128)(2,1)} async-done(((bf16[729,1152]{0,1:T(8,128)(2,1)}), bf16[729,288]{0,1:T(8,128)(2,1)}) %reduce-scatter.27.cloned.1.call-update) | async-done | bytes 419920 | tf_op jit(solution)/shard_map/while/body/eval_jaxpr/reduce_scatter | solution.py:24
  883.8 39.7 %reduce-scatter.29.cloned.1.call-done = bf16[729,288]{0,1:T(8,128)(2,1)} async-done(((bf16[729,1152]{0,1:T(8,128)(2,1)}), bf16[729,288]{0,1:T(8,128)(2,1)}) %reduce-scatter.29.cloned.1.call-update) | async-done | bytes 419920 | tf_op jit(solution)/shard_map/while/body/eval_jaxpr/reduce_scatter | solution.py:24
  942.1 37.1 %all-gather.19.cloned.1.call-done = bf16[729,1152]{0,1:T(8,128)(2,1)} async-done(((bf16[729,288]{0,1:T(8,128)(2,1)}), bf16[729,1152]{0,1:T(8,128)(2,1)}) %all-gather.19.cloned.1.call-update) | async-done | bytes 1679632 | tf_op jit(solution)/shard_map/while/body/eval_jaxpr/all_gather | solution.py:20
  1121.0 27.0 %all-gather.23.cloned.1.call-done = bf16[729,1152]{0,1:T(8,128)(2,1)} async-done(((bf16[729,288]{0,1:T(8,128)(2,1)}), bf16[729,1152]{0,1:T(8,128)(2,1)}) %all-gather.23.cloned.1.call-update) | async-done | bytes 1679632 | tf_op jit(solution)/shard_map/while/body/eval_jaxpr/all_gather | solution.py:198
  1183.5 27.2 %all-gather.9.cloned.1.call-done = bf16[729,1152]{0,1:T(8,128)(2,1)} async-done(((bf16[729,288]{0,1:T(8,128)(2,1)}), bf16[729,1152]{0,1:T(8,128)(2,1)}) %all-gather.9.cloned.1.call-update) | async-done | bytes 1679632 | tf_op jit(solution)/shard_map/while/body/eval_jaxpr/all_gather | solution.py:20
  1210.8 31.8 %all-gather.11.cloned.1.call-done = bf16[3,1152,288]{2,1,0:T(8,128)(2,1)} async-done(((bf16[3,144,288]{2,1,0:T(8,128)(2,1)}), bf16[3,1152,288]{2,1,0:T(8,128)(2,1)}) %all-gather.11.cloned.1.call-update) | async-done | bytes 1990672 | tf_op jit(solution)/shard_map/while/body/eval_jaxpr/all_gather | solution.py:85
  1258.0 36.8 %reduce-scatter.25.cloned.1.call-done = bf16[729,288]{0,1:T(8,128)(2,1)} async-done(((bf16[729,1152]{0,1:T(8,128)(2,1)}), bf16[729,288]{0,1:T(8,128)(2,1)}) %reduce-scatter.25.cloned.1.call-update) | async-done | bytes 419920 | tf_op jit(solution)/shard_map/while/body/eval_jaxpr/reduce_scatter | solution.py:24
  1326.8 41.4 %all-gather.13.cloned.1.call-done = bf16[729,1152]{0,1:T(8,128)(2,1)} async-done(((bf16[729,288]{0,1:T(8,128)(2,1)}), bf16[729,1152]{0,1:T(8,128)(2,1)}) %all-gather.13.cloned.1.call-update) | async-done | bytes 1679632 | tf_op jit(solution)/shard_map/while/body/eval_jaxpr/all_gather | solution.py:20
  1374.5 25.5 %all-gather.17.cloned.1.call-done = bf16[1076,1152]{0,1:T(8,128)(2,1)} async-done(((bf16[1076,144]{0,1:T(8,128)(2,1)}), bf16[1076,1152]{0,1:T(8,128)(2,1)}) %all-gather.17.cloned.1.call-update) | async-done | bytes 2479120 | tf_op jit(solution)/shard_map/while/body/eval_jaxpr/all_gather | solution.py:88
  1419.2 30.3 %reduce-scatter.27.cloned.1.call-done = bf16[729,288]{0,1:T(8,128)(2,1)} async-done(((bf16[729,1152]{0,1:T(8,128)(2,1)}), bf16[729,288]{0,1:T(8,128)(2,1)}) %reduce-scatter.27.cloned.1.call-update) | async-done | bytes 419920 | tf_op jit(solution)/shard_map/while/body/eval_jaxpr/reduce_scatter | solution.py:24
  1449.5 39.8 %reduce-scatter.29.cloned.1.call-done = bf16[729,288]{0,1:T(8,128)(2,1)} async-done(((bf16[729,1152]{0,1:T(8,128)(2,1)}), bf16[729,288]{0,1:T(8,128)(2,1)}) %reduce-scatter.29.cloned.1.call-update) | async-done | bytes 419920 | tf_op jit(solution)/shard_map/while/body/eval_jaxpr/reduce_scatter | solution.py:24
  1507.9 37.1 %all-gather.19.cloned.1.call-done = bf16[729,1152]{0,1:T(8,128)(2,1)} async-done(((bf16[729,288]{0,1:T(8,128)(2,1)}), bf16[729,1152]{0,1:T(8,128)(2,1)}) %all-gather.19.cloned.1.call-update) | async-done | bytes 1679632 | tf_op jit(solution)/shard_map/while/body/eval_jaxpr/all_gather | solution.py:20
  1686.9 27.0 %all-gather.23.cloned.1.call-done = bf16[729,1152]{0,1:T(8,128)(2,1)} async-done(((bf16[729,288]{0,1:T(8,128)(2,1)}), bf16[729,1152]{0,1:T(8,128)(2,1)}) %all-gather.23.cloned.1.call-update) | async-done | bytes 1679632 | tf_op jit(solution)/shard_map/while/body/eval_jaxpr/all_gather | solution.py:198
  1767.3 23.0 %all-reduce.4 = (f32[288]{0:T(512)}, f32[288]{0:T(512)}, f32[288]{0:T(512)}, f32[288]{0:T(512)}, f32[288]{0:T(512)}, /*index=5*/f32[288]{0:T(512)}, f32[288]{0:T(512)}, f32[1076]{0:T(1024)}, f32[288]{0:T(512)}) all-reduce(f32[288]{0:T(512)S(1)} %copy-done.58, f32[288]{0:T(512)S(1)} %copy-done.55, ...), channel_id=1, replica_groups=mesh['fsdp'=8,'tensor'=4] {'fsdp'}, use_global_device_ids=true, to_apply=%region_35.36 | all-reduce | flops 3380 | bytes 27040 | tf_op jit(solution)/shard_map/psum | solution.py:270
  1811.9 43.3 %reduce-scatter.21.cloned.1.call-done = bf16[144,1076]{1,0:T(8,128)(2,1)} async-done(((bf16[1152,1076]{1,0:T(8,128)(2,1)}), bf16[144,1076]{1,0:T(8,128)(2,1)}) %reduce-scatter.21.cloned.1.call-update) | async-done | bytes 309904
  1857.5 44.2 %reduce-scatter.23.cloned.1.call-done = bf16[144,1076]{1,0:T(8,128)(2,1)} async-done(((bf16[1152,1076]{1,0:T(8,128)(2,1)}), bf16[144,1076]{1,0:T(8,128)(2,1)}) %reduce-scatter.23.cloned.1.call-update) | async-done | bytes 309904
  (728 shorter events, 853.7 us)
Async XLA Ops:
  38.9 72.5 %all-gather.11.cloned.1.call-start = ((), (), s32[]{:S(2)}) async-start(), calls=%async_computation.13 | async-start | bytes 2985984 | tf_op jit(solution)/shard_map/while/body/eval_jaxpr/all_gather | solution.py:85
  39.6 123.9 %reduce-scatter.25.cloned.1.call-start = ((), (), s32[]{:S(2)}) async-start(), calls=%async_computation.14 | async-start | bytes 2211840 | tf_op jit(solution)/shard_map/while/body/eval_jaxpr/reduce_scatter | solution.py:24
  126.6 110.1 %all-gather.13.cloned.1.call-start = ((), (), s32[]{:S(2)}) async-start(), calls=%async_computation.15 | async-start | bytes 2211840 | tf_op jit(solution)/shard_map/while/body/eval_jaxpr/all_gather | solution.py:20
  177.9 90.6 %all-gather.17.cloned.1.call-start = ((), (), s32[]{:S(2)}) async-start(), calls=%async_computation.17 | async-start | bytes 2985984 | tf_op jit(solution)/shard_map/while/body/eval_jaxpr/all_gather | solution.py:88
  178.5 139.5 %reduce-scatter.27.cloned.1.call-start = ((), (), s32[]{:S(2)}) async-start(), calls=%async_computation.18 | async-start | bytes 2211840 | tf_op jit(solution)/shard_map/while/body/eval_jaxpr/reduce_scatter | solution.py:24
  280.5 77.4 %reduce-scatter.29.cloned.1.call-start = ((), (), s32[]{:S(2)}) async-start(), calls=%async_computation.19 | async-start | bytes 2211840 | tf_op jit(solution)/shard_map/while/body/eval_jaxpr/reduce_scatter | solution.py:24
  287.2 126.4 %all-gather.19.cloned.1.call-start = ((), (), s32[]{:S(2)}) async-start(), calls=%async_computation.20 | async-start | bytes 2211840 | tf_op jit(solution)/shard_map/while/body/eval_jaxpr/all_gather | solution.py:20
  375.1 124.7 %reduce-scatter.31.cloned.1.call-start = ((), (), s32[]{:S(2)}) async-start(), calls=%async_computation.21 | async-start | bytes 2211840 | tf_op jit(solution)/shard_map/while/body/eval_jaxpr/reduce_scatter | solution.py:24
  462.4 78.9 %all-gather.21.cloned.1.call-start = ((), (), s32[]{:S(2)}) async-start(), calls=%async_computation.22 | async-start | bytes 2211840 | tf_op jit(solution)/shard_map/while/body/eval_jaxpr/all_gather | solution.py:197
  463.2 119.1 %all-gather.23.cloned.1.call-start = ((), (), s32[]{:S(2)}) async-start(), calls=%async_computation.23 | async-start | bytes 2211840 | tf_op jit(solution)/shard_map/while/body/eval_jaxpr/all_gather | solution.py:198
  606.9 70.3 %all-gather.11.cloned.1.call-start = ((), (), s32[]{:S(2)}) async-start(), calls=%async_computation.13 | async-start | bytes 2985984 | tf_op jit(solution)/shard_map/while/body/eval_jaxpr/all_gather | solution.py:85
  607.5 121.9 %reduce-scatter.25.cloned.1.call-start = ((), (), s32[]{:S(2)}) async-start(), calls=%async_computation.14 | async-start | bytes 2211840 | tf_op jit(solution)/shard_map/while/body/eval_jaxpr/reduce_scatter | solution.py:24
  692.4 110.2 %all-gather.13.cloned.1.call-start = ((), (), s32[]{:S(2)}) async-start(), calls=%async_computation.15 | async-start | bytes 2211840 | tf_op jit(solution)/shard_map/while/body/eval_jaxpr/all_gather | solution.py:20
  743.7 90.6 %all-gather.17.cloned.1.call-start = ((), (), s32[]{:S(2)}) async-start(), calls=%async_computation.17 | async-start | bytes 2985984 | tf_op jit(solution)/shard_map/while/body/eval_jaxpr/all_gather | solution.py:88
  744.3 139.5 %reduce-scatter.27.cloned.1.call-start = ((), (), s32[]{:S(2)}) async-start(), calls=%async_computation.18 | async-start | bytes 2211840 | tf_op jit(solution)/shard_map/while/body/eval_jaxpr/reduce_scatter | solution.py:24
  846.3 77.2 %reduce-scatter.29.cloned.1.call-start = ((), (), s32[]{:S(2)}) async-start(), calls=%async_computation.19 | async-start | bytes 2211840 | tf_op jit(solution)/shard_map/while/body/eval_jaxpr/reduce_scatter | solution.py:24
  853.0 126.2 %all-gather.19.cloned.1.call-start = ((), (), s32[]{:S(2)}) async-start(), calls=%async_computation.20 | async-start | bytes 2211840 | tf_op jit(solution)/shard_map/while/body/eval_jaxpr/all_gather | solution.py:20
  940.7 124.8 %reduce-scatter.31.cloned.1.call-start = ((), (), s32[]{:S(2)}) async-start(), calls=%async_computation.21 | async-start | bytes 2211840 | tf_op jit(solution)/shard_map/while/body/eval_jaxpr/reduce_scatter | solution.py:24
  1028.0 78.9 %all-gather.21.cloned.1.call-start = ((), (), s32[]{:S(2)}) async-start(), calls=%async_computation.22 | async-start | bytes 2211840 | tf_op jit(solution)/shard_map/while/body/eval_jaxpr/all_gather | solution.py:197
  1028.9 119.1 %all-gather.23.cloned.1.call-start = ((), (), s32[]{:S(2)}) async-start(), calls=%async_computation.23 | async-start | bytes 2211840 | tf_op jit(solution)/shard_map/while/body/eval_jaxpr/all_gather | solution.py:198
  1172.8 121.9 %reduce-scatter.25.cloned.1.call-start = ((), (), s32[]{:S(2)}) async-start(), calls=%async_computation.14 | async-start | bytes 2211840 | tf_op jit(solution)/shard_map/while/body/eval_jaxpr/reduce_scatter | solution.py:24
  1257.9 110.3 %all-gather.13.cloned.1.call-start = ((), (), s32[]{:S(2)}) async-start(), calls=%async_computation.15 | async-start | bytes 2211840 | tf_op jit(solution)/shard_map/while/body/eval_jaxpr/all_gather | solution.py:20
  1309.1 90.9 %all-gather.17.cloned.1.call-start = ((), (), s32[]{:S(2)}) async-start(), calls=%async_computation.17 | async-start | bytes 2985984 | tf_op jit(solution)/shard_map/while/body/eval_jaxpr/all_gather | solution.py:88
  1309.7 139.8 %reduce-scatter.27.cloned.1.call-start = ((), (), s32[]{:S(2)}) async-start(), calls=%async_computation.18 | async-start | bytes 2211840 | tf_op jit(solution)/shard_map/while/body/eval_jaxpr/reduce_scatter | solution.py:24
  1412.0 77.4 %reduce-scatter.29.cloned.1.call-start = ((), (), s32[]{:S(2)}) async-start(), calls=%async_computation.19 | async-start | bytes 2211840 | tf_op jit(solution)/shard_map/while/body/eval_jaxpr/reduce_scatter | solution.py:24
  1418.7 126.4 %all-gather.19.cloned.1.call-start = ((), (), s32[]{:S(2)}) async-start(), calls=%async_computation.20 | async-start | bytes 2211840 | tf_op jit(solution)/shard_map/while/body/eval_jaxpr/all_gather | solution.py:20
  1506.6 124.8 %reduce-scatter.31.cloned.1.call-start = ((), (), s32[]{:S(2)}) async-start(), calls=%async_computation.21 | async-start | bytes 2211840 | tf_op jit(solution)/shard_map/while/body/eval_jaxpr/reduce_scatter | solution.py:24
  1593.9 78.9 %all-gather.21.cloned.1.call-start = ((), (), s32[]{:S(2)}) async-start(), calls=%async_computation.22 | async-start | bytes 2211840 | tf_op jit(solution)/shard_map/while/body/eval_jaxpr/all_gather | solution.py:197
  1594.8 119.1 %all-gather.23.cloned.1.call-start = ((), (), s32[]{:S(2)}) async-start(), calls=%async_computation.23 | async-start | bytes 2211840 | tf_op jit(solution)/shard_map/while/body/eval_jaxpr/all_gather | solution.py:198
  1730.2 78.8 %reduce-scatter.17.cloned.1.call-start = ((), (), s32[]{:S(2)}) async-start(), calls=%async_computation.8 | async-start | bytes 2322432
  1744.1 111.2 %reduce-scatter.21.cloned.1.call-start = ((), (), s32[]{:S(2)}) async-start(), calls=%async_computation.10 | async-start | bytes 2985984
  1750.1 151.6 %reduce-scatter.23.cloned.1.call-start = ((), (), s32[]{:S(2)}) async-start(), calls=%async_computation.11 | async-start | bytes 2985984
  (212 other events, 5234.7 us)
Sparse Core Ops, SparseCore 0:
  39.0 40.3 all-gather.8
  126.1 37.3 reduce-scatter.24
  165.3 30.1 all-gather.14
  197.5 39.1 all-gather.12
  238.4 30.0 all-gather.16
  280.5 37.3 reduce-scatter.26
  320.3 37.4 reduce-scatter.28
  375.2 38.3 all-gather.18
  462.5 37.2 reduce-scatter.30
  502.0 39.2 all-gather.20
  543.2 39.0 all-gather.22
  607.0 38.3 all-gather.8
  691.9 37.3 reduce-scatter.24
  731.1 30.1 all-gather.14
  763.3 39.1 all-gather.12
  804.3 30.0 all-gather.16
  846.4 37.3 reduce-scatter.26
  886.0 37.4 reduce-scatter.28
  940.8 38.3 all-gather.18
  1028.1 37.3 reduce-scatter.30
  1067.7 39.2 all-gather.20
  1108.9 39.0 all-gather.22
  1172.4 38.3 all-gather.8
  1257.3 37.3 reduce-scatter.24
  1296.6 30.1 all-gather.14
  1329.0 39.1 all-gather.12
  1412.1 37.3 reduce-scatter.26
  1451.8 37.4 reduce-scatter.28
  1506.7 38.3 all-gather.18
  1594.0 37.3 reduce-scatter.30
  1633.5 39.2 all-gather.20
  1674.7 39.0 all-gather.22
  (4 shorter events, 119.8 us)
Sparse Core Ops, SparseCore 1:
  1731.1 34.5 reduce-scatter.18
  1768.9 40.1 reduce-scatter.16
  1812.3 42.9 reduce-scatter.20
  1858.8 42.9 reduce-scatter.22
where the time goes:
time: 1920 us; the launch traced here: 1910 us
  waiting for transfers between devices  1170 us (61%)
  matrix products  313 us (16%)
  blocking collectives  188 us (10%)
  other arithmetic  112 us (6%)
  local copies, waits for them, and re-layouts  96.7 us (5%)
    reduce_scatter x12, waiting for transfers between devices, own_columns(): lax.psum_scatter(whole_rows.astype(jnp.bfloat16), 'tensor', scatter_dimen...  387 us
    all_gather x9, waiting for transfers between devices, full_rows(): return lax.all_gather(part_rows, 'tensor', axis=1, tiled=True)  319 us
    psum x12, blocking collectives, across(): return lax.psum((first_term, second_term), 'tensor')  122 us
    unnamed x8, waiting for transfers between devices  103 us
    all_gather x3, waiting for transfers between devices, micro_step(): lax.all_gather(w_qkv, 'fsdp', axis=1, tiled=True)  95.5 us
    all_gather x3, waiting for transfers between devices, micro_step(): lax.all_gather(grad_image.astype(jnp.bfloat16), 'tensor', axis=1, tiled=T...  82.3 us
    all_gather x3, waiting for transfers between devices, micro_step(): lax.all_gather(w_down, 'fsdp', axis=1, tiled=True)  76.4 us
    all_gather x3, waiting for transfers between devices, micro_step(): layer_rows = lax.all_gather(layer_own, 'tensor', axis=1, tiled=True)  61.8 us
  transfers between devices with their start and end apart: 40, of which 39 were waited for; matrix products, arithmetic and copies ran while one was open for 11% of the time, Pallas kernels for 0%

commit v1 on v0

v1 whole, which is shorter than its diff:
```python
from functools import partial

import jax
import jax.numpy as jnp
from jax import lax
from jax.experimental import pallas as pl
from jax.experimental.pallas import tpu as pltpu
from jax.sharding import PartitionSpec as P

HD = 72
CLIP = 4
EPS = 1e-06
F32 = jnp.float32
BF16 = jnp.bfloat16


def dot(a, b, ca, cb):
    return lax.dot_general(a, b, (((ca,), (cb,)), ((), ())), preferred_element_type=F32)


def attn_fwd_kernel(scale, qkv_ref, o_ref, p_ref, l_ref, m_ref):
    q, k, v = qkv_ref[0], qkv_ref[1], qkv_ref[2]
    st = dot(k, q, 0, 0) * scale
    peak = jnp.max(st, axis=0, keepdims=True)
    p = jnp.exp(st - peak)
    total = jnp.sum(p, axis=0, keepdims=True)
    pb = p.astype(BF16)
    p_ref[0] = pb
    o_ref[...] = (dot(v, pb, 1, 0) / total).astype(BF16)
    l_ref[0] = total
    m_ref[0] = jnp.broadcast_to(jnp.max(peak, axis=1, keepdims=True), m_ref.shape[1:])


def attn_fwd(qkv, heads):
    _, inner, length = qkv.shape
    return pl.pallas_call(
        partial(attn_fwd_kernel, HD**-0.5),
        grid=(heads,),
        in_specs=[pl.BlockSpec((3, HD, length), lambda h: (0, h, 0))],
        out_specs=[
            pl.BlockSpec((HD, length), lambda h: (h, 0)),
            pl.BlockSpec((1, length, length), lambda h: (h, 0, 0)),
            pl.BlockSpec((1, 1, length), lambda h: (h, 0, 0)),
            pl.BlockSpec((1, 1, 128), lambda h: (h, 0, 0)),
        ],
        out_shape=[
            jax.ShapeDtypeStruct((inner, length), BF16),
            jax.ShapeDtypeStruct((heads, length, length), BF16),
            jax.ShapeDtypeStruct((heads, 1, length), F32),
            jax.ShapeDtypeStruct((heads, 1, 128), F32),
        ],
        cost_estimate=pl.CostEstimate(
            flops=4 * heads * length * length * 256, bytes_accessed=2 * heads * length * length,
            transcendentals=heads * length * length),
        name="attn_fwd",
    )(qkv)


def attn_bwd_kernel(scale, qkv_ref, do_ref, o_ref, p_ref, l_ref, out_ref):
    q, k, v = qkv_ref[0], qkv_ref[1], qkv_ref[2]
    inv = 1.0 / l_ref[0]
    do = do_ref[...].astype(F32)
    dot_row = jnp.sum(do * o_ref[...].astype(F32), axis=0, keepdims=True) * inv
    dos = (do * inv).astype(BF16)
    p = p_ref[0]
    dp = dot(v, dos, 0, 0)
    ds = (p.astype(F32) * (dp - dot_row)).astype(BF16)
    out_ref[2] = dot(dos, p, 1, 1).astype(BF16)
    out_ref[1] = (dot(q, ds, 1, 1) * scale).astype(BF16)
    out_ref[0] = (dot(k, ds, 1, 0) * scale).astype(BF16)


def attn_bwd(qkv, do, o, p, l, heads):
    _, inner, length = qkv.shape
    return pl.pallas_call(
        partial(attn_bwd_kernel, HD**-0.5),
        grid=(heads,),
        in_specs=[
            pl.BlockSpec((3, HD, length), lambda h: (0, h, 0)),
            pl.BlockSpec((HD, length), lambda h: (h, 0)),
            pl.BlockSpec((HD, length), lambda h: (h, 0)),
            pl.BlockSpec((1, length, length), lambda h: (h, 0, 0)),
            pl.BlockSpec((1, 1, length), lambda h: (h, 0, 0)),
        ],
        out_specs=pl.BlockSpec((3, HD, length), lambda h: (0, h, 0)),
        out_shape=jax.ShapeDtypeStruct((3, inner, length), BF16),
        cost_estimate=pl.CostEstimate(
            flops=8 * heads * length * length * 256, bytes_accessed=2 * heads * length * length,
            transcendentals=0),
        name="attn_bwd",
    )(qkv, do, o, p, l)


def norm(rows, gain, shift):
    centre = jnp.mean(rows, axis=1, keepdims=True)
    centred = rows - centre
    inverse = lax.rsqrt(jnp.mean(centred * centred, axis=1, keepdims=True) + EPS)
    normed = centred * inverse
    return normed, inverse, (normed * gain + shift).astype(BF16)


def norm_back(dz, normed, inverse, gain):
    scaled = dz * gain
    first = jnp.mean(scaled, axis=1, keepdims=True)
    second = jnp.mean(scaled * normed, axis=1, keepdims=True)
    return (scaled - first - normed * second) * inverse


def owners_of(slots, parts):
    if slots == 1:
        return [0]
    return [round(j * (parts - 1) / (slots - 1)) for j in range(slots)]


def on_device(
    tokens, slot_valid, ln1_gain, ln1_bias, w_qkv, b_query, b_value, w_out, b_out,
    ln2_gain, ln2_bias, w_up, b_up, w_down, b_down, grad_out,
):
    parts = lax.axis_size("tensor")
    fsdp = lax.axis_size("fsdp")
    me = lax.axis_index("tensor")
    slots, length, width = tokens.shape
    inner_own = b_query.shape[0]
    inner = inner_own * parts
    heads = inner // HD
    units_own = b_up.shape[0]
    rows_own = w_up.shape[0]
    owners = owners_of(slots, parts)
    mine = jnp.int32(0)
    active = jnp.int32(0)
    for j, z in enumerate(owners):
        mine = jnp.where(me == z, j, mine)
        active = jnp.where(me == z, 1, active)

    small = jnp.concatenate(
        [v.astype(F32) for v in (ln1_gain, ln1_bias, b_query, b_value, b_out, ln2_gain, ln2_bias, b_down, b_up)]
    )
    small = lax.all_gather(small, "tensor", axis=0)
    own = width // parts
    pieces = []
    at = 0
    for size in (own, own, inner_own, inner_own, own, own, own, own, units_own):
        pieces.append(small[:, at : at + size].reshape(-1))
        at += size
    gain_one, bias_one, bias_q, bias_v, bias_out, gain_two, bias_two, bias_down, bias_up = pieces

    def spread(block):
        line = lax.all_gather(block, "tensor", axis=1)
        return lax.all_gather(line.reshape(rows_own, -1), "fsdp", axis=0, tiled=True)

    qkv_own = jnp.transpose(w_qkv, (1, 0, 2)).reshape(rows_own, 3 * inner_own)
    attn_own = jnp.concatenate([qkv_own, jnp.transpose(w_out)], axis=1)
    line = lax.all_gather(attn_own, "tensor", axis=0)
    attn_line = jnp.concatenate(
        [line[z, :, c * inner_own : (c + 1) * inner_own] for c in range(4) for z in range(parts)], axis=1
    )
    attn_full = lax.all_gather(attn_line, "fsdp", axis=0, tiled=True)
    ffn_own = jnp.concatenate([w_up, jnp.transpose(w_down)], axis=1)
    line = lax.all_gather(ffn_own, "tensor", axis=0)
    ffn_line = jnp.concatenate(
        [line[z, :, c * units_own : (c + 1) * units_own] for c in range(2) for z in range(parts)], axis=1
    )
    up_full = lax.all_gather(ffn_line[:, : parts * units_own], "fsdp", axis=0, tiled=True)
    down_full = lax.all_gather(ffn_line[:, parts * units_own :], "fsdp", axis=0, tiled=True)
    qkv_full = attn_full[:, : 3 * inner]
    out_full = attn_full[:, 3 * inner :]

    image = lax.dynamic_index_in_dim(tokens, mine, 0, keepdims=False).astype(F32)
    valid = lax.dynamic_index_in_dim(slot_valid, mine, 0, keepdims=False)
    use = (valid > 0) & (active > 0)
    keep = valid.astype(F32)
    error = lax.dynamic_index_in_dim(grad_out, mine, 0, keepdims=False)
    error = jnp.where(use, error, jnp.zeros_like(error))

    normed_one, inverse_one, a_one = norm(image, gain_one, bias_one)
    qkv_bias = jnp.concatenate([bias_q, jnp.zeros_like(bias_q), bias_v])
    qkv = (dot(qkv_full, a_one, 0, 1) + qkv_bias[:, None]).astype(BF16).reshape(3, inner, length)
    heads_t, probs, totals, peaks = attn_fwd(qkv, heads)
    resid = image + dot(heads_t, out_full, 0, 1) + bias_out
    normed_two, inverse_two, a_two = norm(resid, gain_two, bias_two)
    pre = dot(a_two, up_full, 1, 0) + bias_up
    inner_tanh = jnp.tanh(0.7978845608028654 * (pre + 0.044715 * pre * pre * pre))
    act = (0.5 * pre * (1.0 + inner_tanh)).astype(BF16)
    slope = 0.5 * (1.0 + inner_tanh) + 0.5 * pre * (1.0 - inner_tanh * inner_tanh) * (
        0.7978845608028654 * (1.0 + 3 * 0.044715 * pre * pre)
    )
    layer = ((resid + dot(act, down_full, 1, 1) + bias_down) * keep).astype(BF16)
    layer_all = lax.all_gather(layer, "tensor", axis=0)
    layer_out = jnp.stack([layer_all[z] for z in owners])

    g_down = dot(error, act, 0, 0).astype(BF16)
    d_pre = (dot(error, down_full, 1, 0) * slope).astype(BF16)
    g_up = dot(a_two, d_pre, 0, 0).astype(BF16)
    d_two = dot(d_pre, up_full, 1, 1)
    up_err = error.astype(F32)
    d_resid = up_err + norm_back(d_two, normed_two, inverse_two, gain_two)
    d_attn = d_resid.astype(BF16)
    g_out = dot(d_attn, heads_t, 0, 1).astype(BF16)
    d_heads = dot(out_full, d_attn, 0, 1).astype(BF16)
    d_qkv = attn_bwd(qkv, d_heads, heads_t, probs, totals, heads).reshape(3 * inner, length)
    g_qkv = dot(a_one, d_qkv, 0, 1).astype(BF16)
    d_one = dot(d_qkv, qkv_full, 0, 1)
    d_image = d_resid + norm_back(d_one, normed_one, inverse_one, gain_one)
    image_all = lax.all_gather(d_image.astype(BF16), "tensor", axis=0)
    grad_tokens = jnp.stack([image_all[z] for z in owners]).astype(F32)

    def scatter(block):
        return lax.psum_scatter(block, "fsdp", scatter_dimension=0, tiled=True)

    s_up, s_down, s_out, s_qkv = scatter(g_up), scatter(g_down), scatter(g_out), scatter(g_qkv)

    def by_part(block, count, size):
        return jnp.transpose(block.reshape(rows_own, count, parts, size), (2, 0, 1, 3)).reshape(parts, rows_own, count * size)

    z_ffn = lax.psum_scatter(
        jnp.concatenate([by_part(s_up, 1, units_own), by_part(s_down, 1, units_own)], axis=2),
        "tensor", scatter_dimension=0, tiled=False)
    z_attn = lax.psum_scatter(
        jnp.concatenate([by_part(s_qkv, 3, inner_own), by_part(s_out, 1, inner_own)], axis=2),
        "tensor", scatter_dimension=0, tiled=False)
    grad_up = z_ffn[:, :units_own].astype(F32)
    grad_down = jnp.transpose(z_ffn[:, units_own:]).astype(F32)
    grad_qkv = jnp.transpose(z_attn[:, : 3 * inner_own].reshape(rows_own, 3, inner_own), (1, 0, 2)).astype(F32)
    grad_out_w = jnp.transpose(z_attn[:, 3 * inner_own :]).astype(F32)

    d_qkv_f = d_qkv.astype(F32)
    sums = (
        jnp.sum(d_one * normed_one, axis=0),
        jnp.sum(d_one, axis=0),
        jnp.sum(d_two * normed_two, axis=0),
        jnp.sum(d_two, axis=0),
        jnp.sum(d_attn.astype(F32), axis=0),
        jnp.sum(up_err, axis=0),
        jnp.sum(d_qkv_f[:inner], axis=1),
        jnp.sum(d_qkv_f[2 * inner :], axis=1),
        jnp.sum(d_pre.astype(F32), axis=0),
    )
    sizes = [v.shape[0] // parts for v in sums]
    packed = jnp.concatenate([v.reshape(parts, -1) for v in sums], axis=1)
    packed = lax.psum(packed, ("fsdp", "tensor"))
    packed = lax.dynamic_index_in_dim(packed, me, 0, keepdims=False)
    outs = []
    at = 0
    for size in sizes:
        outs.append(packed[at : at + size])
        at += size
    peaks = jnp.where(use, peaks[:, 0, 0], -1e30)
    peaks = lax.pmax(peaks, ("fsdp", "tensor"))
    heads_own = heads // parts
    top = lax.dynamic_slice_in_dim(peaks, me * heads_own, heads_own, 0)
    factor = jnp.repeat(jnp.sqrt(CLIP / jnp.maximum(top, CLIP * 1.0)), HD)
    clipped = w_qkv[:2].astype(F32) * factor
    return (
        layer_out, grad_tokens, outs[0], outs[1], grad_qkv, outs[6], outs[7], grad_out_w, outs[4],
        outs[2], outs[3], grad_up, outs[8], grad_down, outs[5], top, clipped, b_query.astype(F32) * factor,
    )


def solution(mesh):
    placed = (
        P("fsdp", None, None), P("fsdp"), P("tensor"), P("tensor"), P(None, "fsdp", "tensor"), P("tensor"),
        P("tensor"), P("tensor", "fsdp"), P("tensor"), P("tensor"), P("tensor"), P("fsdp", "tensor"),
        P("tensor"), P("tensor", "fsdp"), P("tensor"), P("fsdp", None, None),
    )
    return jax.shard_map(
        on_device,
        mesh=mesh,
        in_specs=placed,
        out_specs=(
            P("fsdp", None, None), P("fsdp", None, None), P("tensor"), P("tensor"), P(None, "fsdp", "tensor"),
            P("tensor"), P("tensor"), P("tensor", "fsdp"), P("tensor"), P("tensor"), P("tensor"),
            P("fsdp", "tensor"), P("tensor"), P("tensor", "fsdp"), P("tensor"), P("tensor"),
            P(None, "fsdp", "tensor"), P("tensor"),
        ),
        check_vma=False,
    )
```

time: 1920 us -> 970 us (0.51)
  waiting for transfers between devices: 1170 us -> 540 us
  matrix products: 313 us -> 152 us
  blocking collectives: 188 us -> 113 us
  other arithmetic: 112 us -> 44.4 us
  local copies, waits for them, and re-layouts: 96.7 us -> 48.8 us
  Pallas kernels: 0 us -> 46.5 us
    all_gather x24 -> x7, waiting for transfers between devices: 673 us -> 307 us  [the longest x1 124 us: on_device(): layer_all = lax.all_gather(layer, 'tensor', axis=0)]
    dot_general x54 -> x12, matrix products: 313 us -> 152 us  [dot(): lax.dot_general(a, b, (((ca,), (cb,)), ((), ())), preferred_element_type=...]
    reduce_scatter x12 -> x6, waiting for transfers between devices: 387 us -> 232 us  [the longest x4 162 us: scatter(): return lax.psum_scatter(block, 'fsdp', scatter_dimension=0, tiled=True)]
    unnamed x8 -> x13, waiting for transfers between devices: 103 us -> 0.21 us
    psum x13 -> x1, blocking collectives: 145 us -> 46.2 us  [on_device(): packed = lax.psum(packed, ('fsdp', 'tensor'))]
    pallas_call x0 -> x2, Pallas kernels: none -> 46.5 us  [the longest x1 24.7 us: attn_bwd(): pl.pallas_call(partial(attn_bwd_kernel, HD ** (-0.5)), grid=(heads,), in_...]
    pmax x1, blocking collectives: 10.7 us -> 50.1 us  [on_device(): peaks = lax.pmax(peaks, ('fsdp', 'tensor'))]
    dynamic_update_slice x12 -> x0, local copies, waits for them, and re-layouts: 33.1 us -> none  [on_device(): lax.scan(micro_step, (big_start, small_start, peak_start), (tokens, grad_...]
  transfers between devices with their start and end apart: 40 -> 13, of which waited for: 39 -> 12; matrix products, arithmetic and copies ran while one was open for 11% -> 20% of each run, Pallas kernels for 0% -> 5%
where the time goes in v1:
time: 970 us; the launch traced here: 962 us
  waiting for transfers between devices  540 us (56%)
  matrix products  152 us (16%)
  blocking collectives  113 us (12%)
  local copies, waits for them, and re-layouts  48.8 us (5%)
  Pallas kernels  46.5 us (5%)
  other arithmetic  44.4 us (5%)
  between operations  16.9 us (2%)
    reduce_scatter x4, waiting for transfers between devices, scatter(): return lax.psum_scatter(block, 'fsdp', scatter_dimension=0, tiled=True)  162 us
    dot_general x12, matrix products, dot(): lax.dot_general(a, b, (((ca,), (cb,)), ((), ())), preferred_element_type=...  152 us
    all_gather x1, waiting for transfers between devices, on_device(): layer_all = lax.all_gather(layer, 'tensor', axis=0)  124 us
    pmax x1, blocking collectives, on_device(): peaks = lax.pmax(peaks, ('fsdp', 'tensor'))  50.1 us
    reduce_scatter x1, waiting for transfers between devices, on_device(): lax.psum_scatter(jnp.concatenate([by_part(s_up, 1, units_own), by_part(s_...  48.4 us
    all_gather x1, waiting for transfers between devices, on_device(): line = lax.all_gather(ffn_own, 'tensor', axis=0)  48.1 us
    all_gather x1, waiting for transfers between devices, on_device(): lax.all_gather(ffn_line[:, parts * units_own:], 'fsdp', axis=0, tiled=True)  48.1 us
    psum x1, blocking collectives, on_device(): packed = lax.psum(packed, ('fsdp', 'tensor'))  46.2 us
  transfers between devices with their start and end apart: 13, of which 12 were waited for; matrix products, arithmetic and copies ran while one was open for 20% of the time, Pallas kernels for 5%

profile of v1, /device:TPU:10, one launch (start us, length us, event | category | flops | bytes accessed | tf_op | source)
XLA Modules:
  0.0 962.3 jit_solution(1252222892059181795)
XLA Ops:
  12.6 31.4 %all-gather.21.cloned.1.call-done = bf16[576,1152]{1,0:T(8,128)(2,1)} async-done(((bf16[144,1152]{1,0:T(8,128)(2,1)}), bf16[576,1152]{1,0:T(8,128)(2,1)}) %all-gather.21.cloned.1.call-update) | async-done | bytes 1327120 | tf_op jit(solution)/shard_map/all_gather | solution.py:153
  48.4 48.1 %all-gather.23.cloned.1.call-done = bf16[576,2152]{1,0:T(8,128)(2,1)} async-done(((bf16[144,2152]{1,0:T(8,128)(2,1)}), bf16[576,2152]{1,0:T(8,128)(2,1)}) %all-gather.23.cloned.1.call-update) | async-done | bytes 2479120 | tf_op jit(solution)/shard_map/all_gather | solution.py:159
  105.4 17.2 %all-reduce = f32[13520]{0:T(1024)S(1)} all-reduce(f32[13520]{0:T(1024)S(1)} %dynamic-update-slice), channel_id=3, replica_groups=mesh['fsdp'=8,'tensor'=4] {'tensor'}, use_global_device_ids=true, to_apply=%add | all-reduce | flops 13520 | bytes 108160
  129.1 34.3 %all-gather.15.cloned.1.call-done = bf16[1152,4608]{1,0:T(8,128)(2,1)} async-done(((bf16[144,4608]{1,0:T(8,128)(2,1)}), bf16[1152,4608]{1,0:T(8,128)(2,1)}) %all-gather.15.cloned.1.call-update) | async-done | bytes 10616848 | tf_op jit(solution)/shard_map/all_gather | solution.py:157
  163.5 12.3 %add_convert_fusion = bf16[3456,729]{0,1:T(8,128)(2,1)} fusion(bf16[1152,4608]{1,0:T(8,128)(2,1)} %all-gather.15.cloned.1.call-done, f32[3456]{0:T(1024)S(1)} %pad_maximum_fusion.5, f32[1152]{0:T(1024)S(1)} %add.131, f32[1152]{0:T(1024)S(1)} %mul.178, f32[729]{0:T(1024)S(1)} %add_rsqrt_fusion.1, f32[729]{0:T(1024)S(1)} %broadcast_multiply_fusion.5, ...), kind=kOutput, calls=%fused_computation.15 | convolution fusion | flops 5814831104 | bytes 14726092 | tf_op jit(solution)/shard_map/dot_general | solution.py:18
  175.8 8.0 copy.58
  183.8 21.7 %attn_fwd.1 = (bf16[1152,729]{1,0:T(8,128)(2,1)}, bf16[16,729,729]{2,1,0:T(8,128)(2,1)}, f32[16,1,729]{2,1,0:T(1,128)}, f32[16,1,128]{2,1,0:T(1,128)}) custom-call(bf16[3,1152,729]{2,1,0:T(8,128)(2,1)} %bitcast.154), custom_call_target="tpu_custom_call" | custom-call | flops 8707129344 | bytes 17006112 | tf_op jit(solution)/shard_map/attn_fwd/pallas_call | solution.py:36
  205.5 5.5 fusion.69
  211.5 14.9 %all-gather.17.cloned.1.call-done = bf16[1152,4304]{1,0:T(8,128)(2,1)} async-done(((bf16[144,4304]{1,0:T(8,128)(2,1)}), bf16[1152,4304]{1,0:T(8,128)(2,1)}) %all-gather.17.cloned.1.call-update) | async-done | bytes 9916432 | tf_op jit(solution)/shard_map/all_gather | solution.py:163
  226.4 14.9 %fusion.67 = f32[729,4304]{1,0:T(8,128)} fusion(bf16[1152,4304]{1,0:T(8,128)(2,1)} %all-gather.17.cloned.1.call-done, f32[729,1152]{1,0:T(8,128)S(1)} %get-tuple-element.138, f32[1152]{0:T(1024)S(1)} %add.141, f32[1152]{0:T(1024)S(1)} %mul.184, f32[729]{0:T(1024)S(1)} %add_rsqrt_fusion, f32[729]{0:T(1024)S(1)} %broadcast_multiply_fusion.4), kind=kOutput, calls=%fused_computation.150 | convolution fusion | flops 7233266176 | bytes 25841160 | tf_op jit(solution)/shard_map/dot_general | solution.py:18
  241.3 48.1 %all-gather.19.cloned.1.call-done = bf16[1152,4304]{1,0:T(8,128)(2,1)} async-done(((bf16[144,4304]{1,0:T(8,128)(2,1)}), bf16[1152,4304]{1,0:T(8,128)(2,1)}) %all-gather.19.cloned.1.call-update) | async-done | bytes 9916432 | tf_op jit(solution)/shard_map/all_gather | solution.py:164
  289.4 20.0 %convert_reduce_fusion = (f32[4304]{0:T(1024)}, bf16[729,4304]{1,0:T(8,128)(2,1)}) fusion(f32[729,4304]{1,0:T(8,128)} %fusion.67, f32[4304]{0:T(1024)S(1)} %add.144, bf16[1152,4304]{1,0:T(8,128)(2,1)} %all-gather.19.cloned.1.call-done, bf16[3,729,1152]{2,1,0:T(8,128)(2,1)} %param.31, s32[]{:T(128)S(6)} %select_n.52, pred[]{:T(512)S(6)} %and.4), kind=kOutput, calls=%fused_computation.13 | convolution fusion | flops 7298928640 | bytes 30844708 | tf_op jit(solution)/shard_map/dot_general | solution.py:18
  309.4 16.6 %multiply_reduce_fusion = (f32[1152]{0:T(1024)}, f32[729]{0:T(1024)S(1)}, f32[729]{0:T(1024)S(1)}, f32[1152]{0:T(1024)}, f32[729,1152]{1,0:T(8,128)}) fusion(f32[729,1152]{1,0:T(8,128)S(1)} %get-tuple-element.138, f32[729]{0:T(1024)S(1)} %add_rsqrt_fusion, f32[729]{0:T(1024)S(1)} %broadcast_multiply_fusion.4, f32[1152]{0:T(1024)S(1)} %mul.184, ...), kind=kOutput, calls=%fused_computation.56 | convolution fusion | flops 7236621312 | bytes 22935600 | tf_op jit(solution)/shard_map/dot_general | solution.py:18
  331.3 4.1 convolution_convert_fusion.3
  335.5 6.5 convolution_convert_fusion.4
  342.0 4.1 copy.59.do_ref
  346.1 24.7 %attn_bwd.1 = bf16[3,1152,729]{2,1,0:T(8,128)(2,1)} custom-call(bf16[3,1152,729]{2,1,0:T(8,128)(2,1)} %bitcast.155, bf16[1152,729]{1,0:T(8,128)(2,1)} %copy.59.do_ref, bf16[1152,729]{1,0:T(8,128)(2,1)} %get-tuple-element.22.o_ref, bf16[16,729,729]{2,1,0:T(8,128)(2,1)} %get-tuple-element.23.p_ref, f32[16,1,729]{2,1,0:T(1,128)} %get-tuple-element.24.l_ref), custom_call_target="tpu_custom_call" | custom-call | flops 17414258688 | bytes 17006112 | tf_op jit(solution)/shard_map/attn_bwd/pallas_call | solution.py:75
  370.8 12.3 %convolution_convert_fusion.2 = bf16[1152,3456]{1,0:T(8,128)(2,1)} fusion(bf16[3456,729]{1,0:T(8,128)(2,1)} %bitcast.156, f32[1152]{0:T(1024)S(1)} %add.131, f32[1152]{0:T(1024)S(1)} %mul.178, f32[729]{0:T(1024)S(1)} %add_rsqrt_fusion.1, f32[729]{0:T(1024)S(1)} %broadcast_multiply_fusion.5, bf16[3,729,1152]{2,1,0:T(8,128)(2,1)} %param.16, s32[]{:T(128)S(6)} %select_n.52), kind=kOutput, calls=%fused_computation.4 | convolution fusion | flops 5813773312 | bytes 14981836 | tf_op jit(solution)/shard_map/dot_general | solution.py:18
  383.2 15.0 %convolution_convert_fusion = bf16[1152,4304]{1,0:T(8,128)(2,1)} fusion(bf16[3,729,1152]{2,1,0:T(8,128)(2,1)} %param.31, s32[]{:T(128)S(6)} %select_n.52, pred[]{:T(512)S(6)} %and.4, f32[729,4304]{1,0:T(8,128)} %fusion.67, f32[4304]{0:T(1024)S(1)} %add.144), kind=kOutput, calls=%fused_computation.2 | convolution fusion | flops 7266241536 | bytes 24441668 | tf_op jit(solution)/shard_map/dot_general | solution.py:18
  398.3 14.0 %convolution_convert_fusion.1 = bf16[1152,4304]{1,0:T(8,128)(2,1)} fusion(bf16[729,4304]{1,0:T(8,128)(2,1)} %get-tuple-element.142, f32[729,1152]{1,0:T(8,128)S(1)} %get-tuple-element.138, f32[1152]{0:T(1024)S(1)} %add.141, f32[1152]{0:T(1024)S(1)} %mul.184, f32[729]{0:T(1024)S(1)} %add_rsqrt_fusion, f32[729]{0:T(1024)S(1)} %broadcast_multiply_fusion.4), kind=kOutput, calls=%fused_computation.3 | convolution fusion | flops 7238224384 | bytes 19565928 | tf_op jit(solution)/shard_map/dot_general | solution.py:18
  412.4 14.1 %fusion.32 = (f32[1152]{0:T(1024)}, f32[729]{0:T(1024)S(1)}, f32[729]{0:T(1024)S(1)}, f32[1152]{0:T(1024)}, f32[729,1152]{1,0:T(8,128)S(1)}) fusion(f32[729]{0:T(1024)S(1)} %add_rsqrt_fusion.1, f32[729]{0:T(1024)S(1)} %broadcast_multiply_fusion.5, bf16[3,729,1152]{2,1,0:T(8,128)(2,1)} %param.16, s32[]{:T(128)S(6)} %select_n.52, f32[1152]{0:T(1024)S(1)} %mul.178, ...), kind=kOutput, calls=%fused_computation.49 | convolution fusion | flops 5813146624 | bytes 18351508 | tf_op jit(solution)/shard_map/dot_general | solution.py:18
  430.7 16.6 %fusion.39 = bf16[1,729,1152]{2,1,0:T(8,128)(2,1)} fusion(f32[729,1152]{1,0:T(8,128)S(1)} %get-tuple-element.138, bf16[1152,4304]{1,0:T(8,128)(2,1)} %all-gather.19.cloned.1.call-done, f32[]{:T(128)} %bitcast.32, f32[1152]{0:T(1024)S(1)} %add.150, f32[729,4304]{1,0:T(8,128)} %fusion.67, f32[4304]{0:T(1024)S(1)} %add.144), kind=kOutput, calls=%fused_computation.65 | convolution fusion | flops 7263802368 | bytes 27527556 | tf_op jit(solution)/shard_map/dot_general | solution.py:18
  457.7 78.7 %reduce-scatter.15.cloned.1.call-done = bf16[144,4304]{1,0:T(8,128)(2,1)} async-done(((bf16[1152,4304]{1,0:T(8,128)(2,1)}), bf16[144,4304]{1,0:T(8,128)(2,1)}) %reduce-scatter.15.cloned.1.call-update) | async-done | bytes 1239568 | tf_op jit(solution)/shard_map/reduce_scatter | solution.py:208
  539.7 79.9 %reduce-scatter.13.cloned.1.call-done = bf16[144,4304]{1,0:T(8,128)(2,1)} async-done(((bf16[1152,4304]{1,0:T(8,128)(2,1)}), bf16[144,4304]{1,0:T(8,128)(2,1)}) %reduce-scatter.13.cloned.1.call-update) | async-done | bytes 1239568 | tf_op jit(solution)/shard_map/reduce_scatter | solution.py:208
  625.4 50.1 %pmax.7 = f32[16]{0:T(128)S(1)} all-reduce(f32[16]{0:T(128)S(1)} %fusion.58), channel_id=1, replica_groups=mesh['fsdp'=8,'tensor'=4] {'fsdp','tensor'}, use_global_device_ids=true, to_apply=%region_24.25 | all-reduce | flops 16 | bytes 128 | tf_op jit(solution)/shard_map/pmax | solution.py:248
  677.7 7.4 convert_element_type.152
  689.6 46.2 %psum.7 = f32[4,3380]{1,0:T(4,128)S(1)} all-reduce(f32[4,3380]{1,0:T(4,128)S(1)} %concatenate.38), channel_id=1, replica_groups=mesh['fsdp'=8,'tensor'=4] {'fsdp','tensor'}, use_global_device_ids=true, to_apply=%region_17.18 | all-reduce | flops 13520 | bytes 108160 | tf_op jit(solution)/shard_map/psum | solution.py:240
  737.1 6.5 all-gather.27.cloned.1.call-done
  743.6 123.9 %all-gather.25.cloned.1.call-done = bf16[4,729,1152]{2,1,0:T(8,128)(2,1)} async-done(((bf16[1,729,1152]{2,1,0:T(8,128)(2,1)}), bf16[4,729,1152]{2,1,0:T(8,128)(2,1)}) %all-gather.25.cloned.1.call-update) | async-done | bytes 6718480 | tf_op jit(solution)/shard_map/all_gather | solution.py:188
  874.3 4.6 maximum_convert_fusion
  878.9 21.6 %reduce-scatter.11.cloned.1.call-done = bf16[1,144,1152]{2,1,0:T(8,128)(2,1)} async-done(((bf16[4,144,1152]{2,1,0:T(8,128)(2,1)}), bf16[1,144,1152]{2,1,0:T(8,128)(2,1)}) %reduce-scatter.11.cloned.1.call-update) | async-done | bytes 331792 | tf_op jit(solution)/shard_map/reduce_scatter | solution.py:218
  904.5 48.4 %reduce-scatter.17.cloned.1.call-done = bf16[1,144,2152]{2,1,0:T(8,128)(2,1)} async-done(((bf16[4,144,2152]{2,1,0:T(8,128)(2,1)}), bf16[1,144,2152]{2,1,0:T(8,128)(2,1)}) %reduce-scatter.17.cloned.1.call-update) | async-done | bytes 619792 | tf_op jit(solution)/shard_map/reduce_scatter | solution.py:215
  (158 shorter events, 73.5 us)
Async XLA Ops:
  7.2 36.8 %all-gather.21.cloned.1.call-start = ((), (), s32[]{:S(2)}) async-start(), calls=%async_computation.15 | async-start | bytes 1658880 | tf_op jit(solution)/shard_map/all_gather | solution.py:153
  10.4 86.2 %all-gather.23.cloned.1.call-start = ((), (), s32[]{:S(2)}) async-start(), calls=%async_computation.16 | async-start | bytes 3133440 | tf_op jit(solution)/shard_map/all_gather | solution.py:159
  12.5 150.9 %all-gather.15.cloned.1.call-start = ((), (), s32[]{:S(2)}) async-start(), calls=%async_computation.6 | async-start | bytes 11943936 | tf_op jit(solution)/shard_map/all_gather | solution.py:157
  48.4 178.0 %all-gather.17.cloned.1.call-start = ((), (), s32[]{:S(2)}) async-start(), calls=%async_computation.7 | async-start | bytes 11280384 | tf_op jit(solution)/shard_map/all_gather | solution.py:163
  99.0 5.8 copy-start.10
  99.0 5.8 copy-start.11
  99.0 5.8 copy-start.13
  99.1 5.8 copy-start.14
  99.1 5.8 copy-start.15
  99.1 5.8 copy-start.16
  99.1 5.8 copy-start.17
  99.1 5.8 copy-start.18
  99.1 5.8 copy-start.19
  101.3 22.8 %copy-start.20 = (s32[3]{0:T(128)S(1)}, s32[3]{0:T(128)}, u32[]{:S(2)}) copy-start(s32[3]{0:T(128)} %param.17) | copy-start | bytes 40
  101.3 188.1 %all-gather.19.cloned.1.call-start = ((), (), s32[]{:S(2)}) async-start(), calls=%async_computation.8 | async-start | bytes 11280384 | tf_op jit(solution)/shard_map/all_gather | solution.py:164
  103.5 343.9 %reduce-scatter.9.cloned.1.call-start = ((), (), s32[]{:S(2)}) async-start(), calls=%async_computation.10 | async-start | bytes 2985984 | tf_op jit(solution)/shard_map/reduce_scatter | solution.py:208
  326.0 5.3 copy-start.22
  335.5 117.1 %reduce-scatter.7.cloned.1.call-start = ((), (), s32[]{:S(2)}) async-start(), calls=%async_computation.9 | async-start | bytes 8957952 | tf_op jit(solution)/shard_map/reduce_scatter | solution.py:208
  383.2 153.2 %reduce-scatter.15.cloned.1.call-start = ((), (), s32[]{:S(2)}) async-start(), calls=%async_computation.13 | async-start | bytes 11280384 | tf_op jit(solution)/shard_map/reduce_scatter | solution.py:208
  398.2 221.4 %reduce-scatter.13.cloned.1.call-start = ((), (), s32[]{:S(2)}) async-start(), calls=%async_computation.12 | async-start | bytes 11280384 | tf_op jit(solution)/shard_map/reduce_scatter | solution.py:208
  412.3 331.3 %all-gather.27.cloned.1.call-start = ((), (), s32[]{:S(2)}) async-start(), calls=%async_computation.18 | async-start | bytes 8478720 | tf_op jit(solution)/shard_map/all_gather | solution.py:204
  412.3 14.1 %copy-start.1 = (f32[729,1152]{1,0:T(8,128)S(1)}, f32[729,1152]{1,0:T(8,128)}, u32[]{:S(2)}) copy-start(f32[729,1152]{1,0:T(8,128)} %copy-done) | copy-start | bytes 10077700
  429.9 437.5 %all-gather.25.cloned.1.call-start = ((), (), s32[]{:S(2)}) async-start(), calls=%async_computation.17 | async-start | bytes 8478720 | tf_op jit(solution)/shard_map/all_gather | solution.py:188
  447.3 453.2 %reduce-scatter.11.cloned.1.call-start = ((), (), s32[]{:S(2)}) async-start(), calls=%async_computation.11 | async-start | bytes 1658880 | tf_op jit(solution)/shard_map/reduce_scatter | solution.py:218
  457.7 495.3 %reduce-scatter.17.cloned.1.call-start = ((), (), s32[]{:S(2)}) async-start(), calls=%async_computation.14 | async-start | bytes 3133440 | tf_op jit(solution)/shard_map/reduce_scatter | solution.py:215
  623.0 53.3 %copy-start.12 = (bf16[288]{0:T(512)(128)(2,1)S(1)}, bf16[288]{0:T(512)(128)(2,1)}, u32[]{:S(2)}) copy-start(bf16[288]{0:T(512)(128)(2,1)} %param.21) | copy-start | bytes 1732
  623.0 53.9 %copy-start.2 = (bf16[3,144,288]{2,1,0:T(8,128)(2,1)S(1)}, bf16[3,144,288]{2,1,0:T(8,128)(2,1)}, u32[]{:S(2)}) copy-start(bf16[3,144,288]{2,1,0:T(8,128)(2,1)} %param.20) | copy-start | bytes 746500
  677.7 7.5 copy-start.4
  677.7 7.5 copy-start.6
  677.7 7.6 copy-start.5
  677.7 7.9 copy-start.8
  677.7 8.0 copy-start.7
  (8 other events, 24.1 us)
Sparse Core Ops, SparseCore 0:
  10.5 33.4 all-gather.20
  46.1 50.3 all-gather.22
  99.0 64.3 all-gather.14
  165.2 61.1 all-gather.16
  228.1 61.2 all-gather.18
  335.6 42.9 reduce-scatter.8
  383.3 69.1 reduce-scatter.6
  456.7 79.5 reduce-scatter.14
  540.0 79.5 reduce-scatter.12
  621.0 122.5 all-gather.26
  745.8 121.6 all-gather.24
  869.6 30.8 reduce-scatter.10
  902.8 50.0 reduce-scatter.16

commit v2 on v1

--- a/solution.py
+++ b/solution.py
@@ -112,6 +112,91 @@
     return [round(j * (parts - 1) / (slots - 1)) for j in range(slots)]
 
 
+def pick(block, index, axis=0):
+    return lax.dynamic_index_in_dim(block, index, axis, keepdims=False)
+
+
+def plus(a, b):
+    return (a.astype(F32) + b.astype(F32)).astype(BF16)
+
+
+def shift(block, by):
+    parts = lax.axis_size("tensor")
+    return lax.ppermute(block, "tensor", [(z, (z + by) % parts) for z in range(parts)])
+
+
+def flip(block, bit):
+    size = lax.axis_size("fsdp")
+    return lax.ppermute(block, "fsdp", [(i, i ^ (1 << bit)) for i in range(size)])
+
+
+def line_gather(block):
+    parts = lax.axis_size("tensor")
+    me = lax.axis_index("tensor")
+    near = jnp.stack([block] + [shift(block, k) for k in range(1, parts)])
+    return [pick(near, lax.rem(me - z + parts, parts)) for z in range(parts)]
+
+
+def line_scatter(blocks):
+    parts = lax.axis_size("tensor")
+    me = lax.axis_index("tensor")
+    total = pick(blocks, me).astype(F32)
+    for k in range(1, parts):
+        total = total + shift(pick(blocks, lax.rem(me + k, parts)), k).astype(F32)
+    return total
+
+
+def line_share(block, owners, chunks):
+    parts = lax.axis_size("tensor")
+    me = lax.axis_index("tensor")
+    rows = block.shape[0]
+    step = -(-rows // chunks // 16) * 16
+    found = []
+    for at in range(0, rows, step):
+        part = block[at : min(at + step, rows)]
+        below, above = [part], [part]
+        for s in range(1, parts):
+            up = [(z, z + 1) for z in range(parts - 1) if z - s + 1 in owners]
+            down = [(z, z - 1) for z in range(1, parts) if z + s - 1 in owners]
+            below.append(lax.ppermute(below[-1], "tensor", up) if up else None)
+            above.append(lax.ppermute(above[-1], "tensor", down) if down else None)
+        outs = []
+        for z in owners:
+            out = part
+            for other in range(parts):
+                if other > z:
+                    out = jnp.where(me == other, below[other - z], out)
+                elif other < z:
+                    out = jnp.where(me == other, above[z - other], out)
+            outs.append(out)
+        found.append(jnp.stack(outs))
+    return jnp.concatenate(found, axis=1)
+
+
+def plane_scatter(block):
+    size = lax.axis_size("fsdp")
+    me = lax.axis_index("fsdp")
+    bits = size.bit_length() - 1
+    rows, cols = block.shape[0] // size, block.shape[1]
+    block = block.reshape((2,) * bits + (rows, cols))
+
+    def halve(part, bit, axis):
+        own = lax.rem(lax.shift_right_logical(me, bit), 2)
+        return plus(pick(part, own, axis), flip(pick(part, 1 - own, axis), bit))
+
+    block = halve(block, 0, bits - 1)
+    cut = -(-(rows // 2) // 16) * 16
+    outs = []
+    for lo, hi, order in ((0, cut, list(range(1, bits))), (cut, rows, list(range(bits - 1, 0, -1)))):
+        part = lax.slice_in_dim(block, lo, hi, axis=bits - 1)
+        left = list(range(bits - 1, 0, -1))
+        for bit in order:
+            part = halve(part, bit, left.index(bit))
+            left.remove(bit)
+        outs.append(part)
+    return jnp.concatenate(outs, axis=0)
+
+
 def on_device(
     tokens, slot_valid, ln1_gain, ln1_bias, w_qkv, b_query, b_value, w_out, b_out,
     ln2_gain, ln2_bias, w_up, b_up, w_down, b_down, grad_out,
@@ -132,10 +217,27 @@
         mine = jnp.where(me == z, j, mine)
         active = jnp.where(me == z, 1, active)
 
+    qkv_own = jnp.transpose(w_qkv, (1, 0, 2)).reshape(rows_own, 3 * inner_own)
+    attn_own = jnp.concatenate([qkv_own, jnp.transpose(w_out)], axis=1)
+    line = line_gather(attn_own)
+    attn_line = jnp.concatenate(
+        [line[z][:, c * inner_own : (c + 1) * inner_own] for c in range(4) for z in range(parts)], axis=1
+    )
+    attn_full = lax.all_gather(attn_line, "fsdp", axis=0, tiled=True)
+    ffn_own = jnp.concatenate([w_up, jnp.transpose(w_down)], axis=1)
+    line = line_gather(ffn_own)
+    ffn_line = jnp.concatenate(
+        [line[z][:, c * units_own : (c + 1) * units_own] for c in range(2) for z in range(parts)], axis=1
+    )
+    up_full = lax.all_gather(ffn_line[:, : parts * units_own], "fsdp", axis=0, tiled=True)
+    down_full = lax.all_gather(ffn_line[:, parts * units_own :], "fsdp", axis=0, tiled=True)
+    qkv_full = attn_full[:, : 3 * inner]
+    out_full = attn_full[:, 3 * inner :]
+
     small = jnp.concatenate(
         [v.astype(F32) for v in (ln1_gain, ln1_bias, b_query, b_value, b_out, ln2_gain, ln2_bias, b_down, b_up)]
     )
-    small = lax.all_gather(small, "tensor", axis=0)
+    small = jnp.stack(line_gather(small))
     own = width // parts
     pieces = []
     at = 0
@@ -144,32 +246,11 @@
         at += size
     gain_one, bias_one, bias_q, bias_v, bias_out, gain_two, bias_two, bias_down, bias_up = pieces
 
-    def spread(block):
-        line = lax.all_gather(block, "tensor", axis=1)
-        return lax.all_gather(line.reshape(rows_own, -1), "fsdp", axis=0, tiled=True)
-
-    qkv_own = jnp.transpose(w_qkv, (1, 0, 2)).reshape(rows_own, 3 * inner_own)
-    attn_own = jnp.concatenate([qkv_own, jnp.transpose(w_out)], axis=1)
-    line = lax.all_gather(attn_own, "tensor", axis=0)
-    attn_line = jnp.concatenate(
-        [line[z, :, c * inner_own : (c + 1) * inner_own] for c in range(4) for z in range(parts)], axis=1
-    )
-    attn_full = lax.all_gather(attn_line, "fsdp", axis=0, tiled=True)
-    ffn_own = jnp.concatenate([w_up, jnp.transpose(w_down)], axis=1)
-    line = lax.all_gather(ffn_own, "tensor", axis=0)
-    ffn_line = jnp.concatenate(
-        [line[z, :, c * units_own : (c + 1) * units_own] for c in range(2) for z in range(parts)], axis=1
-    )
-    up_full = lax.all_gather(ffn_line[:, : parts * units_own], "fsdp", axis=0, tiled=True)
-    down_full = lax.all_gather(ffn_line[:, parts * units_own :], "fsdp", axis=0, tiled=True)
-    qkv_full = attn_full[:, : 3 * inner]
-    out_full = attn_full[:, 3 * inner :]
-
-    image = lax.dynamic_index_in_dim(tokens, mine, 0, keepdims=False).astype(F32)
-    valid = lax.dynamic_index_in_dim(slot_valid, mine, 0, keepdims=False)
+    image = pick(tokens, mine).astype(F32)
+    valid = pick(slot_valid, mine)
     use = (valid > 0) & (active > 0)
     keep = valid.astype(F32)
-    error = lax.dynamic_index_in_dim(grad_out, mine, 0, keepdims=False)
+    error = pick(grad_out, mine)
     error = jnp.where(use, error, jnp.zeros_like(error))
 
     normed_one, inverse_one, a_one = norm(image, gain_one, bias_one)
@@ -185,13 +266,13 @@
         0.7978845608028654 * (1.0 + 3 * 0.044715 * pre * pre)
     )
     layer = ((resid + dot(act, down_full, 1, 1) + bias_down) * keep).astype(BF16)
-    layer_all = lax.all_gather(layer, "tensor", axis=0)
-    layer_out = jnp.stack([layer_all[z] for z in owners])
+    layer_out = line_share(layer, owners, CHUNKS)
 
     g_down = dot(error, act, 0, 0).astype(BF16)
     d_pre = (dot(error, down_full, 1, 0) * slope).astype(BF16)
     g_up = dot(a_two, d_pre, 0, 0).astype(BF16)
     d_two = dot(d_pre, up_full, 1, 1)
+    d_two, g_up, g_down = lax.optimization_barrier((d_two, g_up, g_down))
     up_err = error.astype(F32)
     d_resid = up_err + norm_back(d_two, normed_two, inverse_two, gain_two)
     d_attn = d_resid.astype(BF16)
@@ -201,27 +282,18 @@
     g_qkv = dot(a_one, d_qkv, 0, 1).astype(BF16)
     d_one = dot(d_qkv, qkv_full, 0, 1)
     d_image = d_resid + norm_back(d_one, normed_one, inverse_one, gain_one)
-    image_all = lax.all_gather(d_image.astype(BF16), "tensor", axis=0)
-    grad_tokens = jnp.stack([image_all[z] for z in owners]).astype(F32)
-
-    def scatter(block):
-        return lax.psum_scatter(block, "fsdp", scatter_dimension=0, tiled=True)
-
-    s_up, s_down, s_out, s_qkv = scatter(g_up), scatter(g_down), scatter(g_out), scatter(g_qkv)
+    grad_tokens = line_share(d_image.astype(BF16), owners, CHUNKS).astype(F32)
 
     def by_part(block, count, size):
         return jnp.transpose(block.reshape(rows_own, count, parts, size), (2, 0, 1, 3)).reshape(parts, rows_own, count * size)
 
-    z_ffn = lax.psum_scatter(
-        jnp.concatenate([by_part(s_up, 1, units_own), by_part(s_down, 1, units_own)], axis=2),
-        "tensor", scatter_dimension=0, tiled=False)
-    z_attn = lax.psum_scatter(
-        jnp.concatenate([by_part(s_qkv, 3, inner_own), by_part(s_out, 1, inner_own)], axis=2),
-        "tensor", scatter_dimension=0, tiled=False)
-    grad_up = z_ffn[:, :units_own].astype(F32)
-    grad_down = jnp.transpose(z_ffn[:, units_own:]).astype(F32)
-    grad_qkv = jnp.transpose(z_attn[:, : 3 * inner_own].reshape(rows_own, 3, inner_own), (1, 0, 2)).astype(F32)
-    grad_out_w = jnp.transpose(z_attn[:, 3 * inner_own :]).astype(F32)
+    z_down = line_scatter(by_part(scatter(g_down), 1, units_own))
+    z_up = line_scatter(by_part(scatter(g_up), 1, units_own))
+    z_out = line_scatter(by_part(scatter_late(g_out), 1, inner_own))
+    z_qkv = line_scatter(by_part(scatter_late(g_qkv), 3, inner_own))
+    grad_down = jnp.transpose(z_down)
+    grad_qkv = jnp.transpose(z_qkv.reshape(rows_own, 3, inner_own), (1, 0, 2))
+    grad_out_w = jnp.transpose(z_out)
 
     d_qkv_f = d_qkv.astype(F32)
     sums = (
@@ -236,24 +308,34 @@
         jnp.sum(d_pre.astype(F32), axis=0),
     )
     sizes = [v.shape[0] // parts for v in sums]
-    packed = jnp.concatenate([v.reshape(parts, -1) for v in sums], axis=1)
-    packed = lax.psum(packed, ("fsdp", "tensor"))
-    packed = lax.dynamic_index_in_dim(packed, me, 0, keepdims=False)
+    packed = line_scatter(jnp.concatenate([v.reshape(parts, -1) for v in sums], axis=1))
+    top = jnp.where(use, peaks[:, 0, 0], -1e30)
+    for k in range(1, parts):
+        top = jnp.maximum(top, shift(jnp.where(use, peaks[:, 0, 0], -1e30), k))
+    for bit in range(fsdp.bit_length() - 1):
+        packed = packed + flip(packed, bit)
+        top = jnp.maximum(top, flip(top, bit))
     outs = []
     at = 0
     for size in sizes:
         outs.append(packed[at : at + size])
         at += size
-    peaks = jnp.where(use, peaks[:, 0, 0], -1e30)
-    peaks = lax.pmax(peaks, ("fsdp", "tensor"))
     heads_own = heads // parts
-    top = lax.dynamic_slice_in_dim(peaks, me * heads_own, heads_own, 0)
+    top = lax.dynamic_slice_in_dim(top, me * heads_own, heads_own, 0)
     factor = jnp.repeat(jnp.sqrt(CLIP / jnp.maximum(top, CLIP * 1.0)), HD)
     clipped = w_qkv[:2].astype(F32) * factor
     return (
         layer_out, grad_tokens, outs[0], outs[1], grad_qkv, outs[6], outs[7], grad_out_w, outs[4],
-        outs[2], outs[3], grad_up, outs[8], grad_down, outs[5], top, clipped, b_query.astype(F32) * factor,
-    )
+        outs[2], outs[3], z_up, outs[8], grad_down, outs[5], top, clipped, b_query.astype(F32) * factor,
+    )
+
+
+def scatter(block):
+    return lax.psum_scatter(block, "fsdp", scatter_dimension=0, tiled=True)
+
+
+scatter_late = plane_scatter
+CHUNKS = 2
 
 
 def solution(mesh):

time: 970 us -> 795 us (0.82)
  waiting for transfers between devices: 540 us -> 301 us
  starting transfers between devices: 0.54 us -> 120 us
  blocking collectives: 113 us -> 0 us
  local copies, waits for them, and re-layouts: 48.8 us -> 95.8 us
  other arithmetic: 44.4 us -> 60 us
    ppermute x0 -> x67, waiting for transfers between devices: none -> 263 us  [the longest x27 126 us: shift(): lax.ppermute(block, 'tensor', [(z, (z + by) % parts) for z in range(parts)])]
    all_gather x4 -> x0, waiting for transfers between devices: 210 us -> none  [the longest x1 124 us: on_device(): layer_all = lax.all_gather(layer, 'tensor', axis=0)]
    reduce_scatter x4 -> x2, waiting for transfers between devices: 162 us -> 0.02 us  [scatter(): return lax.psum_scatter(block, 'fsdp', scatter_dimension=0, tiled=True)]
    ppermute x0 -> x67, starting transfers between devices: none -> 120 us  [the longest x27 45.7 us: shift(): lax.ppermute(block, 'tensor', [(z, (z + by) % parts) for z in range(parts)])]
    reduce_scatter x2 -> x0, waiting for transfers between devices: 70.1 us -> none  [the longest x1 48.4 us: on_device(): lax.psum_scatter(jnp.concatenate([by_part(s_up, 1, units_own), by_part(s_...]
    pmax x1 -> x0, blocking collectives: 50.1 us -> none  [on_device(): peaks = lax.pmax(peaks, ('fsdp', 'tensor'))]
    psum x1 -> x0, blocking collectives: 46.2 us -> none  [on_device(): packed = lax.psum(packed, ('fsdp', 'tensor'))]
    unnamed x50 -> x112, local copies, waits for them, and re-layouts: 3.73 us -> 45.4 us
  transfers between devices with their start and end apart: 13 -> 72, of which waited for: 12 -> 33; matrix products, arithmetic and copies ran while one was open for 20% -> 29% of each run, Pallas kernels for 5% -> 6%
where the time goes in v2:
time: 795 us; the launch traced here: 787 us
  waiting for transfers between devices  301 us (38%)
  matrix products  145 us (18%)
  starting transfers between devices  120 us (15%)
  local copies, waits for them, and re-layouts  95.8 us (12%)
  other arithmetic  60 us (8%)
  Pallas kernels  46.8 us (6%)
  between operations  17 us (2%)
    dot_general x12, matrix products, dot(): lax.dot_general(a, b, (((ca,), (cb,)), ((), ())), preferred_element_type=...  145 us
    ppermute x27, waiting for transfers between devices, shift(): lax.ppermute(block, 'tensor', [(z, (z + by) % parts) for z in range(parts)])  126 us
    ppermute x12, waiting for transfers between devices, line_share(): above.append(lax.ppermute(above[-1], 'tensor', down) if down else None)  69.9 us
    ppermute x16, waiting for transfers between devices, flip(): return lax.ppermute(block, 'fsdp', [(i, i ^ 1 << bit) for i in range(size)])  46.2 us
    ppermute x27, starting transfers between devices, shift(): lax.ppermute(block, 'tensor', [(z, (z + by) % parts) for z in range(parts)])  45.7 us
    unnamed x112, local copies, waits for them, and re-layouts  45.4 us
    all_gather x1, waiting for transfers between devices, on_device(): lax.all_gather(ffn_line[:, parts * units_own:], 'fsdp', axis=0, tiled=True)  32.5 us
    ppermute x12, starting transfers between devices, line_share(): above.append(lax.ppermute(above[-1], 'tensor', down) if down else None)  29.2 us
  transfers between devices with their start and end apart: 72, of which 33 were waited for; matrix products, arithmetic and copies ran while one was open for 29% of the time, Pallas kernels for 6%

profile of v2, /device:TPU:10, one launch (start us, length us, event | category | flops | bytes accessed | tf_op | source)
XLA Modules:
  0.0 786.6 jit_solution(12195857410742751683)
XLA Ops:
  15.3 12.0 %collective-permute-done.1 = bf16[144,1152]{1,0:T(8,128)(2,1)S(1)} collective-permute-done((bf16[144,1152]{1,0:T(8,128)(2,1)S(1)}, bf16[144,1152]{1,0:T(8,128)(2,1)S(1)}, u32[]{:S(2)}, u32[]{:S(2)}) %collective-permute-start.1) | collective-permute-done | bytes 331808 | tf_op jit(solution)/shard_map/ppermute | solution.py:125
  27.3 13.3 %collective-permute-done = bf16[144,1152]{1,0:T(8,128)(2,1)S(1)} collective-permute-done((bf16[144,1152]{1,0:T(8,128)(2,1)S(1)}, bf16[144,1152]{1,0:T(8,128)(2,1)S(1)}, u32[]{:S(2)}, u32[]{:S(2)}) %collective-permute-start) | collective-permute-done | bytes 331808 | tf_op jit(solution)/shard_map/ppermute | solution.py:125
  48.2 23.9 %collective-permute-done.7 = bf16[144,2152]{1,0:T(8,128)(2,1)S(1)} collective-permute-done((bf16[144,2152]{1,0:T(8,128)(2,1)S(1)}, bf16[144,2152]{1,0:T(8,128)(2,1)S(1)}, u32[]{:S(2)}, u32[]{:S(2)}) %collective-permute-start.7) | collective-permute-done | bytes 619808 | tf_op jit(solution)/shard_map/ppermute | solution.py:125
  72.1 26.4 %collective-permute-done.6 = bf16[144,2152]{1,0:T(8,128)(2,1)S(1)} collective-permute-done((bf16[144,2152]{1,0:T(8,128)(2,1)S(1)}, bf16[144,2152]{1,0:T(8,128)(2,1)S(1)}, u32[]{:S(2)}, u32[]{:S(2)}) %collective-permute-start.6) | collective-permute-done | bytes 619808 | tf_op jit(solution)/shard_map/ppermute | solution.py:125
  116.1 13.9 %add_convert_fusion = bf16[3456,729]{0,1:T(8,128)(2,1)} fusion(bf16[1152,4608]{1,0:T(8,128)(2,1)} %all-gather.4.cloned.1.call-done, f32[3456]{0:T(1024)S(1)} %pad_maximum_fusion.8, f32[1152]{0:T(1024)S(1)} %add.344, f32[1152]{0:T(1024)S(1)} %mul.178, f32[729]{0:T(1024)S(1)} %add_rsqrt_fusion.1, f32[729]{0:T(1024)S(1)} %broadcast_multiply_fusion.5, ...), kind=kOutput, calls=%fused_computation.15 | convolution fusion | flops 5814831104 | bytes 14726092 | tf_op jit(solution)/shard_map/dot_general | solution.py:18
  129.9 8.0 %copy.70 = bf16[3456,729]{1,0:T(8,128)(2,1)} copy(bf16[3456,729]{0,1:T(8,128)(2,1)} %add_convert_fusion) | data formatting | bytes 10077696 | tf_op jit(solution)/shard_map/convert_element_type | solution.py:258
  137.9 21.7 %attn_fwd.1 = (bf16[1152,729]{1,0:T(8,128)(2,1)}, bf16[16,729,729]{2,1,0:T(8,128)(2,1)}, f32[16,1,729]{2,1,0:T(1,128)}, f32[16,1,128]{2,1,0:T(1,128)}) custom-call(bf16[3,1152,729]{2,1,0:T(8,128)(2,1)} %bitcast.245), custom_call_target="tpu_custom_call" | custom-call | flops 8707129344 | bytes 17006112 | tf_op jit(solution)/shard_map/attn_fwd/pallas_call | solution.py:36
  171.8 14.6 %fusion.85 = f32[729,4304]{1,0:T(8,128)} fusion(bf16[1152,4304]{1,0:T(8,128)(2,1)} %all-gather.6.cloned.1.call-done, f32[729,1152]{1,0:T(8,128)S(1)} %get-tuple-element.203, f32[1152]{0:T(1024)S(1)} %add.354, f32[1152]{0:T(1024)S(1)} %mul.184, f32[729]{0:T(1024)S(1)} %add_rsqrt_fusion, f32[729]{0:T(1024)S(1)} %broadcast_multiply_fusion.4), kind=kOutput, calls=%fused_computation.209 | convolution fusion | flops 7233266176 | bytes 25841160 | tf_op jit(solution)/shard_map/dot_general | solution.py:18
  186.4 16.5 %convolution_convert_fusion = bf16[1152,4304]{0,1:T(8,128)(2,1)} fusion(bf16[3,729,1152]{2,1,0:T(8,128)(2,1)} %param.31, s32[]{:T(128)S(6)} %select_n.309, pred[]{:T(512)S(6)} %and.15, f32[729,4304]{1,0:T(8,128)} %fusion.85, f32[4304]{0:T(1024)S(1)} %add.357), kind=kOutput, calls=%fused_computation.2 | convolution fusion | flops 7266241536 | bytes 24441668 | tf_op jit(solution)/shard_map/dot_general | solution.py:18
  202.9 32.5 %all-gather.8.cloned.1.call-done = bf16[1152,4304]{1,0:T(8,128)(2,1)} async-done(((bf16[144,4304]{1,0:T(8,128)(2,1)}), bf16[1152,4304]{1,0:T(8,128)(2,1)}) %all-gather.8.cloned.1.call-update) | async-done | bytes 9916432 | tf_op jit(solution)/shard_map/all_gather | solution.py:233
  235.5 17.7 %convert_reduce_fusion = (f32[4304]{0:T(1024)S(1)}, bf16[729,4304]{1,0:T(8,128)(2,1)S(1)}) fusion(f32[729,4304]{1,0:T(8,128)} %fusion.85, f32[4304]{0:T(1024)S(1)} %add.357, bf16[1152,4304]{1,0:T(8,128)(2,1)} %all-gather.8.cloned.1.call-done, bf16[3,729,1152]{2,1,0:T(8,128)(2,1)} %param.31, s32[]{:T(128)S(6)} %select_n.309, pred[]{:T(512)S(6)} %and.15), kind=kOutput, calls=%fused_computation.13 | convolution fusion | flops 7298928640 | bytes 30844708 | tf_op jit(solution)/shard_map/dot_general | solution.py:18
  255.8 12.2 %convolution_convert_fusion.1 = bf16[1152,4304]{0,1:T(8,128)(2,1)} fusion(bf16[729,4304]{1,0:T(8,128)(2,1)S(1)} %get-tuple-element.206, f32[729,1152]{1,0:T(8,128)S(1)} %get-tuple-element.203, f32[1152]{0:T(1024)S(1)} %add.354, f32[1152]{0:T(1024)S(1)} %mul.184, f32[729]{0:T(1024)S(1)} %add_rsqrt_fusion, f32[729]{0:T(1024)S(1)} %broadcast_multiply_fusion.4), kind=kOutput, calls=%fused_computation.3 | convolution fusion | flops 7238224384 | bytes 19565928 | tf_op jit(solution)/shard_map/dot_general | solution.py:18
  267.9 14.7 %fusion.97 = f32[729,1152]{1,0:T(8,128)} fusion(bf16[729,4304]{1,0:T(8,128)(2,1)} %copy-done.47, bf16[1152,4304]{1,0:T(8,128)(2,1)} %all-gather.6.cloned.1.call-done), kind=kOutput, calls=%fused_computation.221 | convolution fusion | flops 7229067264 | bytes 19550880 | tf_op jit(solution)/shard_map/dot_general | solution.py:18
  282.6 14.1 %copy.78 = bf16[1152,4304]{1,0:T(8,128)(2,1)} copy(bf16[1152,4304]{0,1:T(8,128)(2,1)} %convolution_convert_fusion.1) | data formatting | bytes 19832832
  297.6 17.3 %fusion.39 = bf16[729,1152]{1,0:T(8,128)(2,1)} fusion(f32[729,1152]{1,0:T(8,128)S(1)} %get-tuple-element.203, bf16[1152,4304]{1,0:T(8,128)(2,1)} %all-gather.8.cloned.1.call-done, f32[]{:T(128)} %bitcast.21, f32[1152]{0:T(1024)S(1)} %add.363, f32[729,4304]{1,0:T(8,128)} %fusion.85, f32[4304]{0:T(1024)S(1)} %add.357), kind=kOutput, calls=%fused_computation.64 | convolution fusion | flops 7263802368 | bytes 27527556 | tf_op jit(solution)/shard_map/dot_general | solution.py:18
  342.2 25.1 %attn_bwd.1 = bf16[3,1152,729]{2,1,0:T(8,128)(2,1)} custom-call(bf16[3,1152,729]{2,1,0:T(8,128)(2,1)} %bitcast.246, bf16[1152,729]{1,0:T(8,128)(2,1)} %copy.71.do_ref, bf16[1152,729]{1,0:T(8,128)(2,1)} %get-tuple-element.25.o_ref, bf16[16,729,729]{2,1,0:T(8,128)(2,1)} %get-tuple-element.27.p_ref, f32[16,1,729]{2,1,0:T(1,128)} %get-tuple-element.28.l_ref), custom_call_target="tpu_custom_call" | custom-call | flops 17414258688 | bytes 17006112 | tf_op jit(solution)/shard_map/attn_bwd/pallas_call | solution.py:75
  371.5 13.8 %fusion.33 = (f32[1152]{0:T(1024)S(1)}, f32[729]{0:T(1024)S(1)}, f32[729]{0:T(1024)S(1)}, f32[1152]{0:T(1024)S(1)}, f32[729,1152]{1,0:T(8,128)}) fusion(f32[729]{0:T(1024)S(1)} %copy-done.32, f32[729]{0:T(1024)S(1)} %copy-done.27, bf16[3,729,1152]{2,1,0:T(8,128)(2,1)} %param.16, s32[]{:T(128)S(6)} %select_n.309, f32[1152]{0:T(1024)S(1)} %copy-done.29, ...), kind=kOutput, calls=%fused_computation.52 | convolution fusion | flops 5813146624 | bytes 18081940 | tf_op jit(solution)/shard_map/dot_general | solution.py:18
  386.0 9.7 %convolution_convert_fusion.2 = bf16[1152,3456]{1,0:T(8,128)(2,1)S(1)} fusion(bf16[3456,729]{1,0:T(8,128)(2,1)S(1)} %bitcast.250, f32[1152]{0:T(1024)S(1)} %copy-done.34, f32[1152]{0:T(1024)S(1)} %copy-done.29, f32[729]{0:T(1024)S(1)} %copy-done.32, f32[729]{0:T(1024)S(1)} %copy-done.27, bf16[3,729,1152]{2,1,0:T(8,128)(2,1)} %param.16, s32[]{:T(128)S(6)} %select_n.309), kind=kOutput, calls=%fused_computation.4 | convolution fusion | flops 5813773312 | bytes 14712268 | tf_op jit(solution)/shard_map/dot_general | solution.py:18
  419.7 14.1 %copy.80 = bf16[1152,4304]{1,0:T(8,128)(2,1)} copy(bf16[1152,4304]{0,1:T(8,128)(2,1)} %convolution_convert_fusion) | data formatting | bytes 19832832
  465.9 13.0 %collective-permute-done.27 = bf16[361,1152]{1,0:T(8,128)(2,1)} collective-permute-done((bf16[361,1152]{1,0:T(8,128)(2,1)}, bf16[361,1152]{1,0:T(8,128)(2,1)}, u32[]{:S(2)}, u32[]{:S(2)}) %collective-permute-start.27) | collective-permute-done | bytes 831776 | tf_op jit(solution)/shard_map/ppermute | solution.py:161
  480.8 7.1 collective-permute-done.12
  489.8 7.1 collective-permute-done.9
  496.9 8.8 %collective-permute-start.16 = (bf16[361,1152]{1,0:T(8,128)(2,1)}, bf16[361,1152]{1,0:T(8,128)(2,1)}, u32[]{:S(2)}, u32[]{:S(2)}) collective-permute-start(bf16[361,1152]{1,0:T(8,128)(2,1)} %collective-permute-done.15), channel_id=1, source_target_pairs={{1,2},{5,6},{9,10},{13,14},{17,18},{21,22},{25,26},{29,30}} | collective-permute-start | bytes 2495240 | tf_op jit(solution)/shard_map/ppermute | solution.py:161
  527.2 16.5 %collective-permute-done.31 = bf16[361,1152]{1,0:T(8,128)(2,1)} collective-permute-done((bf16[361,1152]{1,0:T(8,128)(2,1)}, bf16[361,1152]{1,0:T(8,128)(2,1)}, u32[]{:S(2)}, u32[]{:S(2)}) %collective-permute-start.31) | collective-permute-done | bytes 831776 | tf_op jit(solution)/shard_map/ppermute | solution.py:162
  546.3 8.8 %collective-permute-done.53 = bf16[144,288]{1,0:T(8,128)(2,1)S(1)} collective-permute-done((bf16[144,288]{1,0:T(8,128)(2,1)S(1)}, bf16[144,288]{1,0:T(8,128)(2,1)S(1)}, u32[]{:S(2)}, u32[]{:S(2)}) %collective-permute-start.53) | collective-permute-done | bytes 82976 | tf_op jit(solution)/shard_map/ppermute | solution.py:125
  555.1 8.2 %collective-permute-start.54 = (bf16[144,288]{1,0:T(8,128)(2,1)S(1)}, bf16[144,288]{1,0:T(8,128)(2,1)S(1)}, u32[]{:S(2)}, u32[]{:S(2)}) collective-permute-start(bf16[144,288]{1,0:T(8,128)(2,1)S(1)} %bitcast.270), channel_id=1, source_target_pairs={{0,3},{1,0},{2,1},{3,2},{4,7},{5,4},{6,5},{7,6},{8,11},{9,8},{10,9... | collective-permute-start | bytes 248840 | tf_op jit(solution)/shard_map/ppermute | solution.py:125
  584.0 12.5 %collective-permute-done.25 = bf16[368,1152]{1,0:T(8,128)(2,1)} collective-permute-done((bf16[368,1152]{1,0:T(8,128)(2,1)S(1)}, bf16[368,1152]{1,0:T(8,128)(2,1)}, u32[]{:S(2)}, u32[]{:S(2)}) %collective-permute-start.25) | collective-permute-done | bytes 847904 | tf_op jit(solution)/shard_map/ppermute | solution.py:162
  601.7 13.0 %collective-permute-done.32 = bf16[361,1152]{1,0:T(8,128)(2,1)S(1)} collective-permute-done((bf16[361,1152]{1,0:T(8,128)(2,1)}, bf16[361,1152]{1,0:T(8,128)(2,1)S(1)}, u32[]{:S(2)}, u32[]{:S(2)}) %collective-permute-start.32) | collective-permute-done | bytes 831776 | tf_op jit(solution)/shard_map/ppermute | solution.py:162
  624.9 7.9 %collective-permute-done.14 = bf16[368,1152]{1,0:T(8,128)(2,1)S(1)} collective-permute-done((bf16[368,1152]{1,0:T(8,128)(2,1)S(1)}, bf16[368,1152]{1,0:T(8,128)(2,1)S(1)}, u32[]{:S(2)}, u32[]{:S(2)}) %collective-permute-start.14) | collective-permute-done | bytes 847904 | tf_op jit(solution)/shard_map/ppermute | solution.py:162
  643.0 7.6 collective-permute-done.26
  662.8 18.5 %collective-permute-done.40 = bf16[2,80,3456]{2,1,0:T(8,128)(2,1)S(1)} collective-permute-done((bf16[2,80,3456]{2,1,0:T(8,128)(2,1)S(1)}, bf16[2,80,3456]{2,1,0:T(8,128)(2,1)S(1)}, u32[]{:S(2)}, u32[]{:S(2)}) %collective-permute-start.40) | collective-permute-done | bytes 1105952 | tf_op jit(solution)/shard_map/ppermute | solution.py:130
  739.5 18.3 %collective-permute-done.55 = bf16[144,1076]{1,0:T(8,128)(2,1)S(1)} collective-permute-done((bf16[144,1076]{1,0:T(8,128)(2,1)}, bf16[144,1076]{1,0:T(8,128)(2,1)S(1)}, u32[]{:S(2)}, u32[]{:S(2)}) %collective-permute-start.55) | collective-permute-done | bytes 309920 | tf_op jit(solution)/shard_map/ppermute | solution.py:125
  (381 shorter events, 300.9 us)
Async XLA Ops:
  7.2 108.9 %all-gather.4.cloned.1.call-start = ((), (), s32[]{:S(2)}) async-start(), calls=%async_computation.2 | async-start | bytes 11943936 | tf_op jit(solution)/shard_map/all_gather | solution.py:226
  43.8 128.0 %all-gather.6.cloned.1.call-start = ((), (), s32[]{:S(2)}) async-start(), calls=%async_computation.3 | async-start | bytes 11280384 | tf_op jit(solution)/shard_map/all_gather | solution.py:232
  44.1 54.3 %collective-permute-start.6 = (bf16[144,2152]{1,0:T(8,128)(2,1)S(1)}, bf16[144,2152]{1,0:T(8,128)(2,1)S(1)}, u32[]{:S(2)}, u32[]{:S(2)}) collective-permute-start(bf16[144,2152]{1,0:T(8,128)(2,1)S(1)} %pad_maximum_fusion.3), channel_id=1, source_target_pairs={{0,1},{1,2},{2,3},{3,0},{4,5},{5,6},{6,7},{7,4},{8,9},{9,10},{10,1... | collective-permute-start | bytes 1859336 | tf_op jit(solution)/shard_map/ppermute | solution.py:125
  46.7 54.6 %collective-permute-start.8 = (bf16[144,2152]{1,0:T(8,128)(2,1)S(1)}, bf16[144,2152]{1,0:T(8,128)(2,1)S(1)}, u32[]{:S(2)}, u32[]{:S(2)}) collective-permute-start(bf16[144,2152]{1,0:T(8,128)(2,1)S(1)} %pad_maximum_fusion.3), channel_id=1, source_target_pairs={{0,3},{1,0},{2,1},{3,2},{4,7},{5,4},{6,5},{7,6},{8,11},{9,8},{10,9... | collective-permute-start | bytes 1859336 | tf_op jit(solution)/shard_map/ppermute | solution.py:125
  104.8 130.7 %all-gather.8.cloned.1.call-start = ((), (), s32[]{:S(2)}) async-start(), calls=%async_computation.4 | async-start | bytes 11280384 | tf_op jit(solution)/shard_map/all_gather | solution.py:233
  107.0 597.9 %reduce-scatter.7.cloned.1.call-start = ((), (), s32[]{:S(2)}) async-start(), calls=%async_computation.5 | async-start | bytes 11280384 | tf_op jit(solution)/shard_map/reduce_scatter | solution.py:334
  296.7 411.4 %reduce-scatter.9.cloned.1.call-start = ((), (), s32[]{:S(2)}) async-start(), calls=%async_computation.6 | async-start | bytes 11280384 | tf_op jit(solution)/shard_map/reduce_scatter | solution.py:334
  319.5 97.0 %collective-permute-start.63 = (f32[16]{0:T(128)S(1)}, f32[16]{0:T(128)S(1)}, u32[]{:S(2)}, u32[]{:S(2)}) collective-permute-start(f32[16]{0:T(128)S(1)} %fusion.80), channel_id=1, source_target_pairs={{0,3},{1,0},{2,1},{3,2},{4,7},{5,4},{6,5},{7,6},{8,11},{9,8},{10,9... | collective-permute-start | bytes 200 | tf_op jit(solution)/shard_map/ppermute | solution.py:125
  341.8 98.7 %collective-permute-start.47 = (bf16[2,2,144,1152]{3,2,1,0:T(8,128)(2,1)S(1)}, bf16[2,2,144,1152]{3,2,1,0:T(8,128)(2,1)}, u32[]{:S(2)}, u32[]{:S(2)}) collective-permute-start(bf16[2,2,144,1152]{3,2,1,0:T(8,128)(2,1)S(1)} %dynamic-slice_bitcast_fusion.1), channel_id=1, source_target_pairs={{0,4},{4,0},{8,12},{12,8},{16,20},{20,16},{24,28},{28,24},{1,5},{5... | collective-permute-start | bytes 3981320 | tf_op jit(solution)/shard_map/ppermute | solution.py:130
  415.2 40.0 %collective-permute-start.18 = (bf16[361,1152]{1,0:T(8,128)(2,1)}, bf16[361,1152]{1,0:T(8,128)(2,1)}, u32[]{:S(2)}, u32[]{:S(2)}) collective-permute-start(bf16[361,1152]{1,0:T(8,128)(2,1)} %slice.267), channel_id=1, source_target_pairs={{2,1},{3,2},{6,5},{7,6},{10,9},{11,10},{14,13},{15,14},{18,17},{19... | collective-permute-start | bytes 2495240 | tf_op jit(solution)/shard_map/ppermute | solution.py:162
  416.5 40.0 %collective-permute-start.15 = (bf16[361,1152]{1,0:T(8,128)(2,1)}, bf16[361,1152]{1,0:T(8,128)(2,1)}, u32[]{:S(2)}, u32[]{:S(2)}) collective-permute-start(bf16[361,1152]{1,0:T(8,128)(2,1)} %slice.267), channel_id=1, source_target_pairs={{0,1},{2,3},{4,5},{6,7},{8,9},{10,11},{12,13},{14,15},{16,17},{18,... | collective-permute-start | bytes 2495240 | tf_op jit(solution)/shard_map/ppermute | solution.py:161
  455.2 32.8 %collective-permute-start.12 = (bf16[368,1152]{1,0:T(8,128)(2,1)S(1)}, bf16[368,1152]{1,0:T(8,128)(2,1)S(1)}, u32[]{:S(2)}, u32[]{:S(2)}) collective-permute-start(bf16[368,1152]{1,0:T(8,128)(2,1)S(1)} %copy-done.19), channel_id=1, source_target_pairs={{2,1},{3,2},{6,5},{7,6},{10,9},{11,10},{14,13},{15,14},{18,17},{19... | collective-permute-start | bytes 2543624 | tf_op jit(solution)/shard_map/ppermute | solution.py:162
  456.5 40.5 %collective-permute-start.9 = (bf16[368,1152]{1,0:T(8,128)(2,1)S(1)}, bf16[368,1152]{1,0:T(8,128)(2,1)S(1)}, u32[]{:S(2)}, u32[]{:S(2)}) collective-permute-start(bf16[368,1152]{1,0:T(8,128)(2,1)S(1)} %copy-done.19), channel_id=1, source_target_pairs={{0,1},{2,3},{4,5},{6,7},{8,9},{10,11},{12,13},{14,15},{16,17},{18,... | collective-permute-start | bytes 2543624 | tf_op jit(solution)/shard_map/ppermute | solution.py:161
  460.8 45.2 %collective-permute-start.24 = (bf16[368,1152]{1,0:T(8,128)(2,1)}, bf16[368,1152]{1,0:T(8,128)(2,1)S(1)}, u32[]{:S(2)}, u32[]{:S(2)}) collective-permute-start(bf16[368,1152]{1,0:T(8,128)(2,1)} %slice.268), channel_id=1, source_target_pairs={{2,1},{3,2},{6,5},{7,6},{10,9},{11,10},{14,13},{15,14},{18,17},{19... | collective-permute-start | bytes 2543624 | tf_op jit(solution)/shard_map/ppermute | solution.py:162
  478.9 40.4 %collective-permute-start.21 = (bf16[368,1152]{1,0:T(8,128)(2,1)}, bf16[368,1152]{1,0:T(8,128)(2,1)}, u32[]{:S(2)}, u32[]{:S(2)}) collective-permute-start(bf16[368,1152]{1,0:T(8,128)(2,1)} %slice.268), channel_id=1, source_target_pairs={{0,1},{2,3},{4,5},{6,7},{8,9},{10,11},{12,13},{14,15},{16,17},{18,... | collective-permute-start | bytes 2543624 | tf_op jit(solution)/shard_map/ppermute | solution.py:161
  487.9 36.4 %collective-permute-start.19 = (bf16[361,1152]{1,0:T(8,128)(2,1)}, bf16[361,1152]{1,0:T(8,128)(2,1)}, u32[]{:S(2)}, u32[]{:S(2)}) collective-permute-start(bf16[361,1152]{1,0:T(8,128)(2,1)} %collective-permute-done.18), channel_id=1, source_target_pairs={{1,0},{2,1},{5,4},{6,5},{9,8},{10,9},{13,12},{14,13},{17,16},{18,1... | collective-permute-start | bytes 2495240 | tf_op jit(solution)/shard_map/ppermute | solution.py:162
  506.1 37.6 %collective-permute-start.31 = (bf16[361,1152]{1,0:T(8,128)(2,1)}, bf16[361,1152]{1,0:T(8,128)(2,1)}, u32[]{:S(2)}, u32[]{:S(2)}) collective-permute-start(bf16[361,1152]{1,0:T(8,128)(2,1)} %collective-permute-done.30), channel_id=1, source_target_pairs={{1,0},{2,1},{5,4},{6,5},{9,8},{10,9},{13,12},{14,13},{17,16},{18,1... | collective-permute-start | bytes 2495240 | tf_op jit(solution)/shard_map/ppermute | solution.py:162
  508.0 36.4 %collective-permute-start.28 = (bf16[361,1152]{1,0:T(8,128)(2,1)}, bf16[361,1152]{1,0:T(8,128)(2,1)}, u32[]{:S(2)}, u32[]{:S(2)}) collective-permute-start(bf16[361,1152]{1,0:T(8,128)(2,1)} %collective-permute-done.27), channel_id=1, source_target_pairs={{1,2},{5,6},{9,10},{13,14},{17,18},{21,22},{25,26},{29,30}} | collective-permute-start | bytes 2495240 | tf_op jit(solution)/shard_map/ppermute | solution.py:161
  519.3 52.2 %collective-permute-start.13 = (bf16[368,1152]{1,0:T(8,128)(2,1)}, bf16[368,1152]{1,0:T(8,128)(2,1)S(1)}, u32[]{:S(2)}, u32[]{:S(2)}) collective-permute-start(bf16[368,1152]{1,0:T(8,128)(2,1)} %copy-done.22), channel_id=1, source_target_pairs={{1,0},{2,1},{5,4},{6,5},{9,8},{10,9},{13,12},{14,13},{17,16},{18,1... | collective-permute-start | bytes 2543624 | tf_op jit(solution)/shard_map/ppermute | solution.py:162
  524.4 52.9 %collective-permute-start.10 = (bf16[368,1152]{1,0:T(8,128)(2,1)}, bf16[368,1152]{1,0:T(8,128)(2,1)S(1)}, u32[]{:S(2)}, u32[]{:S(2)}) collective-permute-start(bf16[368,1152]{1,0:T(8,128)(2,1)} %copy-done.24), channel_id=1, source_target_pairs={{1,2},{5,6},{9,10},{13,14},{17,18},{21,22},{25,26},{29,30}} | collective-permute-start | bytes 2543624 | tf_op jit(solution)/shard_map/ppermute | solution.py:161
  525.9 53.6 %collective-permute-start.20 = (bf16[361,1152]{1,0:T(8,128)(2,1)}, bf16[361,1152]{1,0:T(8,128)(2,1)S(1)}, u32[]{:S(2)}, u32[]{:S(2)}) collective-permute-start(bf16[361,1152]{1,0:T(8,128)(2,1)} %collective-permute-done.19), channel_id=1, source_target_pairs={{1,0},{5,4},{9,8},{13,12},{17,16},{21,20},{25,24},{29,28}} | collective-permute-start | bytes 2495240 | tf_op jit(solution)/shard_map/ppermute | solution.py:162
  543.7 37.3 %collective-permute-start.17 = (bf16[361,1152]{1,0:T(8,128)(2,1)}, bf16[361,1152]{1,0:T(8,128)(2,1)S(1)}, u32[]{:S(2)}, u32[]{:S(2)}) collective-permute-start(bf16[361,1152]{1,0:T(8,128)(2,1)} %collective-permute-done.16), channel_id=1, source_target_pairs={{2,3},{6,7},{10,11},{14,15},{18,19},{22,23},{26,27},{30,31}} | collective-permute-start | bytes 2495240 | tf_op jit(solution)/shard_map/ppermute | solution.py:161
  570.8 65.4 %collective-permute-start.39 = (bf16[2,2,144,3456]{3,2,1,0:T(8,128)(2,1)}, bf16[2,2,144,3456]{3,2,1,0:T(8,128)(2,1)S(1)}, u32[]{:S(2)}, u32[]{:S(2)}) collective-permute-start(bf16[2,2,144,3456]{3,2,1,0:T(8,128)(2,1)} %dynamic-slice_bitcast_fusion), channel_id=1, source_target_pairs={{0,4},{4,0},{8,12},{12,8},{16,20},{20,16},{24,28},{28,24},{1,5},{5... | collective-permute-start | bytes 11943944 | tf_op jit(solution)/shard_map/ppermute | solution.py:130
  579.5 35.3 %collective-permute-start.32 = (bf16[361,1152]{1,0:T(8,128)(2,1)}, bf16[361,1152]{1,0:T(8,128)(2,1)S(1)}, u32[]{:S(2)}, u32[]{:S(2)}) collective-permute-start(bf16[361,1152]{1,0:T(8,128)(2,1)} %collective-permute-done.31), channel_id=1, source_target_pairs={{1,0},{5,4},{9,8},{13,12},{17,16},{21,20},{25,24},{29,28}} | collective-permute-start | bytes 2495240 | tf_op jit(solution)/shard_map/ppermute | solution.py:162
  581.1 38.8 %collective-permute-start.29 = (bf16[361,1152]{1,0:T(8,128)(2,1)}, bf16[361,1152]{1,0:T(8,128)(2,1)S(1)}, u32[]{:S(2)}, u32[]{:S(2)}) collective-permute-start(bf16[361,1152]{1,0:T(8,128)(2,1)} %collective-permute-done.28), channel_id=1, source_target_pairs={{2,3},{6,7},{10,11},{14,15},{18,19},{22,23},{26,27},{30,31}} | collective-permute-start | bytes 2495240 | tf_op jit(solution)/shard_map/ppermute | solution.py:161
  596.5 36.3 %collective-permute-start.14 = (bf16[368,1152]{1,0:T(8,128)(2,1)S(1)}, bf16[368,1152]{1,0:T(8,128)(2,1)S(1)}, u32[]{:S(2)}, u32[]{:S(2)}) collective-permute-start(bf16[368,1152]{1,0:T(8,128)(2,1)S(1)} %collective-permute-done.13), channel_id=1, source_target_pairs={{1,0},{5,4},{9,8},{13,12},{17,16},{21,20},{25,24},{29,28}} | collective-permute-start | bytes 2543624 | tf_op jit(solution)/shard_map/ppermute | solution.py:162
  614.7 35.9 %collective-permute-start.26 = (bf16[368,1152]{1,0:T(8,128)(2,1)}, bf16[368,1152]{1,0:T(8,128)(2,1)}, u32[]{:S(2)}, u32[]{:S(2)}) collective-permute-start(bf16[368,1152]{1,0:T(8,128)(2,1)} %collective-permute-done.25), channel_id=1, source_target_pairs={{1,0},{5,4},{9,8},{13,12},{17,16},{21,20},{25,24},{29,28}} | collective-permute-start | bytes 2543624 | tf_op jit(solution)/shard_map/ppermute | solution.py:162
  719.9 37.9 %collective-permute-start.55 = (bf16[144,1076]{1,0:T(8,128)(2,1)}, bf16[144,1076]{1,0:T(8,128)(2,1)S(1)}, u32[]{:S(2)}, u32[]{:S(2)}) collective-permute-start(bf16[144,1076]{1,0:T(8,128)(2,1)} %bitcast.237), channel_id=1, source_target_pairs={{0,1},{1,2},{2,3},{3,0},{4,5},{5,6},{6,7},{7,4},{8,9},{9,10},{10,1... | collective-permute-start | bytes 929672 | tf_op jit(solution)/shard_map/ppermute | solution.py:125
  722.7 37.6 %collective-permute-start.57 = (bf16[144,1076]{1,0:T(8,128)(2,1)}, bf16[144,1076]{1,0:T(8,128)(2,1)}, u32[]{:S(2)}, u32[]{:S(2)}) collective-permute-start(bf16[144,1076]{1,0:T(8,128)(2,1)} %bitcast.235), channel_id=1, source_target_pairs={{0,3},{1,0},{2,1},{3,2},{4,7},{5,4},{6,5},{7,6},{8,11},{9,8},{10,9... | collective-permute-start | bytes 929672 | tf_op jit(solution)/shard_map/ppermute | solution.py:125
  722.7 42.4 %collective-permute-start.56 = (bf16[144,1076]{1,0:T(8,128)(2,1)}, bf16[144,1076]{1,0:T(8,128)(2,1)}, u32[]{:S(2)}, u32[]{:S(2)}) collective-permute-start(bf16[144,1076]{1,0:T(8,128)(2,1)} %bitcast.236), channel_id=1, source_target_pairs={{0,2},{1,3},{2,0},{3,1},{4,6},{5,7},{6,4},{7,5},{8,10},{9,11},{10,... | collective-permute-start | bytes 929672 | tf_op jit(solution)/shard_map/ppermute | solution.py:125
  735.6 36.5 %collective-permute-start.59 = (bf16[144,1076]{1,0:T(8,128)(2,1)S(1)}, bf16[144,1076]{1,0:T(8,128)(2,1)S(1)}, u32[]{:S(2)}, u32[]{:S(2)}) collective-permute-start(bf16[144,1076]{1,0:T(8,128)(2,1)S(1)} %bitcast.264), channel_id=1, source_target_pairs={{0,2},{1,3},{2,0},{3,1},{4,6},{5,7},{6,4},{7,5},{8,10},{9,11},{10,... | collective-permute-start | bytes 929672 | tf_op jit(solution)/shard_map/ppermute | solution.py:125
  737.2 41.4 %collective-permute-start.60 = (bf16[144,1076]{1,0:T(8,128)(2,1)S(1)}, bf16[144,1076]{1,0:T(8,128)(2,1)S(1)}, u32[]{:S(2)}, u32[]{:S(2)}) collective-permute-start(bf16[144,1076]{1,0:T(8,128)(2,1)S(1)} %bitcast.263), channel_id=1, source_target_pairs={{0,3},{1,0},{2,1},{3,2},{4,7},{5,4},{6,5},{7,6},{8,11},{9,8},{10,9... | collective-permute-start | bytes 929672 | tf_op jit(solution)/shard_map/ppermute | solution.py:125
  (90 other events, 1425.5 us)
Sparse Core Ops, SparseCore 0:
  43.9 64.6 all-gather.3
  110.6 61.1 all-gather.5
  174.2 61.1 all-gather.7
  296.9 79.5 reduce-scatter.6
  434.6 88.9 reduce-scatter.8

commit v3 on v2

--- a/solution.py
+++ b/solution.py
@@ -116,18 +116,9 @@
     return lax.dynamic_index_in_dim(block, index, axis, keepdims=False)
 
 
-def plus(a, b):
-    return (a.astype(F32) + b.astype(F32)).astype(BF16)
-
-
 def shift(block, by):
     parts = lax.axis_size("tensor")
     return lax.ppermute(block, "tensor", [(z, (z + by) % parts) for z in range(parts)])
-
-
-def flip(block, bit):
-    size = lax.axis_size("fsdp")
-    return lax.ppermute(block, "fsdp", [(i, i ^ (1 << bit)) for i in range(size)])
 
 
 def line_gather(block):
@@ -137,64 +128,323 @@
     return [pick(near, lax.rem(me - z + parts, parts)) for z in range(parts)]
 
 
-def line_scatter(blocks):
+def line_share(block, owners):
     parts = lax.axis_size("tensor")
     me = lax.axis_index("tensor")
-    total = pick(blocks, me).astype(F32)
-    for k in range(1, parts):
-        total = total + shift(pick(blocks, lax.rem(me + k, parts)), k).astype(F32)
-    return total
-
-
-def line_share(block, owners, chunks):
+    far = [block] + [
+        lax.ppermute(block, "tensor", [(z, (z + k) % parts) for z in owners]) for k in range(1, parts)]
+    outs = []
+    for z in owners:
+        out = block
+        for k in range(1, parts):
+            out = jnp.where(me == (z + k) % parts, far[k], out)
+        outs.append(out)
+    return jnp.stack(outs)
+
+
+def wgrad_kernel(x_ref, y_ref, out_ref):
+    out_ref[...] = dot(x_ref[...], y_ref[...], 0, 0).astype(BF16)
+
+
+def wgrad(x, y, tile=512):
+    length, width = x.shape
+    cols = y.shape[1]
+    return pl.pallas_call(
+        wgrad_kernel,
+        grid=(-(-cols // tile),),
+        in_specs=[
+            pl.BlockSpec((length, width), lambda i: (0, 0)),
+            pl.BlockSpec((length, tile), lambda i: (0, i)),
+        ],
+        out_specs=pl.BlockSpec((width, tile), lambda i: (0, i)),
+        out_shape=jax.ShapeDtypeStruct((width, cols), BF16),
+        cost_estimate=pl.CostEstimate(
+            flops=2 * length * width * cols, bytes_accessed=2 * (length + width) * cols, transcendentals=0),
+        name="wgrad",
+    )(x, y)
+
+
+def add_rows(dst, src, rows):
+    step = 16 if rows % 16 == 0 else 8
+
+    def body(i, carry):
+        at = pl.ds(pl.multiple_of(i * step, step), step)
+        dst[at, :] = (dst[at, :].astype(F32) + src[at, :].astype(F32)).astype(BF16)
+        return carry
+
+    lax.fori_loop(0, rows // step, body, 0)
+
+
+def tail_kernel(plan, *refs):
+    parts, fsdp, owners, spans, mats, rows, cut, summed = plan
+    bits = fsdp.bit_length() - 1
+    part_bits = parts.bit_length() - 1
+    chips = fsdp // 2
+    slots, chunks = len(owners), len(spans)
+    refs = list(refs)
+    take = lambda n: [refs.pop(0) for _ in range(n)]
+    grads = take(mats)
+    image, vec = take(2)
+    sums = take(mats)
+    shared, total = take(2)
+    own = take(mats)
+    other = take(mats)
+    halves = [[take(bits - 1) for _ in range(2)] for _ in range(mats)]
+    walk, meet = take(2)
+    core_send, core_recv, local_sem, half_send, half_recv, hop_send, hop_recv, vec_send, vec_recv = take(9)
+    place = lax.axis_index("fsdp")
+    me = lax.axis_index("tensor")
+
+    def moved(index, mask):
+        out = index
+        for b in range(8):
+            if mask >> b & 1:
+                out = out + (1 - 2 * ((index // 2**b) % 2)) * 2**b
+        return out
+
+    barrier = pltpu.get_barrier_semaphore()
+    for b in range(bits):
+        pl.semaphore_signal(barrier, inc=1, device_id={"fsdp": moved(place, 1 << b)}, device_id_type=pl.DeviceIdType.MESH)
+    for b in range(part_bits):
+        pl.semaphore_signal(barrier, inc=1, device_id={"tensor": moved(me, 1 << b)}, device_id_type=pl.DeviceIdType.MESH)
+    for m in range(parts):
+        near = [z for z in (m - 1, m + 1) if 0 <= z < parts]
+
+        @pl.when(me == m)
+        def _():
+            for z in near:
+                pl.semaphore_signal(barrier, inc=1, device_id={"tensor": me + (z - m)}, device_id_type=pl.DeviceIdType.MESH)
+            pl.semaphore_wait(barrier, bits + part_bits + len(near))
+
+    def hop(j, c, side, m):
+        lo, hi = spans[c]
+        rows_at = pl.ds(lo, hi - lo)
+        src = image.at[rows_at] if owners[j] == m else shared.at[j, rows_at]
+        return pltpu.make_async_remote_copy(
+            src_ref=src, dst_ref=shared.at[j, rows_at], send_sem=hop_send.at[side, j, c],
+            recv_sem=hop_recv.at[j, c], device_id={"tensor": me + (2 * side - 1)},
+            device_id_type=pl.DeviceIdType.MESH)
+
+    sent = [[] for _ in range(parts)]
+
+    def send_hop(j, c, side, m):
+        hop(j, c, side, m).start()
+        sent[m].append((j, c, side))
+
+    def arrive(m, first):
+        order = sorted((abs(owners[j] - m) * chunks + c, j, c) for j in range(slots) for c in range(chunks) if owners[j] != m)
+        for key, j, c in order:
+            if (key < 2 * chunks) != first:
+                continue
+            side = 1 if m > owners[j] else 0
+            hop(j, c, 0 if m > 0 else 1, m).wait_recv()
+            if 0 <= m + 2 * side - 1 < parts:
+                send_hop(j, c, side, m)
+
+    for m in range(parts):
+        if m in owners:
+
+            @pl.when(me == m)
+            def _():
+                for c in range(chunks):
+                    for side in (1, 0):
+                        if 0 <= m + 2 * side - 1 < parts:
+                            send_hop(owners.index(m), c, side, m)
+
+    mine = place % 2
+    chip = place - mine
+    order = sorted(range(chips), key=lambda r: (-bin(r).count("1"), r))
+    cores, locals_ = {}, {}
+    for r in order:
+        base = moved(chip, 2 * r)
+        for i in range(mats):
+            cores[r, i] = pltpu.make_async_remote_copy(
+                src_ref=grads[i].at[base + 1 - mine], dst_ref=other[i].at[r], send_sem=core_send.at[i, r],
+                recv_sem=core_recv.at[i, r], device_id={"fsdp": moved(place, 1)}, device_id_type=pl.DeviceIdType.MESH)
+            cores[r, i].start()
+            locals_[r, i] = pltpu.make_async_copy(grads[i].at[base + mine], own[i].at[r], local_sem.at[i, r])
+            locals_[r, i].start()
+    for r in order:
+        for i in range(mats):
+            cores[r, i].wait_recv()
+            locals_[r, i].wait()
+            add_rows(own[i].at[r], other[i].at[r], rows)
+
+    ranges = ((0, cut), (cut, rows))
+    orders = (list(range(bits - 1)), list(range(bits - 2, -1, -1)))
+    left = [list(range(chips)), list(range(chips))]
+    flying = []
+    for s in range(bits - 1):
+        landing = []
+        for h in range(2):
+            lo, hi = ranges[h]
+            b = 1 << orders[h][s]
+            stay = [r for r in left[h] if not r & b]
+            left[h] = stay
+            for k, r in enumerate(stay):
+                for i in range(mats):
+                    copy = pltpu.make_async_remote_copy(
+                        src_ref=own[i].at[r | b, pl.ds(lo, hi - lo)], dst_ref=halves[i][h][s].at[k],
+                        send_sem=half_send.at[i, h, s, k], recv_sem=half_recv.at[i, h, s, k],
+                        device_id={"fsdp": moved(place, 2 * b)}, device_id_type=pl.DeviceIdType.MESH)
+                    copy.start()
+                    flying.append(copy)
+                    landing.append((copy, own[i].at[r, pl.ds(lo, hi - lo)], halves[i][h][s].at[k], hi - lo))
+        if s == 0:
+            walk[0] = vec[...]
+            partners = [("fsdp", place, b) for b in range(bits)] + [("tensor", me, b) for b in range(part_bits)]
+            for k, (axis, index, b) in enumerate(partners):
+                copy = pltpu.make_async_remote_copy(
+                    src_ref=walk.at[k], dst_ref=meet.at[k], send_sem=vec_send.at[k], recv_sem=vec_recv.at[k],
+                    device_id={axis: moved(index, 1 << b)}, device_id_type=pl.DeviceIdType.MESH)
+                copy.start()
+                flying.append(copy)
+                copy.wait_recv()
+                walk[k + 1, :summed] = walk[k, :summed] + meet[k, :summed]
+                walk[k + 1, summed:] = jnp.maximum(walk[k, summed:], meet[k, summed:])
+            total[...] = walk[len(partners)]
+        if s == 0:
+            for m in range(parts):
+
+                @pl.when(me == m)
+                def _():
+                    arrive(m, True)
+
+        for copy, dst, src, count in landing:
+            copy.wait_recv()
+            add_rows(dst, src, count)
+    for i in range(mats):
+        sums[i][...] = own[i][0]
+    for m in range(parts):
+
+        @pl.when(me == m)
+        def _():
+            arrive(m, False)
+            for j, c, side in sent[m]:
+                hop(j, c, side, m).wait_send()
+
+    for r in order:
+        for i in range(mats):
+            cores[r, i].wait_send()
+    for copy in flying:
+        copy.wait_send()
+
+
+def tail(grads, image, vec, summed, owners, chunks):
     parts = lax.axis_size("tensor")
+    fsdp = lax.axis_size("fsdp")
+    bits, part_bits = fsdp.bit_length() - 1, parts.bit_length() - 1
+    chips = fsdp // 2
+    length, width = image.shape
+    rows = grads[0].shape[0] // fsdp
+    grads = [g.reshape(fsdp, rows, g.shape[1]) for g in grads]
+    cols = [g.shape[2] for g in grads]
+    cut = -(-(rows // 2) // 16) * 16
+    step = -(-length // chunks // 16) * 16
+    spans = tuple((at, min(at + step, length)) for at in range(0, length, step))
+    mats, slots, steps = len(grads), len(owners), bits + part_bits
+    any_spec = pl.BlockSpec(memory_space=pl.ANY)
+    vmem = pl.BlockSpec(memory_space=pltpu.VMEM)
+    scratch = [pltpu.VMEM((chips, rows, c), BF16) for c in cols] * 2
+    for c in cols:
+        for count in (cut, rows - cut):
+            scratch += [pltpu.VMEM((chips >> (s + 1), count, c), BF16) for s in range(bits - 1)]
+    scratch += [pltpu.VMEM((steps + 1,) + vec.shape, F32), pltpu.VMEM((steps,) + vec.shape, F32)]
+    dma = pltpu.SemaphoreType.DMA
+    scratch += [
+        dma((mats, chips)), dma((mats, chips)), dma((mats, chips)),
+        dma((mats, 2, bits - 1, chips // 2)), dma((mats, 2, bits - 1, chips // 2)),
+        dma((2, slots, len(spans))), dma((slots, len(spans))), dma((steps,)), dma((steps,)),
+    ]
+    plan = (parts, fsdp, tuple(owners), spans, mats, rows, cut, summed)
+    return pl.pallas_call(
+        partial(tail_kernel, plan),
+        in_specs=[any_spec] * (mats + 1) + [vmem],
+        out_specs=[vmem] * mats + [any_spec, vmem],
+        out_shape=[jax.ShapeDtypeStruct((rows, c), BF16) for c in cols]
+        + [jax.ShapeDtypeStruct((slots, length, width), BF16), jax.ShapeDtypeStruct(vec.shape, F32)],
+        scratch_shapes=scratch,
+        compiler_params=pltpu.CompilerParams(collective_id=0, has_side_effects=True),
+        cost_estimate=pl.CostEstimate(flops=0, bytes_accessed=250_000_000, transcendentals=0),
+        name="tail",
+    )(*grads, image, vec)
+
+
+def line_kernel(parts, mats, rows, *refs):
+    own, outs, up, down = (refs[i * mats : (i + 1) * mats] for i in range(4))
+    send_sem, recv_sem = refs[4 * mats :]
     me = lax.axis_index("tensor")
-    rows = block.shape[0]
-    step = -(-rows // chunks // 16) * 16
-    found = []
-    for at in range(0, rows, step):
-        part = block[at : min(at + step, rows)]
-        below, above = [part], [part]
-        for s in range(1, parts):
-            up = [(z, z + 1) for z in range(parts - 1) if z - s + 1 in owners]
-            down = [(z, z - 1) for z in range(1, parts) if z + s - 1 in owners]
-            below.append(lax.ppermute(below[-1], "tensor", up) if up else None)
-            above.append(lax.ppermute(above[-1], "tensor", down) if down else None)
-        outs = []
-        for z in owners:
-            out = part
-            for other in range(parts):
-                if other > z:
-                    out = jnp.where(me == other, below[other - z], out)
-                elif other < z:
-                    out = jnp.where(me == other, above[z - other], out)
-            outs.append(out)
-        found.append(jnp.stack(outs))
-    return jnp.concatenate(found, axis=1)
-
-
-def plane_scatter(block):
-    size = lax.axis_size("fsdp")
-    me = lax.axis_index("fsdp")
-    bits = size.bit_length() - 1
-    rows, cols = block.shape[0] // size, block.shape[1]
-    block = block.reshape((2,) * bits + (rows, cols))
-
-    def halve(part, bit, axis):
-        own = lax.rem(lax.shift_right_logical(me, bit), 2)
-        return plus(pick(part, own, axis), flip(pick(part, 1 - own, axis), bit))
-
-    block = halve(block, 0, bits - 1)
-    cut = -(-(rows // 2) // 16) * 16
-    outs = []
-    for lo, hi, order in ((0, cut, list(range(1, bits))), (cut, rows, list(range(bits - 1, 0, -1)))):
-        part = lax.slice_in_dim(block, lo, hi, axis=bits - 1)
-        left = list(range(bits - 1, 0, -1))
-        for bit in order:
-            part = halve(part, bit, left.index(bit))
-            left.remove(bit)
-        outs.append(part)
-    return jnp.concatenate(outs, axis=0)
+    barrier = pltpu.get_barrier_semaphore()
+    step = 16 if rows % 16 == 0 else 8
+
+    def copy(i, t, side, m, way=None):
+        land = (down, up)[side][i]
+        src = own[i] if m == (parts - 1, 0)[side] else land
+        return pltpu.make_async_remote_copy(
+            src_ref=src.at[t], dst_ref=land.at[t], send_sem=send_sem.at[side, i, t],
+            recv_sem=recv_sem.at[side, i, t], device_id={"tensor": me + (way or 2 * side - 1)},
+            device_id_type=pl.DeviceIdType.MESH)
+
+    for m in range(parts):
+        near = [z for z in (m - 1, m + 1) if 0 <= z < parts]
+
+        @pl.when(me == m)
+        def _():
+            for z in near:
+                pl.semaphore_signal(barrier, inc=1, device_id={"tensor": me + (z - m)}, device_id_type=pl.DeviceIdType.MESH)
+            pl.semaphore_wait(barrier, len(near))
+
+    for m in range(parts):
+
+        @pl.when(me == m)
+        def _():
+            ups = [(1, t) for t in range(parts - 1, m, -1)]
+            downs = [(0, t) for t in range(m)]
+            turn = []
+            for k in range(parts):
+                turn += ups[k : k + 1] + downs[k : k + 1]
+            for side, t in turn:
+                for i in range(mats):
+                    if m != (parts - 1, 0)[side]:
+                        copy(i, t, side, m).wait_recv()
+                        add_rows((down, up)[side][i].at[t], own[i].at[t], rows)
+                    copy(i, t, side, m).start()
+            for i in range(mats):
+                for side in (1, 0):
+                    if m != (parts - 1, 0)[side]:
+                        copy(i, m, side, m, 1 - 2 * side).wait_recv()
+
+                def body(k, carry):
+                    at = pl.ds(pl.multiple_of(k * step, step), step)
+                    value = own[i][m, at, :].astype(F32)
+                    if m > 0:
+                        value = value + up[i][m, at, :].astype(F32)
+                    if m < parts - 1:
+                        value = value + down[i][m, at, :].astype(F32)
+                    outs[i][at, :] = value
+                    return carry
+
+                lax.fori_loop(0, rows // step, body, 0)
+            for side, t in turn:
+                for i in range(mats):
+                    copy(i, t, side, m).wait_send()
+
+
+def line_reduce(blocks):
+    parts = lax.axis_size("tensor")
+    mats, rows = len(blocks), blocks[0].shape[1]
+    vmem = pl.BlockSpec(memory_space=pltpu.VMEM)
+    dma = pltpu.SemaphoreType.DMA
+    return pl.pallas_call(
+        partial(line_kernel, parts, mats, rows),
+        in_specs=[vmem] * mats,
+        out_specs=[vmem] * mats,
+        out_shape=[jax.ShapeDtypeStruct(b.shape[1:], F32) for b in blocks],
+        scratch_shapes=[pltpu.VMEM(b.shape, BF16) for b in blocks] * 2 + [dma((2, mats, parts)), dma((2, mats, parts))],
+        compiler_params=pltpu.CompilerParams(collective_id=1, has_side_effects=True),
+        cost_estimate=pl.CostEstimate(flops=0, bytes_accessed=200_000_000, transcendentals=0),
+        name="line_reduce",
+    )(*blocks)
 
 
 def on_device(
@@ -266,11 +516,11 @@
         0.7978845608028654 * (1.0 + 3 * 0.044715 * pre * pre)
     )
     layer = ((resid + dot(act, down_full, 1, 1) + bias_down) * keep).astype(BF16)
-    layer_out = line_share(layer, owners, CHUNKS)
-
-    g_down = dot(error, act, 0, 0).astype(BF16)
+    layer_out = line_share(layer, owners)
+
+    g_down = wgrad(error, act)
     d_pre = (dot(error, down_full, 1, 0) * slope).astype(BF16)
-    g_up = dot(a_two, d_pre, 0, 0).astype(BF16)
+    g_up = wgrad(a_two, d_pre)
     d_two = dot(d_pre, up_full, 1, 1)
     d_two, g_up, g_down = lax.optimization_barrier((d_two, g_up, g_down))
     up_err = error.astype(F32)
@@ -282,18 +532,7 @@
     g_qkv = dot(a_one, d_qkv, 0, 1).astype(BF16)
     d_one = dot(d_qkv, qkv_full, 0, 1)
     d_image = d_resid + norm_back(d_one, normed_one, inverse_one, gain_one)
-    grad_tokens = line_share(d_image.astype(BF16), owners, CHUNKS).astype(F32)
-
-    def by_part(block, count, size):
-        return jnp.transpose(block.reshape(rows_own, count, parts, size), (2, 0, 1, 3)).reshape(parts, rows_own, count * size)
-
-    z_down = line_scatter(by_part(scatter(g_down), 1, units_own))
-    z_up = line_scatter(by_part(scatter(g_up), 1, units_own))
-    z_out = line_scatter(by_part(scatter_late(g_out), 1, inner_own))
-    z_qkv = line_scatter(by_part(scatter_late(g_qkv), 3, inner_own))
-    grad_down = jnp.transpose(z_down)
-    grad_qkv = jnp.transpose(z_qkv.reshape(rows_own, 3, inner_own), (1, 0, 2))
-    grad_out_w = jnp.transpose(z_out)
+    d_image = d_image.astype(BF16)
 
     d_qkv_f = d_qkv.astype(F32)
     sums = (
@@ -308,13 +547,27 @@
         jnp.sum(d_pre.astype(F32), axis=0),
     )
     sizes = [v.shape[0] // parts for v in sums]
-    packed = line_scatter(jnp.concatenate([v.reshape(parts, -1) for v in sums], axis=1))
-    top = jnp.where(use, peaks[:, 0, 0], -1e30)
-    for k in range(1, parts):
-        top = jnp.maximum(top, shift(jnp.where(use, peaks[:, 0, 0], -1e30), k))
-    for bit in range(fsdp.bit_length() - 1):
-        packed = packed + flip(packed, bit)
-        top = jnp.maximum(top, flip(top, bit))
+    vec = jnp.concatenate([v.reshape(parts, -1) for v in sums], axis=1).reshape(-1)
+    count = vec.shape[0]
+    summed = -(-count // 1024) * 8
+    vec = jnp.pad(vec, (0, summed * 128 - count)).reshape(summed, 128)
+    top = jnp.pad(jnp.where(use, peaks[:, 0, 0], -1e30), (0, 1024 - heads)).reshape(8, 128)
+    p_qkv, p_out, shared, vec = tail(
+        (g_qkv, g_out), d_image, jnp.concatenate([vec, top]), summed, owners, CHUNKS)
+    grad_tokens = jnp.stack([jnp.where(me == z, d_image, shared[j]) for j, z in enumerate(owners)]).astype(F32)
+    packed = pick(vec[:summed].reshape(-1)[:count].reshape(parts, -1), me)
+    top = vec[summed]
+
+    def by_part(block, count, size):
+        return jnp.transpose(block.reshape(rows_own, count, parts, size), (2, 0, 1, 3)).reshape(parts, rows_own, count * size)
+
+    z_down, z_up, z_qkv, z_out = line_reduce([
+        by_part(scatter(g_down), 1, units_own), by_part(scatter(g_up), 1, units_own),
+        by_part(p_qkv, 3, inner_own), by_part(p_out, 1, inner_own)])
+    grad_down = jnp.transpose(z_down)
+    grad_qkv = jnp.transpose(z_qkv.reshape(rows_own, 3, inner_own), (1, 0, 2))
+    grad_out_w = jnp.transpose(z_out)
+
     outs = []
     at = 0
     for size in sizes:
@@ -334,7 +587,6 @@
     return lax.psum_scatter(block, "fsdp", scatter_dimension=0, tiled=True)
 
 
-scatter_late = plane_scatter
 CHUNKS = 2
 
 

time: 795 us -> 692 us (0.87)
  Pallas kernels: 46.8 us -> 310 us
  waiting for transfers between devices: 301 us -> 112 us
  starting transfers between devices: 120 us -> 14.9 us
  local copies, waits for them, and re-layouts: 95.8 us -> 51.8 us
  matrix products: 145 us -> 124 us
    pallas_call x0 -> x4, Pallas kernels: none -> 263 us  [the longest x1 156 us: tail(): pl.pallas_call(partial(tail_kernel, plan), in_specs=[any_spec] * (mats +...]
    ppermute x40 -> x3, waiting for transfers between devices: 136 us -> 0.01 us  [line_share(): lax.ppermute(block, 'tensor', [(z, (z + k) % parts) for z in owners])]
    ppermute x40 -> x3, starting transfers between devices: 74.3 us -> 3.86 us  [line_share(): lax.ppermute(block, 'tensor', [(z, (z + k) % parts) for z in owners])]
    ppermute x27 -> x9, waiting for transfers between devices: 126 us -> 78.3 us  [shift(): lax.ppermute(block, 'tensor', [(z, (z + by) % parts) for z in range(parts)])]
    unnamed x112 -> x58, local copies, waits for them, and re-layouts: 45.4 us -> 4.34 us
    ppermute x27 -> x9, starting transfers between devices: 45.7 us -> 10.9 us  [shift(): lax.ppermute(block, 'tensor', [(z, (z + by) % parts) for z in range(parts)])]
    dot_general x12 -> x10, matrix products: 145 us -> 124 us  [dot(): lax.dot_general(a, b, (((ca,), (cb,)), ((), ())), preferred_element_type=...]
    another operation x6 -> x3, other arithmetic: 17.8 us -> 9.25 us  [the longest x2 6.34 us: line_share(): return jnp.stack(outs)]
  transfers between devices with their start and end apart: 72 -> 17, of which waited for: 33 -> 7; matrix products, arithmetic and copies ran while one was open for 29% -> 26% of each run, Pallas kernels for 6% -> 32%
where the time goes in v3:
time: 692 us; the launch traced here: 683 us
  Pallas kernels  310 us (45%)
  matrix products  124 us (18%)
  waiting for transfers between devices  112 us (16%)
  other arithmetic  54.7 us (8%)
  local copies, waits for them, and re-layouts  51.8 us (7%)
  between operations  16 us (2%)
  starting transfers between devices  14.9 us (2%)
    pallas_call x1, Pallas kernels, tail(): pl.pallas_call(partial(tail_kernel, plan), in_specs=[any_spec] * (mats +...  156 us
    dot_general x10, matrix products, dot(): lax.dot_general(a, b, (((ca,), (cb,)), ((), ())), preferred_element_type=...  124 us
    pallas_call x1, Pallas kernels, line_reduce(): pl.pallas_call(partial(line_kernel, parts, mats, rows), in_specs=[vmem] *...  78.5 us
    ppermute x9, waiting for transfers between devices, shift(): lax.ppermute(block, 'tensor', [(z, (z + by) % parts) for z in range(parts)])  78.3 us
    all_gather x1, waiting for transfers between devices, on_device(): lax.all_gather(ffn_line[:, parts * units_own:], 'fsdp', axis=0, tiled=True)  30.3 us
    pallas_call x2, Pallas kernels, wgrad(): pl.pallas_call(wgrad_kernel, grid=(-(-cols // tile),), in_specs=[pl.Block...  28.6 us
    pallas_call x1, Pallas kernels, attn_bwd(): pl.pallas_call(partial(attn_bwd_kernel, HD ** (-0.5)), grid=(heads,), in_...  25.3 us
    pallas_call x1, Pallas kernels, attn_fwd(): pl.pallas_call(partial(attn_fwd_kernel, HD ** (-0.5)), grid=(heads,), in_...  21.7 us
  transfers between devices with their start and end apart: 17, of which 7 were waited for; matrix products, arithmetic and copies ran while one was open for 26% of the time, Pallas kernels for 32%

profile of v3, /device:TPU:10, one launch (start us, length us, event | category | flops | bytes accessed | tf_op | source)
XLA Modules:
  0.0 683.4 jit_solution(4173236137954282259)
XLA Ops:
  15.3 12.0 %collective-permute-done.1 = bf16[144,1152]{1,0:T(8,128)(2,1)S(1)} collective-permute-done((bf16[144,1152]{1,0:T(8,128)(2,1)S(1)}, bf16[144,1152]{1,0:T(8,128)(2,1)S(1)}, u32[]{:S(2)}, u32[]{:S(2)}) %collective-permute-start.1) | collective-permute-done | bytes 331808 | tf_op jit(solution)/shard_map/ppermute | solution.py:121
  27.3 13.3 %collective-permute-done = bf16[144,1152]{1,0:T(8,128)(2,1)S(1)} collective-permute-done((bf16[144,1152]{1,0:T(8,128)(2,1)S(1)}, bf16[144,1152]{1,0:T(8,128)(2,1)S(1)}, u32[]{:S(2)}, u32[]{:S(2)}) %collective-permute-start) | collective-permute-done | bytes 331808 | tf_op jit(solution)/shard_map/ppermute | solution.py:121
  48.2 23.9 %collective-permute-done.7 = bf16[144,2152]{1,0:T(8,128)(2,1)S(1)} collective-permute-done((bf16[144,2152]{1,0:T(8,128)(2,1)S(1)}, bf16[144,2152]{1,0:T(8,128)(2,1)S(1)}, u32[]{:S(2)}, u32[]{:S(2)}) %collective-permute-start.7) | collective-permute-done | bytes 619808 | tf_op jit(solution)/shard_map/ppermute | solution.py:121
  72.0 26.4 %collective-permute-done.6 = bf16[144,2152]{1,0:T(8,128)(2,1)S(1)} collective-permute-done((bf16[144,2152]{1,0:T(8,128)(2,1)S(1)}, bf16[144,2152]{1,0:T(8,128)(2,1)S(1)}, u32[]{:S(2)}, u32[]{:S(2)}) %collective-permute-start.6) | collective-permute-done | bytes 619808 | tf_op jit(solution)/shard_map/ppermute | solution.py:121
  114.7 3.1 convert_reduce_fusion.2
  118.9 13.0 %add_convert_fusion = bf16[3456,729]{0,1:T(8,128)(2,1)} fusion(bf16[1152,4608]{1,0:T(8,128)(2,1)} %all-gather.4.cloned.1.call-done, f32[3456]{0:T(1024)S(1)} %pad_maximum_fusion.8, f32[1152]{0:T(1024)S(1)} %add.182, f32[1152]{0:T(1024)S(1)} %mul.178, f32[729]{0:T(1024)S(1)} %add_rsqrt_fusion.1, f32[729]{0:T(1024)S(1)} %broadcast_multiply_fusion.5, ...), kind=kOutput, calls=%fused_computation.13 | convolution fusion | flops 5814831104 | bytes 14726092 | tf_op jit(solution)/shard_map/dot_general | solution.py:18
  131.9 8.0 %copy.47 = bf16[3456,729]{1,0:T(8,128)(2,1)} copy(bf16[3456,729]{0,1:T(8,128)(2,1)} %add_convert_fusion) | data formatting | bytes 10077696 | tf_op jit(solution)/shard_map/convert_element_type | solution.py:508
  139.9 21.7 %attn_fwd.1 = (bf16[1152,729]{1,0:T(8,128)(2,1)}, bf16[16,729,729]{2,1,0:T(8,128)(2,1)}, f32[16,1,729]{2,1,0:T(1,128)}, f32[16,1,128]{2,1,0:T(1,128)}) custom-call(bf16[3,1152,729]{2,1,0:T(8,128)(2,1)} %bitcast.149), custom_call_target="tpu_custom_call" | custom-call | flops 8707129344 | bytes 17006112 | tf_op jit(solution)/shard_map/attn_fwd/pallas_call | solution.py:36
  161.6 5.5 fusion.74
  172.3 18.5 %multiply_convert_fusion = (bf16[729,4304]{1,0:T(8,128)(2,1)}, f32[729,4304]{1,0:T(8,128)}) fusion(f32[4304]{0:T(1024)S(1)} %add.195, bf16[729,1152]{1,0:T(8,128)(2,1)} %add_convert_fusion.1.x_ref, bf16[1152,4304]{1,0:T(8,128)(2,1)} %all-gather.6.cloned.1.call-done), kind=kOutput, calls=%fused_computation.12 | convolution fusion | flops 7260442624 | bytes 30438944 | tf_op jit(solution)/shard_map/dot_general | solution.py:18
  190.8 14.3 %wgrad.3 = bf16[1152,4304]{1,0:T(8,128)(2,1)} custom-call(bf16[729,1152]{1,0:T(8,128)(2,1)} %get-tuple-element.105.x_ref, bf16[729,4304]{1,0:T(8,128)(2,1)} %get-tuple-element.160.y_ref), custom_call_target="tpu_custom_call" | custom-call | flops 7229067264 | bytes 16191648 | tf_op jit(solution)/shard_map/wgrad/pallas_call | solution.py:152
  205.1 30.3 %all-gather.8.cloned.1.call-done = bf16[1152,4304]{1,0:T(8,128)(2,1)} async-done(((bf16[144,4304]{1,0:T(8,128)(2,1)}), bf16[1152,4304]{1,0:T(8,128)(2,1)}) %all-gather.8.cloned.1.call-update) | async-done | bytes 9916432 | tf_op jit(solution)/shard_map/all_gather | solution.py:483
  235.4 19.3 %convert_reduce_fusion = (f32[4304]{0:T(1024)S(1)}, bf16[729,4304]{1,0:T(8,128)(2,1)}) fusion(f32[729,4304]{1,0:T(8,128)} %get-tuple-element.161, f32[4304]{0:T(1024)S(1)} %add.195, bf16[729,1152]{1,0:T(8,128)(2,1)} %get-tuple-element.105.x_ref, bf16[1152,4304]{1,0:T(8,128)(2,1)} %all-gather.8.cloned.1.call-done), kind=kOutput, calls=%fused_computation.11 | convolution fusion | flops 7298088960 | bytes 30456160 | tf_op jit(solution)/shard_map/dot_general | solution.py:18
  254.7 14.3 %wgrad.2 = bf16[1152,4304]{1,0:T(8,128)(2,1)} custom-call(bf16[729,1152]{1,0:T(8,128)(2,1)} %add_convert_fusion.1.x_ref, bf16[729,4304]{1,0:T(8,128)(2,1)} %get-tuple-element.164.y_ref), custom_call_target="tpu_custom_call" | custom-call | flops 7229067264 | bytes 16191648 | tf_op jit(solution)/shard_map/wgrad/pallas_call | solution.py:152
  269.0 14.8 %fusion.75 = f32[729,1152]{1,0:T(8,128)} fusion(bf16[729,4304]{1,0:T(8,128)(2,1)} %get-tuple-element.164.y_ref, bf16[1152,4304]{1,0:T(8,128)(2,1)} %all-gather.6.cloned.1.call-done), kind=kOutput, calls=%fused_computation.152 | convolution fusion | flops 7229067264 | bytes 19550880 | tf_op jit(solution)/shard_map/dot_general | solution.py:18
  284.7 14.5 %fusion.38 = bf16[729,1152]{1,0:T(8,128)(2,1)} fusion(f32[729,1152]{1,0:T(8,128)S(1)} %get-tuple-element.159, bf16[729,4304]{1,0:T(8,128)(2,1)} %get-tuple-element.160.y_ref, bf16[1152,4304]{1,0:T(8,128)(2,1)} %all-gather.8.cloned.1.call-done, f32[]{:T(128)} %bitcast.21, f32[1152]{0:T(1024)S(1)} %add.201), kind=kOutput, calls=%fused_computation.59 | convolution fusion | flops 7232425984 | bytes 21235108 | tf_op jit(solution)/shard_map/dot_general | solution.py:18
  303.2 3.4 multiply_reduce_fusion
  306.7 4.3 convert_reduce_fusion.3
  311.2 5.4 convolution_convert_fusion.2
  318.9 25.3 %attn_bwd.1 = bf16[3,1152,729]{2,1,0:T(8,128)(2,1)} custom-call(bf16[3,1152,729]{2,1,0:T(8,128)(2,1)} %bitcast.150, bf16[1152,729]{1,0:T(8,128)(2,1)} %copy.48.do_ref, bf16[1152,729]{1,0:T(8,128)(2,1)} %get-tuple-element.33.o_ref, bf16[16,729,729]{2,1,0:T(8,128)(2,1)} %get-tuple-element.35.p_ref, f32[16,1,729]{2,1,0:T(1,128)} %get-tuple-element.36.l_ref), custom_call_target="tpu_custom_call" | custom-call | flops 17414258688 | bytes 17006112 | tf_op jit(solution)/shard_map/attn_bwd/pallas_call | solution.py:75
  344.2 7.6 %convert_element_type.129 = f32[3456,729]{1,0:T(8,128)} convert(bf16[3456,729]{1,0:T(8,128)(2,1)} %bitcast.151) | non-fusion elementwise | flops 2519424 | bytes 15116544 | tf_op jit(solution)/shard_map/convert_element_type | solution.py:537
  351.8 14.4 %fusion.32 = (f32[1152]{0:T(1024)S(1)}, f32[729]{0:T(1024)}, f32[729]{0:T(1024)}, f32[1152]{0:T(1024)S(1)}, f32[729,1152]{1,0:T(8,128)}) fusion(f32[729]{0:T(1024)S(1)} %copy-done.13, f32[729]{0:T(1024)S(1)} %copy-done.9, bf16[3,729,1152]{2,1,0:T(8,128)(2,1)} %param.16, s32[]{:T(128)S(6)} %select_n.130, f32[1152]{0:T(1024)S(1)} %copy-done.11, ...), kind=kOutput, calls=%fused_computation.47 | convolution fusion | flops 5813146624 | bytes 18081940 | tf_op jit(solution)/shard_map/dot_general | solution.py:18
  367.0 3.6 slice_reduce_fusion
  375.2 6.2 convolution_convert_fusion.1
  381.4 3.8 fusion.31.refs_2_
  385.2 12.2 %convolution_convert_fusion = bf16[1152,3456]{1,0:T(8,128)(2,1)} fusion(bf16[3456,729]{1,0:T(8,128)(2,1)} %bitcast.152, f32[1152]{0:T(1024)S(1)} %copy-done.15, f32[1152]{0:T(1024)S(1)} %copy-done.11, f32[729]{0:T(1024)S(1)} %copy-done.13, f32[729]{0:T(1024)S(1)} %copy-done.9, bf16[3,729,1152]{2,1,0:T(8,128)(2,1)} %param.16, s32[]{:T(128)S(6)} %select_n.130), kind=kOutput, calls=%fused_computation.2 | convolution fusion | flops 5813773312 | bytes 14981836 | tf_op jit(solution)/shard_map/dot_general | solution.py:18
  397.4 156.4 %tail.1 = (bf16[144,3456]{1,0:T(8,128)(2,1)}, bf16[144,1152]{1,0:T(8,128)(2,1)}, bf16[3,729,1152]{2,1,0:T(8,128)(2,1)}, f32[120,128]{1,0:T(8,128)}) custom-call(bf16[8,144,3456]{2,1,0:T(8,128)(2,1)} %bitcast.147, bf16[8,144,1152]{2,1,0:T(8,128)(2,1)} %bitcast.157, bf16[729,1152]{1,0:T(8,128)(2,1)} %fusion.31.refs_2_, f32[120,128]{1,0:T(8,128)} %pad_maximum_fusion.5.refs_3_), custom_call_target="tpu_custom_call" | custom-call | bytes 250000000 | tf_op jit(solution)/shard_map/tail/pallas_call | solution.py:360
  572.2 4.8 maximum_convert_fusion
  577.0 3.4 select_bitcast_fusion.3
  583.3 3.2 reshape.246
  587.7 3.2 reshape.244
  592.2 78.5 %line_reduce.1 = (f32[144,1076]{1,0:T(8,128)}, f32[144,1076]{1,0:T(8,128)}, f32[144,864]{1,0:T(8,128)}, f32[144,288]{1,0:T(8,128)}) custom-call(bf16[4,144,1076]{2,1,0:T(8,128)(2,1)} %bitcast.155, bf16[4,144,1076]{2,1,0:T(8,128)(2,1)} %bitcast.154, bf16[4,144,864]{2,1,0:T(8,128)(2,1)} %reshape.249.refs_2_, bf16[4,144,288]{2,1,0:T(8,128)(2,1)} %bitcast.158), custom_call_target="tpu_custom_call" | custom-call | bytes 200000000 | tf_op jit(solution)/shard_map/line_reduce/pallas_call | solution.py:438
  (179 shorter events, 78.9 us)
Async XLA Ops:
  7.2 111.7 %all-gather.4.cloned.1.call-start = ((), (), s32[]{:S(2)}) async-start(), calls=%async_computation.2 | async-start | bytes 11943936 | tf_op jit(solution)/shard_map/all_gather | solution.py:476
  9.7 17.7 %collective-permute-start.1 = (bf16[144,1152]{1,0:T(8,128)(2,1)S(1)}, bf16[144,1152]{1,0:T(8,128)(2,1)S(1)}, u32[]{:S(2)}, u32[]{:S(2)}) collective-permute-start(bf16[144,1152]{1,0:T(8,128)(2,1)S(1)} %pad_maximum_fusion.4), channel_id=1, source_target_pairs={{0,2},{1,3},{2,0},{3,1},{4,6},{5,7},{6,4},{7,5},{8,10},{9,11},{10,... | collective-permute-start | bytes 995336 | tf_op jit(solution)/shard_map/ppermute | solution.py:121
  12.3 28.3 %collective-permute-start = (bf16[144,1152]{1,0:T(8,128)(2,1)S(1)}, bf16[144,1152]{1,0:T(8,128)(2,1)S(1)}, u32[]{:S(2)}, u32[]{:S(2)}) collective-permute-start(bf16[144,1152]{1,0:T(8,128)(2,1)S(1)} %pad_maximum_fusion.4), channel_id=1, source_target_pairs={{0,1},{1,2},{2,3},{3,0},{4,5},{5,6},{6,7},{7,4},{8,9},{9,10},{10,1... | collective-permute-start | bytes 995336 | tf_op jit(solution)/shard_map/ppermute | solution.py:121
  12.3 28.3 %collective-permute-start.2 = (bf16[144,1152]{1,0:T(8,128)(2,1)S(1)}, bf16[144,1152]{1,0:T(8,128)(2,1)S(1)}, u32[]{:S(2)}, u32[]{:S(2)}) collective-permute-start(bf16[144,1152]{1,0:T(8,128)(2,1)S(1)} %pad_maximum_fusion.4), channel_id=1, source_target_pairs={{0,3},{1,0},{2,1},{3,2},{4,7},{5,4},{6,5},{7,6},{8,11},{9,8},{10,9... | collective-permute-start | bytes 995336 | tf_op jit(solution)/shard_map/ppermute | solution.py:121
  43.8 128.5 %all-gather.6.cloned.1.call-start = ((), (), s32[]{:S(2)}) async-start(), calls=%async_computation.3 | async-start | bytes 11280384 | tf_op jit(solution)/shard_map/all_gather | solution.py:482
  44.0 28.0 %collective-permute-start.7 = (bf16[144,2152]{1,0:T(8,128)(2,1)S(1)}, bf16[144,2152]{1,0:T(8,128)(2,1)S(1)}, u32[]{:S(2)}, u32[]{:S(2)}) collective-permute-start(bf16[144,2152]{1,0:T(8,128)(2,1)S(1)} %pad_maximum_fusion.3), channel_id=1, source_target_pairs={{0,2},{1,3},{2,0},{3,1},{4,6},{5,7},{6,4},{7,5},{8,10},{9,11},{10,... | collective-permute-start | bytes 1859336 | tf_op jit(solution)/shard_map/ppermute | solution.py:121
  44.1 54.3 %collective-permute-start.6 = (bf16[144,2152]{1,0:T(8,128)(2,1)S(1)}, bf16[144,2152]{1,0:T(8,128)(2,1)S(1)}, u32[]{:S(2)}, u32[]{:S(2)}) collective-permute-start(bf16[144,2152]{1,0:T(8,128)(2,1)S(1)} %pad_maximum_fusion.3), channel_id=1, source_target_pairs={{0,1},{1,2},{2,3},{3,0},{4,5},{5,6},{6,7},{7,4},{8,9},{9,10},{10,1... | collective-permute-start | bytes 1859336 | tf_op jit(solution)/shard_map/ppermute | solution.py:121
  46.6 54.6 %collective-permute-start.8 = (bf16[144,2152]{1,0:T(8,128)(2,1)S(1)}, bf16[144,2152]{1,0:T(8,128)(2,1)S(1)}, u32[]{:S(2)}, u32[]{:S(2)}) collective-permute-start(bf16[144,2152]{1,0:T(8,128)(2,1)S(1)} %pad_maximum_fusion.3), channel_id=1, source_target_pairs={{0,3},{1,0},{2,1},{3,2},{4,7},{5,4},{6,5},{7,6},{8,11},{9,8},{10,9... | collective-permute-start | bytes 1859336 | tf_op jit(solution)/shard_map/ppermute | solution.py:121
  102.7 4.5 copy-start.16
  102.8 6.8 copy-start.26
  105.0 130.4 %all-gather.8.cloned.1.call-start = ((), (), s32[]{:S(2)}) async-start(), calls=%async_computation.4 | async-start | bytes 11280384 | tf_op jit(solution)/shard_map/all_gather | solution.py:483
  107.2 476.1 %reduce-scatter.5.cloned.1.call-start = ((), (), s32[]{:S(2)}) async-start(), calls=%async_computation.6 | async-start | bytes 11280384 | tf_op jit(solution)/shard_map/reduce_scatter | solution.py:587
  107.4 10.4 %collective-permute-start.5 = (f32[3380]{0:T(1024)S(1)}, f32[3380]{0:T(1024)S(1)}, u32[]{:S(2)}, u32[]{:S(2)}) collective-permute-start(f32[3380]{0:T(1024)S(1)} %concatenate.30), channel_id=1, source_target_pairs={{0,3},{1,0},{2,1},{3,2},{4,7},{5,4},{6,5},{7,6},{8,11},{9,8},{10,9... | collective-permute-start | bytes 40568 | tf_op jit(solution)/shard_map/ppermute | solution.py:121
  107.4 10.4 %collective-permute-start.4 = (f32[3380]{0:T(1024)S(1)}, f32[3380]{0:T(1024)S(1)}, u32[]{:S(2)}, u32[]{:S(2)}) collective-permute-start(f32[3380]{0:T(1024)S(1)} %concatenate.30), channel_id=1, source_target_pairs={{0,2},{1,3},{2,0},{3,1},{4,6},{5,7},{6,4},{7,5},{8,10},{9,11},{10,... | collective-permute-start | bytes 40568 | tf_op jit(solution)/shard_map/ppermute | solution.py:121
  108.6 9.3 %collective-permute-start.3 = (f32[3380]{0:T(1024)S(1)}, f32[3380]{0:T(1024)S(1)}, u32[]{:S(2)}, u32[]{:S(2)}) collective-permute-start(f32[3380]{0:T(1024)S(1)} %concatenate.30), channel_id=1, source_target_pairs={{0,1},{1,2},{2,3},{3,0},{4,5},{5,6},{6,7},{7,4},{8,9},{9,10},{10,1... | collective-permute-start | bytes 40568 | tf_op jit(solution)/shard_map/ppermute | solution.py:121
  112.6 19.3 %copy-start.8 = (f32[729]{0:T(1024)}, f32[729]{0:T(1024)S(1)}, u32[]{:S(2)}) copy-start(f32[729]{0:T(1024)S(1)} %broadcast_multiply_fusion.5) | copy-start | bytes 8752
  114.7 17.2 %copy-start.12 = (f32[729]{0:T(1024)}, f32[729]{0:T(1024)S(1)}, u32[]{:S(2)}) copy-start(f32[729]{0:T(1024)S(1)} %add_rsqrt_fusion.1) | copy-start | bytes 8752
  118.3 13.6 %copy-start.10 = (f32[1152]{0:T(1024)}, f32[1152]{0:T(1024)S(1)}, u32[]{:S(2)}) copy-start(f32[1152]{0:T(1024)S(1)} %mul.178) | copy-start | bytes 13828
  118.5 13.4 %copy-start.14 = (f32[1152]{0:T(1024)}, f32[1152]{0:T(1024)S(1)}, u32[]{:S(2)}) copy-start(f32[1152]{0:T(1024)S(1)} %add.182) | copy-start | bytes 13828
  283.9 303.9 %reduce-scatter.3.cloned.1.call-start = ((), (), s32[]{:S(2)}) async-start(), calls=%async_computation.5 | async-start | bytes 11280384 | tf_op jit(solution)/shard_map/reduce_scatter | solution.py:587
  299.3 277.7 %collective-permute-start.11 = (bf16[729,1152]{1,0:T(8,128)(2,1)}, bf16[729,1152]{1,0:T(8,128)(2,1)}, u32[]{:S(2)}, u32[]{:S(2)}) collective-permute-start(bf16[729,1152]{1,0:T(8,128)(2,1)} %fusion.38), channel_id=1, source_target_pairs={{0,1},{2,3},{3,0},{4,5},{6,7},{7,4},{8,9},{10,11},{11,8},{12,13},{... | collective-permute-start | bytes 5038856 | tf_op jit(solution)/shard_map/ppermute | solution.py:135
  300.5 276.4 %collective-permute-start.10 = (bf16[729,1152]{1,0:T(8,128)(2,1)}, bf16[729,1152]{1,0:T(8,128)(2,1)}, u32[]{:S(2)}, u32[]{:S(2)}) collective-permute-start(bf16[729,1152]{1,0:T(8,128)(2,1)} %fusion.38), channel_id=1, source_target_pairs={{0,2},{2,0},{3,1},{4,6},{6,4},{7,5},{8,10},{10,8},{11,9},{12,14},{... | collective-permute-start | bytes 5038856 | tf_op jit(solution)/shard_map/ppermute | solution.py:135
  301.8 275.1 %collective-permute-start.9 = (bf16[729,1152]{1,0:T(8,128)(2,1)}, bf16[729,1152]{1,0:T(8,128)(2,1)}, u32[]{:S(2)}, u32[]{:S(2)}) collective-permute-start(bf16[729,1152]{1,0:T(8,128)(2,1)} %fusion.38), channel_id=1, source_target_pairs={{0,3},{2,1},{3,2},{4,7},{6,5},{7,6},{8,11},{10,9},{11,10},{12,15},... | collective-permute-start | bytes 5038856 | tf_op jit(solution)/shard_map/ppermute | solution.py:135
  344.2 7.6 %copy-start.2 = (bf16[3,1152,729]{2,1,0:T(8,128)(2,1)S(1)}, bf16[3,1152,729]{2,1,0:T(8,128)(2,1)}, u32[]{:S(2)}) copy-start(bf16[3,1152,729]{2,1,0:T(8,128)(2,1)} %attn_bwd.1) | copy-start | bytes 15116548
  344.2 7.6 %copy-start.9 = (f32[729]{0:T(1024)S(1)}, f32[729]{0:T(1024)}, u32[]{:S(2)}) copy-start(f32[729]{0:T(1024)} %copy-done.8) | copy-start | bytes 8752
  344.2 7.6 %copy-start.11 = (f32[1152]{0:T(1024)S(1)}, f32[1152]{0:T(1024)}, u32[]{:S(2)}) copy-start(f32[1152]{0:T(1024)} %copy-done.10) | copy-start | bytes 13828
  344.2 7.6 %copy-start.13 = (f32[729]{0:T(1024)S(1)}, f32[729]{0:T(1024)}, u32[]{:S(2)}) copy-start(f32[729]{0:T(1024)} %copy-done.12) | copy-start | bytes 8752
  367.0 8.2 %copy-start.1 = (f32[729,1152]{1,0:T(8,128)S(1)}, f32[729,1152]{1,0:T(8,128)}, u32[]{:S(2)}) copy-start(f32[729,1152]{1,0:T(8,128)} %get-tuple-element.107) | copy-start | bytes 10077700
  375.2 6.2 copy-start.3
  561.1 7.5 %copy-start.18 = (bf16[288]{0:T(512)(128)(2,1)S(1)}, bf16[288]{0:T(512)(128)(2,1)}, u32[]{:S(2)}) copy-start(bf16[288]{0:T(512)(128)(2,1)} %param.21) | copy-start | bytes 1732
  561.1 8.1 %copy-start = (bf16[729,1152]{1,0:T(8,128)(2,1)S(1)}, bf16[729,1152]{1,0:T(8,128)(2,1)}, u32[]{:S(2)}) copy-start(bf16[729,1152]{1,0:T(8,128)(2,1)} %fusion.31.refs_2_) | copy-start | bytes 5038852
  670.7 5.1 copy-start.6
  (12 other events, 49.2 us)
Sparse Core Ops, SparseCore 0:
  43.9 64.6 all-gather.3
  111.1 61.1 all-gather.5
  174.2 61.1 all-gather.7
  284.0 79.6 reduce-scatter.4
  367.1 99.5 reduce-scatter.2

commit v4 on v3

--- a/solution.py
+++ b/solution.py
@@ -116,30 +116,21 @@
     return lax.dynamic_index_in_dim(block, index, axis, keepdims=False)
 
 
-def shift(block, by):
+def first_hop(block, owners):
     parts = lax.axis_size("tensor")
-    return lax.ppermute(block, "tensor", [(z, (z + by) % parts) for z in range(parts)])
-
-
-def line_gather(block):
+    up = [(z, z + 1) for z in owners if z + 1 < parts]
+    down = [(z, z - 1) for z in owners if z > 0]
+    return lax.ppermute(block, "tensor", up), lax.ppermute(block, "tensor", down)
+
+
+def far_hop(near, distance, owners):
     parts = lax.axis_size("tensor")
-    me = lax.axis_index("tensor")
-    near = jnp.stack([block] + [shift(block, k) for k in range(1, parts)])
-    return [pick(near, lax.rem(me - z + parts, parts)) for z in range(parts)]
-
-
-def line_share(block, owners):
-    parts = lax.axis_size("tensor")
-    me = lax.axis_index("tensor")
-    far = [block] + [
-        lax.ppermute(block, "tensor", [(z, (z + k) % parts) for z in owners]) for k in range(1, parts)]
-    outs = []
-    for z in owners:
-        out = block
-        for k in range(1, parts):
-            out = jnp.where(me == (z + k) % parts, far[k], out)
-        outs.append(out)
-    return jnp.stack(outs)
+    up = [(z + 1, z + distance) for z in owners if z + distance < parts]
+    down = [(z - 1, z - distance) for z in owners if z - distance >= 0]
+    return (
+        lax.ppermute(near[0], "tensor", up) if up else None,
+        lax.ppermute(near[1], "tensor", down) if down else None,
+    )
 
 
 def wgrad_kernel(x_ref, y_ref, out_ref):
@@ -195,13 +186,6 @@
     place = lax.axis_index("fsdp")
     me = lax.axis_index("tensor")
 
-    def moved(index, mask):
-        out = index
-        for b in range(8):
-            if mask >> b & 1:
-                out = out + (1 - 2 * ((index // 2**b) % 2)) * 2**b
-        return out
-
     barrier = pltpu.get_barrier_semaphore()
     for b in range(bits):
         pl.semaphore_signal(barrier, inc=1, device_id={"fsdp": moved(place, 1 << b)}, device_id_type=pl.DeviceIdType.MESH)
@@ -231,10 +215,10 @@
         hop(j, c, side, m).start()
         sent[m].append((j, c, side))
 
-    def arrive(m, first):
-        order = sorted((abs(owners[j] - m) * chunks + c, j, c) for j in range(slots) for c in range(chunks) if owners[j] != m)
-        for key, j, c in order:
-            if (key < 2 * chunks) != first:
+    def arrive(m, reach):
+        order = sorted((abs(owners[j] - m), c, j) for j in range(slots) for c in range(chunks) if owners[j] != m)
+        for distance, c, j in order:
+            if distance not in reach:
                 continue
             side = 1 if m > owners[j] else 0
             hop(j, c, 0 if m > 0 else 1, m).wait_recv()
@@ -290,6 +274,12 @@
                     copy.start()
                     flying.append(copy)
                     landing.append((copy, own[i].at[r, pl.ds(lo, hi - lo)], halves[i][h][s].at[k], hi - lo))
+        for m in range(parts):
+
+            @pl.when(me == m)
+            def _():
+                arrive(m, (s + 1,))
+
         if s == 0:
             walk[0] = vec[...]
             partners = [("fsdp", place, b) for b in range(bits)] + [("tensor", me, b) for b in range(part_bits)]
@@ -303,13 +293,6 @@
                 walk[k + 1, :summed] = walk[k, :summed] + meet[k, :summed]
                 walk[k + 1, summed:] = jnp.maximum(walk[k, summed:], meet[k, summed:])
             total[...] = walk[len(partners)]
-        if s == 0:
-            for m in range(parts):
-
-                @pl.when(me == m)
-                def _():
-                    arrive(m, True)
-
         for copy, dst, src, count in landing:
             copy.wait_recv()
             add_rows(dst, src, count)
@@ -319,7 +302,7 @@
 
         @pl.when(me == m)
         def _():
-            arrive(m, False)
+            arrive(m, range(bits, parts))
             for j, c, side in sent[m]:
                 hop(j, c, side, m).wait_send()
 
@@ -370,6 +353,162 @@
     )(*grads, image, vec)
 
 
+def moved(index, mask):
+    out = index
+    for b in range(8):
+        if mask >> b & 1:
+            out = out + (1 - 2 * ((index // 2**b) % 2)) * 2**b
+    return out
+
+
+def front_kernel(plan, *refs):
+    parts, fsdp, rows, cut, thirds = plan
+    bits = fsdp.bit_length() - 1
+    chips = fsdp // 2
+    own, (small, down), full, near, lines = refs[:4], refs[4:6], refs[6:8], refs[8:10], refs[10:12]
+    hop_send, hop_recv, plane_send, plane_recv, core_recv, own_sem = refs[12:]
+    line = (small, near[0], near[1], down)
+    place = lax.axis_index("fsdp")
+    me = lax.axis_index("tensor")
+    barrier = pltpu.get_barrier_semaphore()
+    mesh_id = pl.DeviceIdType.MESH
+    for b in range(bits):
+        pl.semaphore_signal(barrier, inc=1, device_id={"fsdp": moved(place, 1 << b)}, device_id_type=mesh_id)
+    for m in range(parts):
+        beside = [z for z in (m - 1, m + 1) if 0 <= z < parts]
+
+        @pl.when(me == m)
+        def _():
+            for z in beside:
+                pl.semaphore_signal(barrier, inc=1, device_id={"tensor": me + (z - m)}, device_id_type=mesh_id)
+            pl.semaphore_wait(barrier, bits + len(beside))
+
+    def hop(i, z, side, m):
+        return pltpu.make_async_remote_copy(
+            src_ref=own[i] if z == m else line[i].at[z], dst_ref=line[i].at[z], send_sem=hop_send.at[i, z, side],
+            recv_sem=hop_recv.at[i, z], device_id={"tensor": me + (2 * side - 1)}, device_id_type=mesh_id)
+
+    def along(i):
+        line[i][me] = own[i][...]
+        for m in range(parts):
+
+            @pl.when(me == m)
+            def _():
+                sides = [side for side in (0, 1) if 0 <= m + 2 * side - 1 < parts]
+                for side in sides:
+                    hop(i, m, side, m).start()
+                for z in sorted((z for z in range(parts) if z != m), key=lambda z: (abs(z - m), z)):
+                    side = 1 if m > z else 0
+                    hop(i, z, sides[0], m).wait_recv()
+                    if side in sides:
+                        hop(i, z, side, m).start()
+
+    halves = ((0, cut), (cut, rows))
+    orders = (list(range(bits - 1)), list(range(bits - 2, -1, -1)))
+    flying = []
+
+    def step_of(h, r):
+        return max([-1] + [s for s, b in enumerate(orders[h]) if r >> b & 1])
+
+    def pass_on(i, h, r):
+        lo, hi = halves[h]
+        at = pl.ds(lo, hi - lo)
+        block = moved(place, 2 * r)
+        src = lines[i].at[at] if r == 0 else full[i].at[block, at]
+        for s in range(step_of(h, r) + 1, bits - 1):
+            b = orders[h][s]
+            flying.append(pltpu.make_async_remote_copy(
+                src_ref=src, dst_ref=full[i].at[block, at], send_sem=plane_send.at[i, h, r, s],
+                recv_sem=plane_recv.at[i, h, r ^ (1 << b)], device_id={"fsdp": moved(place, 2 << b)},
+                device_id_type=mesh_id))
+            flying[-1].start()
+        flying.append(pltpu.make_async_remote_copy(
+            src_ref=src, dst_ref=full[i].at[block, at], send_sem=plane_send.at[i, h, r, bits - 1],
+            recv_sem=core_recv.at[i, h, r], device_id={"fsdp": moved(place, 1)}, device_id_type=mesh_id))
+        flying[-1].start()
+
+    def landed(i, h, r, sem, other):
+        lo, hi = halves[h]
+        at = pl.ds(lo, hi - lo)
+        block = full[i].at[moved(place, 2 * r + other), at]
+        pltpu.make_async_remote_copy(
+            src_ref=block, dst_ref=block, send_sem=plane_send.at[i, h, r, 0], recv_sem=sem.at[i, h, r],
+            device_id={"fsdp": moved(place, 1)}, device_id_type=mesh_id).wait_recv()
+
+    def begin(i):
+        keep = pltpu.make_async_copy(lines[i], full[i].at[place], own_sem.at[i])
+        keep.start()
+        for h in range(2):
+            pass_on(i, h, 0)
+        return keep
+
+    def go_on(i, last):
+        for s in range(bits - 1):
+            for h in range(2):
+                for r in range(1, chips):
+                    if step_of(h, r) == s and (s == bits - 2) == last:
+                        landed(i, h, r, plane_recv, 0)
+                        pass_on(i, h, r)
+
+    along(0)
+    along(1)
+    for c in range(4):
+        for z in range(parts):
+            lines[0][:, (c * parts + z) * thirds : (c * parts + z + 1) * thirds] = near[0][z, :, c * thirds : (c + 1) * thirds]
+    keeps = [begin(0)]
+    along(2)
+    go_on(0, False)
+    units = near[1].shape[2]
+    for z in range(parts):
+        lines[1][:, z * units : (z + 1) * units] = near[1][z]
+    keeps.append(begin(1))
+    along(3)
+    go_on(0, True)
+    go_on(1, False)
+    go_on(1, True)
+    for i in range(2):
+        keeps[i].wait()
+        for h in range(2):
+            for r in range(chips):
+                landed(i, h, r, core_recv, 1)
+    for copy in flying:
+        copy.wait_send()
+    for m in range(parts):
+
+        @pl.when(me == m)
+        def _():
+            for i in range(4):
+                for z in range(parts):
+                    for side in (0, 1):
+                        if 0 <= m + 2 * side - 1 < parts and (z == m or (side == 1) == (m > z)):
+                            hop(i, z, side, m).wait_send()
+
+
+def front(small, attn, up, down):
+    parts = lax.axis_size("tensor")
+    fsdp = lax.axis_size("fsdp")
+    bits = fsdp.bit_length() - 1
+    rows = up.shape[0]
+    cut = -(-(rows // 2) // 16) * 16
+    vmem = pl.BlockSpec(memory_space=pltpu.VMEM)
+    dma = pltpu.SemaphoreType.DMA
+    wide = [parts * attn.shape[1], parts * up.shape[1]]
+    return pl.pallas_call(
+        partial(front_kernel, (parts, fsdp, rows, cut, attn.shape[1] // 4)),
+        in_specs=[vmem] * 4,
+        out_specs=[vmem] * 2 + [pl.BlockSpec(memory_space=pl.ANY)] * 2,
+        out_shape=[jax.ShapeDtypeStruct((parts,) + small.shape, F32), jax.ShapeDtypeStruct((parts,) + down.shape, BF16)]
+        + [jax.ShapeDtypeStruct((fsdp, rows, c), BF16) for c in wide],
+        scratch_shapes=[pltpu.VMEM((parts,) + attn.shape, BF16), pltpu.VMEM((parts,) + up.shape, BF16)]
+        + [pltpu.VMEM((rows, c), BF16) for c in wide]
+        + [dma((4, parts, 2)), dma((4, parts)), dma((2, 2, fsdp // 2, bits)), dma((2, 2, fsdp // 2)),
+           dma((2, 2, fsdp // 2)), dma((2,))],
+        compiler_params=pltpu.CompilerParams(collective_id=2, has_side_effects=True),
+        cost_estimate=pl.CostEstimate(flops=0, bytes_accessed=250_000_000, transcendentals=0),
+        name="front",
+    )(small, attn, up, down)
+
+
 def line_kernel(parts, mats, rows, *refs):
     own, outs, up, down = (refs[i * mats : (i + 1) * mats] for i in range(4))
     send_sem, recv_sem = refs[4 * mats :]
@@ -469,25 +608,21 @@
 
     qkv_own = jnp.transpose(w_qkv, (1, 0, 2)).reshape(rows_own, 3 * inner_own)
     attn_own = jnp.concatenate([qkv_own, jnp.transpose(w_out)], axis=1)
-    line = line_gather(attn_own)
-    attn_line = jnp.concatenate(
-        [line[z][:, c * inner_own : (c + 1) * inner_own] for c in range(4) for z in range(parts)], axis=1
-    )
-    attn_full = lax.all_gather(attn_line, "fsdp", axis=0, tiled=True)
-    ffn_own = jnp.concatenate([w_up, jnp.transpose(w_down)], axis=1)
-    line = line_gather(ffn_own)
-    ffn_line = jnp.concatenate(
-        [line[z][:, c * units_own : (c + 1) * units_own] for c in range(2) for z in range(parts)], axis=1
-    )
-    up_full = lax.all_gather(ffn_line[:, : parts * units_own], "fsdp", axis=0, tiled=True)
-    down_full = lax.all_gather(ffn_line[:, parts * units_own :], "fsdp", axis=0, tiled=True)
-    qkv_full = attn_full[:, : 3 * inner]
-    out_full = attn_full[:, 3 * inner :]
-
     small = jnp.concatenate(
         [v.astype(F32) for v in (ln1_gain, ln1_bias, b_query, b_value, b_out, ln2_gain, ln2_bias, b_down, b_up)]
     )
-    small = jnp.stack(line_gather(small))
+    count = small.shape[0]
+    tall = -(-count // 1024) * 8
+    small = jnp.pad(small, (0, tall * 128 - count)).reshape(tall, 128)
+    small, down_line, attn_full, up_full = front(small, attn_own, w_up, jnp.transpose(w_down))
+    small = small.reshape(parts, -1)
+    attn_full = attn_full.reshape(width, -1)
+    up_full = up_full.reshape(width, -1)
+    down_line = jnp.concatenate([down_line[z] for z in range(parts)], axis=1)
+    down_full = lax.all_gather(down_line, "fsdp", axis=0, tiled=True)
+    qkv_full = attn_full[:, : 3 * inner]
+    out_full = attn_full[:, 3 * inner :]
+
     own = width // parts
     pieces = []
     at = 0
@@ -515,10 +650,12 @@
     slope = 0.5 * (1.0 + inner_tanh) + 0.5 * pre * (1.0 - inner_tanh * inner_tanh) * (
         0.7978845608028654 * (1.0 + 3 * 0.044715 * pre * pre)
     )
+    g_down = wgrad(error, act)
+    s_down = scatter(g_down)
     layer = ((resid + dot(act, down_full, 1, 1) + bias_down) * keep).astype(BF16)
-    layer_out = line_share(layer, owners)
-
-    g_down = wgrad(error, act)
+    layer, error = lax.optimization_barrier((layer, error))
+    near = first_hop(layer, owners)
+
     d_pre = (dot(error, down_full, 1, 0) * slope).astype(BF16)
     g_up = wgrad(a_two, d_pre)
     d_two = dot(d_pre, up_full, 1, 1)
@@ -529,6 +666,8 @@
     g_out = dot(d_attn, heads_t, 0, 1).astype(BF16)
     d_heads = dot(out_full, d_attn, 0, 1).astype(BF16)
     d_qkv = attn_bwd(qkv, d_heads, heads_t, probs, totals, heads).reshape(3 * inner, length)
+    d_qkv, near, s_down = lax.optimization_barrier((d_qkv, near, s_down))
+    hops = [None, near] + [far_hop(near, d, owners) for d in range(2, parts)]
     g_qkv = dot(a_one, d_qkv, 0, 1).astype(BF16)
     d_one = dot(d_qkv, qkv_full, 0, 1)
     d_image = d_resid + norm_back(d_one, normed_one, inverse_one, gain_one)
@@ -552,18 +691,27 @@
     summed = -(-count // 1024) * 8
     vec = jnp.pad(vec, (0, summed * 128 - count)).reshape(summed, 128)
     top = jnp.pad(jnp.where(use, peaks[:, 0, 0], -1e30), (0, 1024 - heads)).reshape(8, 128)
+    def by_part(block, count, size):
+        return jnp.transpose(block.reshape(rows_own, count, parts, size), (2, 0, 1, 3)).reshape(parts, rows_own, count * size)
+
     p_qkv, p_out, shared, vec = tail(
         (g_qkv, g_out), d_image, jnp.concatenate([vec, top]), summed, owners, CHUNKS)
     grad_tokens = jnp.stack([jnp.where(me == z, d_image, shared[j]) for j, z in enumerate(owners)]).astype(F32)
     packed = pick(vec[:summed].reshape(-1)[:count].reshape(parts, -1), me)
     top = vec[summed]
 
-    def by_part(block, count, size):
-        return jnp.transpose(block.reshape(rows_own, count, parts, size), (2, 0, 1, 3)).reshape(parts, rows_own, count * size)
-
     z_down, z_up, z_qkv, z_out = line_reduce([
-        by_part(scatter(g_down), 1, units_own), by_part(scatter(g_up), 1, units_own),
+        by_part(s_down, 1, units_own), by_part(scatter(g_up), 1, units_own),
         by_part(p_qkv, 3, inner_own), by_part(p_out, 1, inner_own)])
+    z_out, hops = lax.optimization_barrier((z_out, hops))
+    spread = []
+    for z in owners:
+        out = layer
+        for other in range(parts):
+            if other != z:
+                out = jnp.where(me == other, hops[abs(other - z)][0 if other > z else 1], out)
+        spread.append(out)
+    layer_out = jnp.stack(spread)
     grad_down = jnp.transpose(z_down)
     grad_qkv = jnp.transpose(z_qkv.reshape(rows_own, 3, inner_own), (1, 0, 2))
     grad_out_w = jnp.transpose(z_out)
@@ -587,7 +735,7 @@
     return lax.psum_scatter(block, "fsdp", scatter_dimension=0, tiled=True)
 
 
-CHUNKS = 2
+CHUNKS = 3
 
 
 def solution(mesh):

time: 692 us -> 653 us (0.944)
  waiting for transfers between devices: 112 us -> 3.85 us
  Pallas kernels: 310 us -> 390 us
    pallas_call x0 -> x1, Pallas kernels: none -> 113 us  [front(): pl.pallas_call(partial(front_kernel, (parts, fsdp, rows, cut, attn.shape[...]
    ppermute x12 -> x6, waiting for transfers between devices: 78.3 us -> 3.8 us  [the longest x1 2.59 us: first_hop(): lax.ppermute(block, 'tensor', up)]
    pallas_call x1, Pallas kernels: 156 us -> 116 us  [tail(): pl.pallas_call(partial(tail_kernel, plan), in_specs=[any_spec] * (mats +...]
    all_gather x3 -> x1, waiting for transfers between devices: 33.2 us -> 0.01 us  [on_device(): down_full = lax.all_gather(down_line, 'fsdp', axis=0, tiled=True)]
    ppermute x12 -> x6, starting transfers between devices: 14.7 us -> 21.2 us  [the longest x2 14.6 us: far_hop(): lax.ppermute(near[0], 'tensor', up)]
  transfers between devices with their start and end apart: 17 -> 9, of which waited for: 7 -> 2; matrix products, arithmetic and copies ran while one was open for 26% -> 29% of each run, Pallas kernels for 32% -> 43%
where the time goes in v4:
time: 653 us; the launch traced here: 647 us
  Pallas kernels  390 us (60%)
  matrix products  118 us (18%)
  local copies, waits for them, and re-layouts  48.8 us (7%)
  other arithmetic  48.5 us (7%)
  starting transfers between devices  21.8 us (3%)
  between operations  16.1 us (2%)
    dot_general x10, matrix products, dot(): lax.dot_general(a, b, (((ca,), (cb,)), ((), ())), preferred_element_type=...  118 us
    pallas_call x1, Pallas kernels, tail(): pl.pallas_call(partial(tail_kernel, plan), in_specs=[any_spec] * (mats +...  116 us
    pallas_call x1, Pallas kernels, front(): pl.pallas_call(partial(front_kernel, (parts, fsdp, rows, cut, attn.shape[...  113 us
    pallas_call x1, Pallas kernels, line_reduce(): pl.pallas_call(partial(line_kernel, parts, mats, rows), in_specs=[vmem] *...  83.8 us
    pallas_call x2, Pallas kernels, wgrad(): pl.pallas_call(wgrad_kernel, grid=(-(-cols // tile),), in_specs=[pl.Block...  28.6 us
    pallas_call x1, Pallas kernels, attn_bwd(): pl.pallas_call(partial(attn_bwd_kernel, HD ** (-0.5)), grid=(heads,), in_...  26.1 us
    pallas_call x1, Pallas kernels, attn_fwd(): pl.pallas_call(partial(attn_fwd_kernel, HD ** (-0.5)), grid=(heads,), in_...  21.8 us
    ppermute x2, starting transfers between devices, far_hop(): lax.ppermute(near[0], 'tensor', up)  14.6 us
  transfers between devices with their start and end apart: 9, of which 2 were waited for; matrix products, arithmetic and copies ran while one was open for 29% of the time, Pallas kernels for 43%

profile of v4, /device:TPU:10, one launch (start us, length us, event | category | flops | bytes accessed | tf_op | source)
XLA Modules:
  0.0 646.9 jit_solution(2283581724128151625)
XLA Ops:
  8.6 6.3 concatenate.18
  17.3 113.5 %front.1 = (f32[4,32,128]{2,1,0:T(8,128)}, bf16[4,144,1076]{2,1,0:T(8,128)(2,1)}, bf16[8,144,4608]{2,1,0:T(8,128)(2,1)}, bf16[8,144,4304]{2,1,0:T(8,128)(2,1)}) custom-call(f32[32,128]{1,0:T(8,128)} %pad_bitcast_fusion.1.refs_0_, bf16[144,1152]{1,0:T(8,128)(2,1)} %pad_maximum_fusion.1.refs_1_, bf16[144,1076]{1,0:T(8,128)(2,1)} %refs_2_.1, ...), custom_call_target="tpu_custom_call" | custom-call | bytes 250000000 | tf_op jit(solution)/shard_map/front/pallas_call | solution.py:496
  138.9 12.6 %add_convert_fusion = bf16[3456,729]{0,1:T(8,128)(2,1)} fusion(bf16[1152,4608]{1,0:T(8,128)(2,1)} %bitcast.157, f32[3456]{0:T(1024)S(1)} %pad_maximum_fusion.3, f32[1152]{0:T(1024)S(1)} %add.122, f32[1152]{0:T(1024)S(1)} %mul.168, f32[729]{0:T(1024)S(1)} %add_rsqrt_fusion.1, f32[729]{0:T(1024)S(1)} %broadcast_multiply_fusion.5, ...), kind=kOutput, calls=%fused_computation.13 | convolution fusion | flops 5814831104 | bytes 14726092 | tf_op jit(solution)/shard_map/dot_general | solution.py:18
  151.5 8.1 %copy.48 = bf16[3456,729]{1,0:T(8,128)(2,1)} copy(bf16[3456,729]{0,1:T(8,128)(2,1)} %add_convert_fusion) | data formatting | bytes 10077696 | tf_op jit(solution)/shard_map/convert_element_type | solution.py:643
  161.2 21.8 %attn_fwd.1 = (bf16[1152,729]{1,0:T(8,128)(2,1)}, bf16[16,729,729]{2,1,0:T(8,128)(2,1)}, f32[16,1,729]{2,1,0:T(1,128)}, f32[16,1,128]{2,1,0:T(1,128)}) custom-call(bf16[3,1152,729]{2,1,0:T(8,128)(2,1)} %bitcast.136), custom_call_target="tpu_custom_call" | custom-call | flops 8707129344 | bytes 17006112 | tf_op jit(solution)/shard_map/attn_fwd/pallas_call | solution.py:36
  182.9 5.7 fusion.48
  189.2 2.8 select_bitcast_fusion.3.x_ref
  192.6 11.8 %multiply_convert_fusion = (bf16[729,4304]{1,0:T(8,128)(2,1)}, f32[729,4304]{1,0:T(8,128)}) fusion(f32[4304]{0:T(1024)S(1)} %add.135, bf16[729,1152]{1,0:T(8,128)(2,1)S(1)} %add_convert_fusion.1.x_ref, bf16[1152,4304]{1,0:T(8,128)(2,1)S(1)} %bitcast.164), kind=kOutput, calls=%fused_computation.12 | convolution fusion | flops 7260442624 | bytes 30438944 | tf_op jit(solution)/shard_map/dot_general | solution.py:18
  204.5 14.2 %wgrad.3 = bf16[1152,4304]{1,0:T(8,128)(2,1)} custom-call(bf16[729,1152]{1,0:T(8,128)(2,1)} %select_bitcast_fusion.3.x_ref, bf16[729,4304]{1,0:T(8,128)(2,1)} %get-tuple-element.159.y_ref), custom_call_target="tpu_custom_call" | custom-call | flops 7229067264 | bytes 16191648 | tf_op jit(solution)/shard_map/wgrad/pallas_call | solution.py:143
  219.9 14.7 %fusion.34 = bf16[729,1152]{1,0:T(8,128)(2,1)} fusion(f32[729,1152]{1,0:T(8,128)S(1)} %get-tuple-element.158, bf16[729,4304]{1,0:T(8,128)(2,1)} %get-tuple-element.159.y_ref, bf16[1152,4304]{1,0:T(8,128)(2,1)} %all-gather.2.cloned.1.call-done, f32[]{:T(128)} %bitcast.12, f32[1152]{0:T(1024)S(1)} %add.141), kind=kOutput, calls=%fused_computation.54 | convolution fusion | flops 7232425984 | bytes 21235108 | tf_op jit(solution)/shard_map/dot_general | solution.py:18
  234.6 21.5 %convert_reduce_fusion = (f32[4304]{0:T(1024)S(1)}, bf16[729,4304]{1,0:T(8,128)(2,1)}) fusion(f32[729,4304]{1,0:T(8,128)} %get-tuple-element.160, f32[4304]{0:T(1024)S(1)} %add.135, bf16[729,1152]{1,0:T(8,128)(2,1)S(1)} %copy-done.4, bf16[1152,4304]{1,0:T(8,128)(2,1)} %all-gather.2.cloned.1.call-done), kind=kOutput, calls=%fused_computation.11 | convolution fusion | flops 7298088960 | bytes 30456160 | tf_op jit(solution)/shard_map/dot_general | solution.py:18
  256.1 14.4 %wgrad.2 = bf16[1152,4304]{1,0:T(8,128)(2,1)} custom-call(bf16[729,1152]{1,0:T(8,128)(2,1)} %copy-done.7, bf16[729,4304]{1,0:T(8,128)(2,1)} %get-tuple-element.163.y_ref), custom_call_target="tpu_custom_call" | custom-call | flops 7229067264 | bytes 16191648 | tf_op jit(solution)/shard_map/wgrad/pallas_call | solution.py:143
  270.5 15.0 %fusion.49 = f32[729,1152]{1,0:T(8,128)} fusion(bf16[729,4304]{1,0:T(8,128)(2,1)} %get-tuple-element.163.y_ref, bf16[1152,4304]{1,0:T(8,128)(2,1)} %bitcast.161), kind=kOutput, calls=%fused_computation.114 | convolution fusion | flops 7229067264 | bytes 19550880 | tf_op jit(solution)/shard_map/dot_general | solution.py:18
  289.8 3.6 multiply_reduce_fusion
  295.4 5.8 convolution_convert_fusion.2
  301.3 4.3 convolution_convert_fusion.1
  308.2 26.1 %attn_bwd.1 = bf16[3,1152,729]{2,1,0:T(8,128)(2,1)} custom-call(bf16[3,1152,729]{2,1,0:T(8,128)(2,1)} %bitcast.137, bf16[1152,729]{1,0:T(8,128)(2,1)} %copy.49.do_ref, bf16[1152,729]{1,0:T(8,128)(2,1)} %get-tuple-element.51.o_ref, bf16[16,729,729]{2,1,0:T(8,128)(2,1)} %get-tuple-element.56.p_ref, f32[16,1,729]{2,1,0:T(1,128)} %get-tuple-element.57.l_ref), custom_call_target="tpu_custom_call" | custom-call | flops 17414258688 | bytes 17006112 | tf_op jit(solution)/shard_map/attn_bwd/pallas_call | solution.py:75
  338.1 9.9 %collective-permute-start.2 = (bf16[729,1152]{1,0:T(8,128)(2,1)}, bf16[729,1152]{1,0:T(8,128)(2,1)}, u32[]{:S(2)}, u32[]{:S(2)}) collective-permute-start(bf16[729,1152]{1,0:T(8,128)(2,1)} %collective-permute-done), channel_id=1, source_target_pairs={{1,2},{5,6},{9,10},{13,14},{17,18},{21,22},{25,26},{29,30}} | collective-permute-start | bytes 5038856 | tf_op jit(solution)/shard_map/ppermute | solution.py:131
  347.9 4.7 collective-permute-start.4
  356.4 7.5 %convert_element_type.123 = f32[3456,729]{1,0:T(8,128)} convert(bf16[3456,729]{1,0:T(8,128)(2,1)} %bitcast.138) | non-fusion elementwise | flops 2519424 | bytes 15116544 | tf_op jit(solution)/shard_map/convert_element_type | solution.py:676
  363.9 14.4 %fusion.32 = (f32[1152]{0:T(1024)S(1)}, f32[729]{0:T(1024)}, f32[729]{0:T(1024)}, f32[1152]{0:T(1024)S(1)}, f32[729,1152]{1,0:T(8,128)}) fusion(f32[729]{0:T(1024)S(1)} %copy-done.20, f32[729]{0:T(1024)S(1)} %copy-done.16, bf16[3,729,1152]{2,1,0:T(8,128)(2,1)} %param.16, s32[]{:T(128)S(6)} %select_n.108, f32[1152]{0:T(1024)S(1)} %copy-done.18, ...), kind=kOutput, calls=%fused_computation.46 | convolution fusion | flops 5813146624 | bytes 18081940 | tf_op jit(solution)/shard_map/dot_general | solution.py:18
  378.5 3.7 slice_reduce_fusion
  386.6 4.0 fusion.31.refs_2_
  390.6 12.1 %convolution_convert_fusion = bf16[1152,3456]{1,0:T(8,128)(2,1)} fusion(bf16[3456,729]{1,0:T(8,128)(2,1)} %bitcast.139, f32[1152]{0:T(1024)S(1)} %copy-done.22, f32[1152]{0:T(1024)S(1)} %copy-done.18, f32[729]{0:T(1024)S(1)} %copy-done.20, f32[729]{0:T(1024)S(1)} %copy-done.16, bf16[3,729,1152]{2,1,0:T(8,128)(2,1)} %param.16, s32[]{:T(128)S(6)} %select_n.108), kind=kOutput, calls=%fused_computation.2 | convolution fusion | flops 5813773312 | bytes 14981836 | tf_op jit(solution)/shard_map/dot_general | solution.py:18
  402.7 116.3 %tail.1 = (bf16[144,3456]{1,0:T(8,128)(2,1)}, bf16[144,1152]{1,0:T(8,128)(2,1)}, bf16[3,729,1152]{2,1,0:T(8,128)(2,1)}, f32[120,128]{1,0:T(8,128)}) custom-call(bf16[8,144,3456]{2,1,0:T(8,128)(2,1)} %bitcast.134, bf16[8,144,1152]{2,1,0:T(8,128)(2,1)} %bitcast.146, bf16[729,1152]{1,0:T(8,128)(2,1)} %fusion.31.refs_2_, f32[120,128]{1,0:T(8,128)} %pad_maximum_fusion.2.refs_3_), custom_call_target="tpu_custom_call" | custom-call | bytes 250000000 | tf_op jit(solution)/shard_map/tail/pallas_call | solution.py:343
  525.1 3.2 reshape.217
  533.2 2.9 fusion.39
  536.1 4.8 maximum_convert_fusion
  540.9 3.2 reshape.219
  545.3 83.8 %line_reduce.1 = (f32[144,1076]{1,0:T(8,128)}, f32[144,1076]{1,0:T(8,128)}, f32[144,864]{1,0:T(8,128)}, f32[144,288]{1,0:T(8,128)}) custom-call(bf16[4,144,1076]{2,1,0:T(8,128)(2,1)} %bitcast.143, bf16[4,144,1076]{2,1,0:T(8,128)(2,1)} %bitcast.144, bf16[4,144,864]{2,1,0:T(8,128)(2,1)} %reshape.236.refs_2_, bf16[4,144,288]{2,1,0:T(8,128)(2,1)} %bitcast.147), custom_call_target="tpu_custom_call" | custom-call | bytes 200000000 | tf_op jit(solution)/shard_map/line_reduce/pallas_call | solution.py:577
  631.7 2.9 select_bitcast_fusion.1
  634.6 3.0 pad_maximum_fusion
  (156 shorter events, 52.4 us)
Async XLA Ops:
  7.2 212.7 %all-gather.2.cloned.1.call-start = ((), (), s32[]{:S(2)}) async-start(), calls=%async_computation.2 | async-start | bytes 11280384 | tf_op jit(solution)/shard_map/all_gather | solution.py:622
  134.4 199.8 %reduce-scatter.3.cloned.1.call-start = ((), (), s32[]{:S(2)}) async-start(), calls=%async_computation.3 | async-start | bytes 11280384 | tf_op jit(solution)/shard_map/reduce_scatter | solution.py:735
  134.9 16.6 %copy-start.17 = (f32[1152]{0:T(1024)}, f32[1152]{0:T(1024)S(1)}, u32[]{:S(2)}) copy-start(f32[1152]{0:T(1024)S(1)} %mul.168) | copy-start | bytes 13828
  135.0 16.5 %copy-start.21 = (f32[1152]{0:T(1024)}, f32[1152]{0:T(1024)S(1)}, u32[]{:S(2)}) copy-start(f32[1152]{0:T(1024)S(1)} %add.122) | copy-start | bytes 13828
  138.8 12.6 %copy-start.19 = (f32[729]{0:T(1024)}, f32[729]{0:T(1024)S(1)}, u32[]{:S(2)}) copy-start(f32[729]{0:T(1024)S(1)} %add_rsqrt_fusion.1) | copy-start | bytes 8752
  151.5 8.5 %copy-start.25 = (s32[3]{0:T(128)S(1)}, s32[3]{0:T(128)}, u32[]{:S(2)}) copy-start(s32[3]{0:T(128)} %param.17) | copy-start | bytes 40
  182.9 9.7 %slice-start.2 = ((s8[10027008]{0:T(1024)(128)(4,1)}), s8[4194304]{0:T(1024)(128)(4,1)S(1)}, s32[]{:S(2)}) async-start(s8[10027008]{0:T(1024)(128)(4,1)} %bitcast.162), calls=%async_computation.7 | async-start | bytes 8388608
  182.9 9.7 %slice-start.3 = ((s8[10027008]{0:T(1024)(128)(4,1)}), s8[4194304]{0:T(1024)(128)(4,1)S(1)}, s32[]{:S(2)}) async-start(s8[10027008]{0:T(1024)(128)(4,1)} %bitcast.162), calls=%async_computation.8 | async-start | bytes 8388608
  192.6 11.9 %copy-start.7 = (bf16[729,1152]{1,0:T(8,128)(2,1)}, bf16[729,1152]{1,0:T(8,128)(2,1)S(1)}, u32[]{:S(2)}) copy-start(bf16[729,1152]{1,0:T(8,128)(2,1)S(1)} %add_convert_fusion.1.x_ref) | copy-start | bytes 5038852
  218.7 322.2 %reduce-scatter.5.cloned.1.call-start = ((), (), s32[]{:S(2)}) async-start(), calls=%async_computation.4 | async-start | bytes 11280384 | tf_op jit(solution)/shard_map/reduce_scatter | solution.py:735
  219.9 14.7 %copy-start.4 = (bf16[729,1152]{1,0:T(8,128)(2,1)S(1)}, bf16[729,1152]{1,0:T(8,128)(2,1)}, u32[]{:S(2)}) copy-start(bf16[729,1152]{1,0:T(8,128)(2,1)} %select_bitcast_fusion.3.x_ref) | copy-start | bytes 5038852
  287.0 6.4 copy-start.3
  287.0 6.5 copy-start.5
  287.0 49.9 %collective-permute-start = (bf16[729,1152]{1,0:T(8,128)(2,1)}, bf16[729,1152]{1,0:T(8,128)(2,1)}, u32[]{:S(2)}, u32[]{:S(2)}) collective-permute-start(bf16[729,1152]{1,0:T(8,128)(2,1)} %fusion.34), channel_id=1, source_target_pairs={{0,1},{2,3},{4,5},{6,7},{8,9},{10,11},{12,13},{14,15},{16,17},{18,... | collective-permute-start | bytes 5038856 | tf_op jit(solution)/shard_map/ppermute | solution.py:123
  288.5 49.5 %collective-permute-start.1 = (bf16[729,1152]{1,0:T(8,128)(2,1)}, bf16[729,1152]{1,0:T(8,128)(2,1)}, u32[]{:S(2)}, u32[]{:S(2)}) collective-permute-start(bf16[729,1152]{1,0:T(8,128)(2,1)} %fusion.34), channel_id=1, source_target_pairs={{2,1},{3,2},{6,5},{7,6},{10,9},{11,10},{14,13},{15,14},{18,17},{19... | collective-permute-start | bytes 5038856 | tf_op jit(solution)/shard_map/ppermute | solution.py:123
  295.4 5.8 copy-start.1
  295.4 5.8 copy-start.26
  338.0 25.8 %slice-start = ((s8[5308416]{0:T(1024)(128)(4,1)}), s8[4194304]{0:T(1024)(128)(4,1)S(1)}, s32[]{:S(2)}) async-start(s8[5308416]{0:T(1024)(128)(4,1)} %bitcast.140), calls=%async_computation.5 | async-start | bytes 8388608
  338.0 25.8 %slice-start.1 = ((s8[5308416]{0:T(1024)(128)(4,1)}), s8[1114112]{0:T(1024)(128)(4,1)S(1)}, s32[]{:S(2)}) async-start(s8[5308416]{0:T(1024)(128)(4,1)} %bitcast.140), calls=%async_computation.6 | async-start | bytes 2228224
  338.0 25.8 %copy-start.16 = (f32[729]{0:T(1024)S(1)}, f32[729]{0:T(1024)}, u32[]{:S(2)}) copy-start(f32[729]{0:T(1024)} %copy-done.15) | copy-start | bytes 8752
  338.0 25.8 %copy-start.18 = (f32[1152]{0:T(1024)S(1)}, f32[1152]{0:T(1024)}, u32[]{:S(2)}) copy-start(f32[1152]{0:T(1024)} %copy-done.17) | copy-start | bytes 13828
  338.1 25.8 %copy-start.20 = (f32[729]{0:T(1024)S(1)}, f32[729]{0:T(1024)}, u32[]{:S(2)}) copy-start(f32[729]{0:T(1024)} %copy-done.19) | copy-start | bytes 8752
  338.1 291.1 %collective-permute-start.2 = (bf16[729,1152]{1,0:T(8,128)(2,1)}, bf16[729,1152]{1,0:T(8,128)(2,1)}, u32[]{:S(2)}, u32[]{:S(2)}) collective-permute-start(bf16[729,1152]{1,0:T(8,128)(2,1)} %collective-permute-done), channel_id=1, source_target_pairs={{1,2},{5,6},{9,10},{13,14},{17,18},{21,22},{25,26},{29,30}} | collective-permute-start | bytes 5038856 | tf_op jit(solution)/shard_map/ppermute | solution.py:131
  347.9 281.2 %collective-permute-start.4 = (bf16[729,1152]{1,0:T(8,128)(2,1)}, bf16[729,1152]{1,0:T(8,128)(2,1)}, u32[]{:S(2)}, u32[]{:S(2)}) collective-permute-start(bf16[729,1152]{1,0:T(8,128)(2,1)} %collective-permute-done), channel_id=1, source_target_pairs={{1,3},{5,7},{9,11},{13,15},{17,19},{21,23},{25,27},{29,31}} | collective-permute-start | bytes 5038856 | tf_op jit(solution)/shard_map/ppermute | solution.py:131
  352.6 276.5 %collective-permute-start.3 = (bf16[729,1152]{1,0:T(8,128)(2,1)}, bf16[729,1152]{1,0:T(8,128)(2,1)}, u32[]{:S(2)}, u32[]{:S(2)}) collective-permute-start(bf16[729,1152]{1,0:T(8,128)(2,1)} %collective-permute-done.1), channel_id=1, source_target_pairs={{1,0},{2,1},{5,4},{6,5},{9,8},{10,9},{13,12},{14,13},{17,16},{18,1... | collective-permute-start | bytes 5038856 | tf_op jit(solution)/shard_map/ppermute | solution.py:132
  354.6 274.6 %collective-permute-start.5 = (bf16[729,1152]{1,0:T(8,128)(2,1)}, bf16[729,1152]{1,0:T(8,128)(2,1)}, u32[]{:S(2)}, u32[]{:S(2)}) collective-permute-start(bf16[729,1152]{1,0:T(8,128)(2,1)} %collective-permute-done.1), channel_id=1, source_target_pairs={{2,0},{6,4},{10,8},{14,12},{18,16},{22,20},{26,24},{30,28}} | collective-permute-start | bytes 5038856 | tf_op jit(solution)/shard_map/ppermute | solution.py:132
  378.5 8.1 %copy-start.2 = (f32[729,1152]{1,0:T(8,128)S(1)}, f32[729,1152]{1,0:T(8,128)}, u32[]{:S(2)}) copy-start(f32[729,1152]{1,0:T(8,128)} %copy-done.1) | copy-start | bytes 10077700
  523.9 5.7 copy-start.14
  524.3 7.6 %copy-start.8 = (bf16[3,144,288]{2,1,0:T(8,128)(2,1)S(1)}, bf16[3,144,288]{2,1,0:T(8,128)(2,1)}, u32[]{:S(2)}) copy-start(bf16[3,144,288]{2,1,0:T(8,128)(2,1)} %param.20) | copy-start | bytes 746500
  524.3 8.3 %copy-start.24 = (bf16[288]{0:T(512)(128)(2,1)S(1)}, bf16[288]{0:T(512)(128)(2,1)}, u32[]{:S(2)}) copy-start(bf16[288]{0:T(512)(128)(2,1)} %param.21) | copy-start | bytes 1732
  524.3 8.9 %copy-start = (bf16[729,1152]{1,0:T(8,128)(2,1)S(1)}, bf16[729,1152]{1,0:T(8,128)(2,1)}, u32[]{:S(2)}) copy-start(bf16[729,1152]{1,0:T(8,128)(2,1)} %fusion.31.refs_2_) | copy-start | bytes 5038852
  545.3 86.4 %copy-start.6 = (bf16[729,1152]{1,0:T(8,128)(2,1)S(1)}, bf16[729,1152]{1,0:T(8,128)(2,1)}, u32[]{:S(2)}) copy-start(bf16[729,1152]{1,0:T(8,128)(2,1)} %fusion.34) | copy-start | bytes 5038852
  (9 other events, 28.6 us)
Sparse Core Ops, SparseCore 0:
  134.5 68.3 all-gather.1
  218.8 87.7 reduce-scatter.2
  310.2 79.5 reduce-scatter.4

commit v5 on v4

--- a/solution.py
+++ b/solution.py
@@ -89,6 +89,29 @@
             transcendentals=0),
         name="attn_bwd",
     )(qkv, do, o, p, l)
+
+
+def project_kernel(w_ref, a_ref, bias_ref, out_ref):
+    out_ref[...] = (dot(w_ref[...], a_ref[...], 0, 1) + bias_ref[...]).astype(BF16)
+
+
+def project(w, a, bias, tile=384):
+    length, width = a.shape
+    count = bias.shape[0]
+    return pl.pallas_call(
+        project_kernel,
+        grid=(-(-count // tile),),
+        in_specs=[
+            pl.BlockSpec((width, tile), lambda i: (0, i)),
+            pl.BlockSpec((length, width), lambda i: (0, 0)),
+            pl.BlockSpec((tile, 1), lambda i: (i, 0)),
+        ],
+        out_specs=pl.BlockSpec((tile, length), lambda i: (i, 0)),
+        out_shape=jax.ShapeDtypeStruct((count, length), BF16),
+        cost_estimate=pl.CostEstimate(
+            flops=2 * length * width * count, bytes_accessed=2 * (length + width) * count, transcendentals=0),
+        name="project",
+    )(w, a, bias[:, None])
 
 
 def norm(rows, gain, shift):
@@ -640,7 +663,7 @@
 
     normed_one, inverse_one, a_one = norm(image, gain_one, bias_one)
     qkv_bias = jnp.concatenate([bias_q, jnp.zeros_like(bias_q), bias_v])
-    qkv = (dot(qkv_full, a_one, 0, 1) + qkv_bias[:, None]).astype(BF16).reshape(3, inner, length)
+    qkv = project(attn_full, a_one, qkv_bias).reshape(3, inner, length)
     heads_t, probs, totals, peaks = attn_fwd(qkv, heads)
     resid = image + dot(heads_t, out_full, 0, 1) + bias_out
     normed_two, inverse_two, a_two = norm(resid, gain_two, bias_two)
@@ -659,15 +682,15 @@
     d_pre = (dot(error, down_full, 1, 0) * slope).astype(BF16)
     g_up = wgrad(a_two, d_pre)
     d_two = dot(d_pre, up_full, 1, 1)
-    d_two, g_up, g_down = lax.optimization_barrier((d_two, g_up, g_down))
+    d_two, g_up, g_down, near = lax.optimization_barrier((d_two, g_up, g_down, near))
+    hops = [None, near] + [far_hop(near, d, owners) for d in range(2, parts)]
     up_err = error.astype(F32)
     d_resid = up_err + norm_back(d_two, normed_two, inverse_two, gain_two)
     d_attn = d_resid.astype(BF16)
     g_out = dot(d_attn, heads_t, 0, 1).astype(BF16)
     d_heads = dot(out_full, d_attn, 0, 1).astype(BF16)
     d_qkv = attn_bwd(qkv, d_heads, heads_t, probs, totals, heads).reshape(3 * inner, length)
-    d_qkv, near, s_down = lax.optimization_barrier((d_qkv, near, s_down))
-    hops = [None, near] + [far_hop(near, d, owners) for d in range(2, parts)]
+    d_qkv, s_down = lax.optimization_barrier((d_qkv, s_down))
     g_qkv = dot(a_one, d_qkv, 0, 1).astype(BF16)
     d_one = dot(d_qkv, qkv_full, 0, 1)
     d_image = d_resid + norm_back(d_one, normed_one, inverse_one, gain_one)

time: 653 us -> 631 us (0.966)
  matrix products: 118 us -> 105 us
  Pallas kernels: 390 us -> 383 us
    pallas_call x1, Pallas kernels: 116 us -> 99.3 us  [tail(): pl.pallas_call(partial(tail_kernel, plan), in_specs=[any_spec] * (mats +...]
    pallas_call x0 -> x1, Pallas kernels: none -> 13.6 us  [project(): pl.pallas_call(project_kernel, grid=(-(-count // tile),), in_specs=[pl.Bl...]
    dot_general x10 -> x9, matrix products: 118 us -> 105 us  [dot(): lax.dot_general(a, b, (((ca,), (cb,)), ((), ())), preferred_element_type=...]
    convert_element_type x1 -> x0, local copies, waits for them, and re-layouts: 8.12 us -> none  [on_device(): (dot(qkv_full, a_one, 0, 1) + qkv_bias[:, None]).astype(BF16)]
  transfers between devices with their start and end apart: 9 -> 9, of which waited for: 2 -> 0; matrix products, arithmetic and copies ran while one was open for 29% -> 28% of each run, Pallas kernels for 43% -> 43%
where the time goes in v5:
time: 631 us; the launch traced here: 625 us
  Pallas kernels  383 us (61%)
  matrix products  105 us (17%)
  other arithmetic  51.2 us (8%)
  local copies, waits for them, and re-layouts  44.8 us (7%)
  starting transfers between devices  24.7 us (4%)
  between operations  15.9 us (3%)
    pallas_call x1, Pallas kernels, front(): pl.pallas_call(partial(front_kernel, (parts, fsdp, rows, cut, attn.shape[...  113 us
    dot_general x9, matrix products, dot(): lax.dot_general(a, b, (((ca,), (cb,)), ((), ())), preferred_element_type=...  105 us
    pallas_call x1, Pallas kernels, tail(): pl.pallas_call(partial(tail_kernel, plan), in_specs=[any_spec] * (mats +...  99.3 us
    pallas_call x1, Pallas kernels, line_reduce(): pl.pallas_call(partial(line_kernel, parts, mats, rows), in_specs=[vmem] *...  81.4 us
    pallas_call x2, Pallas kernels, wgrad(): pl.pallas_call(wgrad_kernel, grid=(-(-cols // tile),), in_specs=[pl.Block...  28.6 us
    pallas_call x1, Pallas kernels, attn_bwd(): pl.pallas_call(partial(attn_bwd_kernel, HD ** (-0.5)), grid=(heads,), in_...  25.3 us
    pallas_call x1, Pallas kernels, attn_fwd(): pl.pallas_call(partial(attn_fwd_kernel, HD ** (-0.5)), grid=(heads,), in_...  21.8 us
    ppermute x2, starting transfers between devices, far_hop(): lax.ppermute(near[0], 'tensor', up)  17.4 us
  transfers between devices with their start and end apart: 9, of which 0 were waited for; matrix products, arithmetic and copies ran while one was open for 28% of the time, Pallas kernels for 43%

profile of v5, /device:TPU:10, one launch (start us, length us, event | category | flops | bytes accessed | tf_op | source)
XLA Modules:
  0.0 625.2 jit_solution(15717394324217162839)
XLA Ops:
  8.6 6.3 %concatenate.18 = f32[3380]{0:T(1024)S(1)} concatenate(bf16[288]{0:T(512)(128)(2,1)} %param.18, bf16[288]{0:T(512)(128)(2,1)} %param.19, bf16[288]{0:T(512)(128)(2,1)} %param.21, bf16[288]{0:T(512)(128)(2,1)} %param.22, bf16[288]{0:T(512)(128)(2,1)} %param.24, bf16[288]{0:T(512)(128)(2,1)} %param.25, bf16[288]{0:T(512)(128)(2,1)} %param.26, bf16[288]{0:T(512)(128)(2,1)} %param.30, ...), dimensions={0} | concatenate | bytes 20280 | tf_op jit(solution)/shard_map/concatenate | solution.py:634
  17.3 113.5 %front.1 = (f32[4,32,128]{2,1,0:T(8,128)}, bf16[4,144,1076]{2,1,0:T(8,128)(2,1)}, bf16[8,144,4608]{2,1,0:T(8,128)(2,1)}, bf16[8,144,4304]{2,1,0:T(8,128)(2,1)}) custom-call(f32[32,128]{1,0:T(8,128)} %pad_bitcast_fusion.1.refs_0_, bf16[144,1152]{1,0:T(8,128)(2,1)} %pad_maximum_fusion.1.refs_1_, bf16[144,1076]{1,0:T(8,128)(2,1)} %refs_2_.1, ...), custom_call_target="tpu_custom_call" | custom-call | bytes 250000000 | tf_op jit(solution)/shard_map/front/pallas_call | solution.py:519
  142.3 3.4 fusion.22.a_ref
  145.7 13.6 %project.1 = bf16[3456,729]{1,0:T(8,128)(2,1)} custom-call(bf16[1152,4608]{1,0:T(8,128)(2,1)} %bitcast.152, bf16[729,1152]{1,0:T(8,128)(2,1)} %fusion.22.a_ref, f32[3456,1]{1,0:T(8,128)} %broadcast_in_dim.29.bias_ref), custom_call_target="tpu_custom_call" | custom-call | flops 5804752896 | bytes 13001472 | tf_op jit(solution)/shard_map/project/pallas_call | solution.py:101
  159.3 21.8 %attn_fwd.1 = (bf16[1152,729]{1,0:T(8,128)(2,1)}, bf16[16,729,729]{2,1,0:T(8,128)(2,1)}, f32[16,1,729]{2,1,0:T(1,128)}, f32[16,1,128]{2,1,0:T(1,128)}) custom-call(bf16[3,1152,729]{2,1,0:T(8,128)(2,1)} %bitcast.160), custom_call_target="tpu_custom_call" | custom-call | flops 8707129344 | bytes 17006112 | tf_op jit(solution)/shard_map/attn_fwd/pallas_call | solution.py:36
  181.1 5.8 fusion.42
  187.4 2.8 select_bitcast_fusion.3.x_ref
  190.9 11.9 %multiply_convert_fusion = (bf16[729,4304]{1,0:T(8,128)(2,1)}, f32[729,4304]{1,0:T(8,128)}) fusion(f32[4304]{0:T(1024)S(1)} %add.125, bf16[729,1152]{1,0:T(8,128)(2,1)S(1)} %add_convert_fusion.x_ref, bf16[1152,4304]{1,0:T(8,128)(2,1)S(1)} %bitcast.159), kind=kOutput, calls=%fused_computation.12 | convolution fusion | flops 7260442624 | bytes 30438944 | tf_op jit(solution)/shard_map/dot_general | solution.py:18
  202.8 14.2 %wgrad.3 = bf16[1152,4304]{1,0:T(8,128)(2,1)} custom-call(bf16[729,1152]{1,0:T(8,128)(2,1)} %select_bitcast_fusion.3.x_ref, bf16[729,4304]{1,0:T(8,128)(2,1)} %get-tuple-element.159.y_ref), custom_call_target="tpu_custom_call" | custom-call | flops 7229067264 | bytes 16191648 | tf_op jit(solution)/shard_map/wgrad/pallas_call | solution.py:166
  218.0 14.7 %fusion.30 = bf16[729,1152]{1,0:T(8,128)(2,1)} fusion(f32[729,1152]{1,0:T(8,128)S(1)} %get-tuple-element.158, bf16[729,4304]{1,0:T(8,128)(2,1)} %get-tuple-element.159.y_ref, bf16[1152,4304]{1,0:T(8,128)(2,1)} %all-gather.2.cloned.1.call-done, f32[]{:T(128)} %bitcast.12, f32[1152]{0:T(1024)S(1)} %add.131), kind=kOutput, calls=%fused_computation.51 | convolution fusion | flops 7232425984 | bytes 21235108 | tf_op jit(solution)/shard_map/dot_general | solution.py:18
  235.3 21.0 %convert_reduce_fusion = (f32[4304]{0:T(1024)S(1)}, bf16[729,4304]{1,0:T(8,128)(2,1)}) fusion(f32[729,4304]{1,0:T(8,128)} %get-tuple-element.160, f32[4304]{0:T(1024)S(1)} %add.125, bf16[729,1152]{1,0:T(8,128)(2,1)S(1)} %copy-done.4, bf16[1152,4304]{1,0:T(8,128)(2,1)} %all-gather.2.cloned.1.call-done), kind=kOutput, calls=%fused_computation.11 | convolution fusion | flops 7298088960 | bytes 30456160 | tf_op jit(solution)/shard_map/dot_general | solution.py:18
  256.3 14.4 %wgrad.2 = bf16[1152,4304]{1,0:T(8,128)(2,1)} custom-call(bf16[729,1152]{1,0:T(8,128)(2,1)} %copy-done.9, bf16[729,4304]{1,0:T(8,128)(2,1)} %get-tuple-element.163.y_ref), custom_call_target="tpu_custom_call" | custom-call | flops 7229067264 | bytes 16191648 | tf_op jit(solution)/shard_map/wgrad/pallas_call | solution.py:166
  270.7 14.9 %fusion.43 = f32[729,1152]{1,0:T(8,128)} fusion(bf16[729,4304]{1,0:T(8,128)(2,1)} %get-tuple-element.163.y_ref, bf16[1152,4304]{1,0:T(8,128)(2,1)} %bitcast.156), kind=kOutput, calls=%fused_computation.111 | convolution fusion | flops 7229067264 | bytes 19550880 | tf_op jit(solution)/shard_map/dot_general | solution.py:18
  287.2 13.1 %collective-permute-start.2 = (bf16[729,1152]{1,0:T(8,128)(2,1)}, bf16[729,1152]{1,0:T(8,128)(2,1)}, u32[]{:S(2)}, u32[]{:S(2)}) collective-permute-start(bf16[729,1152]{1,0:T(8,128)(2,1)} %collective-permute-done), channel_id=1, source_target_pairs={{1,2},{5,6},{9,10},{13,14},{17,18},{21,22},{25,26},{29,30}} | collective-permute-start | bytes 5038856 | tf_op jit(solution)/shard_map/ppermute | solution.py:154
  300.4 4.3 collective-permute-start.4
  308.8 3.4 multiply_reduce_fusion
  315.8 5.2 convolution_convert_fusion.2
  323.3 25.3 %attn_bwd.1 = bf16[3,1152,729]{2,1,0:T(8,128)(2,1)} custom-call(bf16[3,1152,729]{2,1,0:T(8,128)(2,1)} %bitcast.161, bf16[1152,729]{1,0:T(8,128)(2,1)} %copy.48.do_ref, bf16[1152,729]{1,0:T(8,128)(2,1)} %get-tuple-element.51.o_ref, bf16[16,729,729]{2,1,0:T(8,128)(2,1)} %get-tuple-element.57.p_ref, f32[16,1,729]{2,1,0:T(1,128)} %get-tuple-element.58.l_ref), custom_call_target="tpu_custom_call" | custom-call | flops 17414258688 | bytes 17006112 | tf_op jit(solution)/shard_map/attn_bwd/pallas_call | solution.py:75
  348.6 7.5 %convert_element_type.119 = f32[3456,729]{1,0:T(8,128)} convert(bf16[3456,729]{1,0:T(8,128)(2,1)} %bitcast.135) | non-fusion elementwise | flops 2519424 | bytes 15116544 | tf_op jit(solution)/shard_map/convert_element_type | solution.py:699
  356.1 14.4 %fusion.28 = (f32[1152]{0:T(1024)S(1)}, f32[729]{0:T(1024)}, f32[729]{0:T(1024)}, f32[1152]{0:T(1024)S(1)}, f32[729,1152]{1,0:T(8,128)}) fusion(f32[729]{0:T(1024)S(1)} %copy-done.23, f32[729]{0:T(1024)S(1)} %copy-done.19, bf16[3,729,1152]{2,1,0:T(8,128)(2,1)} %param.16, s32[]{:T(128)S(6)} %select_n.108, f32[1152]{0:T(1024)S(1)} %copy-done.17, ...), kind=kOutput, calls=%fused_computation.43 | convolution fusion | flops 5813146624 | bytes 18081940 | tf_op jit(solution)/shard_map/dot_general | solution.py:18
  370.7 3.6 slice_reduce_fusion
  379.7 5.8 convolution_convert_fusion.1
  385.5 3.8 fusion.27.refs_2_
  389.3 11.2 %convolution_convert_fusion = bf16[1152,3456]{1,0:T(8,128)(2,1)} fusion(bf16[729,1152]{1,0:T(8,128)(2,1)S(1)} %copy-done.10, bf16[3456,729]{1,0:T(8,128)(2,1)} %bitcast.136), kind=kOutput, calls=%fused_computation.2 | convolution fusion | flops 5808734208 | bytes 14681088 | tf_op jit(solution)/shard_map/dot_general | solution.py:18
  400.5 99.3 %tail.1 = (bf16[144,3456]{1,0:T(8,128)(2,1)}, bf16[144,1152]{1,0:T(8,128)(2,1)}, bf16[3,729,1152]{2,1,0:T(8,128)(2,1)}, f32[120,128]{1,0:T(8,128)}) custom-call(bf16[8,144,3456]{2,1,0:T(8,128)(2,1)} %bitcast.133, bf16[8,144,1152]{2,1,0:T(8,128)(2,1)} %bitcast.141, bf16[729,1152]{1,0:T(8,128)(2,1)} %fusion.27.refs_2_, f32[120,128]{1,0:T(8,128)} %pad_maximum_fusion.2.refs_3_), custom_call_target="tpu_custom_call" | custom-call | bytes 250000000 | tf_op jit(solution)/shard_map/tail/pallas_call | solution.py:366
  505.9 3.2 reshape.216
  514.0 2.9 fusion.35
  516.9 4.8 maximum_convert_fusion
  521.7 3.2 reshape.218
  526.2 81.4 %line_reduce.1 = (f32[144,1076]{1,0:T(8,128)}, f32[144,1076]{1,0:T(8,128)}, f32[144,864]{1,0:T(8,128)}, f32[144,288]{1,0:T(8,128)}) custom-call(bf16[4,144,1076]{2,1,0:T(8,128)(2,1)} %bitcast.138, bf16[4,144,1076]{2,1,0:T(8,128)(2,1)} %bitcast.139, bf16[4,144,864]{2,1,0:T(8,128)(2,1)} %reshape.235.refs_2_, bf16[4,144,288]{2,1,0:T(8,128)(2,1)} %bitcast.142), custom_call_target="tpu_custom_call" | custom-call | bytes 200000000 | tf_op jit(solution)/shard_map/line_reduce/pallas_call | solution.py:600
  610.2 2.9 select_bitcast_fusion.1
  613.1 3.0 pad_maximum_fusion
  (152 shorter events, 52.7 us)
Async XLA Ops:
  7.2 210.8 %all-gather.2.cloned.1.call-start = ((), (), s32[]{:S(2)}) async-start(), calls=%async_computation.2 | async-start | bytes 11280384 | tf_op jit(solution)/shard_map/all_gather | solution.py:645
  132.2 5.0 copy-start.26
  134.4 214.2 %reduce-scatter.3.cloned.1.call-start = ((), (), s32[]{:S(2)}) async-start(), calls=%async_computation.3 | async-start | bytes 11280384 | tf_op jit(solution)/shard_map/reduce_scatter | solution.py:758
  134.9 10.8 %copy-start.16 = (f32[1152]{0:T(1024)}, f32[1152]{0:T(1024)S(1)}, u32[]{:S(2)}) copy-start(f32[1152]{0:T(1024)S(1)} %mul.168) | copy-start | bytes 13828
  140.2 19.1 %copy-start.18 = (f32[729]{0:T(1024)}, f32[729]{0:T(1024)S(1)}, u32[]{:S(2)}) copy-start(f32[729]{0:T(1024)S(1)} %broadcast_multiply_fusion.5) | copy-start | bytes 8752
  142.3 17.0 %copy-start.22 = (f32[729]{0:T(1024)}, f32[729]{0:T(1024)S(1)}, u32[]{:S(2)}) copy-start(f32[729]{0:T(1024)S(1)} %add_rsqrt_fusion.1) | copy-start | bytes 8752
  181.1 9.8 %slice-start = ((s8[10027008]{0:T(1024)(128)(4,1)}), s8[4194304]{0:T(1024)(128)(4,1)S(1)}, s32[]{:S(2)}) async-start(s8[10027008]{0:T(1024)(128)(4,1)} %bitcast.157), calls=%async_computation.5 | async-start | bytes 8388608
  181.1 9.8 %slice-start.1 = ((s8[10027008]{0:T(1024)(128)(4,1)}), s8[4194304]{0:T(1024)(128)(4,1)S(1)}, s32[]{:S(2)}) async-start(s8[10027008]{0:T(1024)(128)(4,1)} %bitcast.157), calls=%async_computation.6 | async-start | bytes 8388608
  186.9 3.9 slice-start.2
  190.8 12.0 %copy-start.9 = (bf16[729,1152]{1,0:T(8,128)(2,1)}, bf16[729,1152]{1,0:T(8,128)(2,1)S(1)}, u32[]{:S(2)}) copy-start(bf16[729,1152]{1,0:T(8,128)(2,1)S(1)} %add_convert_fusion.x_ref) | copy-start | bytes 5038852
  217.0 304.7 %reduce-scatter.5.cloned.1.call-start = ((), (), s32[]{:S(2)}) async-start(), calls=%async_computation.4 | async-start | bytes 11280384 | tf_op jit(solution)/shard_map/reduce_scatter | solution.py:758
  218.0 17.3 %copy-start.4 = (bf16[729,1152]{1,0:T(8,128)(2,1)S(1)}, bf16[729,1152]{1,0:T(8,128)(2,1)}, u32[]{:S(2)}) copy-start(bf16[729,1152]{1,0:T(8,128)(2,1)} %select_bitcast_fusion.3.x_ref) | copy-start | bytes 5038852
  232.7 52.9 %collective-permute-start = (bf16[729,1152]{1,0:T(8,128)(2,1)}, bf16[729,1152]{1,0:T(8,128)(2,1)}, u32[]{:S(2)}, u32[]{:S(2)}) collective-permute-start(bf16[729,1152]{1,0:T(8,128)(2,1)} %fusion.30), channel_id=1, source_target_pairs={{0,1},{2,3},{4,5},{6,7},{8,9},{10,11},{12,13},{14,15},{16,17},{18,... | collective-permute-start | bytes 5038856 | tf_op jit(solution)/shard_map/ppermute | solution.py:146
  234.0 51.6 %collective-permute-start.1 = (bf16[729,1152]{1,0:T(8,128)(2,1)}, bf16[729,1152]{1,0:T(8,128)(2,1)}, u32[]{:S(2)}, u32[]{:S(2)}) collective-permute-start(bf16[729,1152]{1,0:T(8,128)(2,1)} %fusion.30), channel_id=1, source_target_pairs={{2,1},{3,2},{6,5},{7,6},{10,9},{11,10},{14,13},{15,14},{18,17},{19... | collective-permute-start | bytes 5038856 | tf_op jit(solution)/shard_map/ppermute | solution.py:146
  287.2 25.0 %copy-start.1 = (f32[729,1152]{1,0:T(8,128)S(1)}, f32[729,1152]{1,0:T(8,128)}, u32[]{:S(2)}) copy-start(f32[729,1152]{1,0:T(8,128)} %fusion.43) | copy-start | bytes 10077700
  287.2 25.0 %copy-start.5 = (bf16[729,1152]{1,0:T(8,128)(2,1)S(1)}, bf16[729,1152]{1,0:T(8,128)(2,1)}, u32[]{:S(2)}) copy-start(bf16[729,1152]{1,0:T(8,128)(2,1)} %select_bitcast_fusion.3.x_ref) | copy-start | bytes 5038852
  287.2 320.4 %collective-permute-start.2 = (bf16[729,1152]{1,0:T(8,128)(2,1)}, bf16[729,1152]{1,0:T(8,128)(2,1)}, u32[]{:S(2)}, u32[]{:S(2)}) collective-permute-start(bf16[729,1152]{1,0:T(8,128)(2,1)} %collective-permute-done), channel_id=1, source_target_pairs={{1,2},{5,6},{9,10},{13,14},{17,18},{21,22},{25,26},{29,30}} | collective-permute-start | bytes 5038856 | tf_op jit(solution)/shard_map/ppermute | solution.py:154
  300.4 307.3 %collective-permute-start.4 = (bf16[729,1152]{1,0:T(8,128)(2,1)}, bf16[729,1152]{1,0:T(8,128)(2,1)}, u32[]{:S(2)}, u32[]{:S(2)}) collective-permute-start(bf16[729,1152]{1,0:T(8,128)(2,1)} %collective-permute-done), channel_id=1, source_target_pairs={{1,3},{5,7},{9,11},{13,15},{17,19},{21,23},{25,27},{29,31}} | collective-permute-start | bytes 5038856 | tf_op jit(solution)/shard_map/ppermute | solution.py:154
  304.7 303.0 %collective-permute-start.3 = (bf16[729,1152]{1,0:T(8,128)(2,1)}, bf16[729,1152]{1,0:T(8,128)(2,1)}, u32[]{:S(2)}, u32[]{:S(2)}) collective-permute-start(bf16[729,1152]{1,0:T(8,128)(2,1)} %collective-permute-done.1), channel_id=1, source_target_pairs={{1,0},{2,1},{5,4},{6,5},{9,8},{10,9},{13,12},{14,13},{17,16},{18,1... | collective-permute-start | bytes 5038856 | tf_op jit(solution)/shard_map/ppermute | solution.py:155
  306.6 301.1 %collective-permute-start.5 = (bf16[729,1152]{1,0:T(8,128)(2,1)}, bf16[729,1152]{1,0:T(8,128)(2,1)}, u32[]{:S(2)}, u32[]{:S(2)}) collective-permute-start(bf16[729,1152]{1,0:T(8,128)(2,1)} %collective-permute-done.1), channel_id=1, source_target_pairs={{2,0},{6,4},{10,8},{14,12},{18,16},{22,20},{26,24},{30,28}} | collective-permute-start | bytes 5038856 | tf_op jit(solution)/shard_map/ppermute | solution.py:155
  348.6 7.5 %copy-start.6 = (bf16[3,1152,729]{2,1,0:T(8,128)(2,1)S(1)}, bf16[3,1152,729]{2,1,0:T(8,128)(2,1)}, u32[]{:S(2)}) copy-start(bf16[3,1152,729]{2,1,0:T(8,128)(2,1)} %attn_bwd.1) | copy-start | bytes 15116548
  348.6 7.5 %copy-start.17 = (f32[1152]{0:T(1024)S(1)}, f32[1152]{0:T(1024)}, u32[]{:S(2)}) copy-start(f32[1152]{0:T(1024)} %copy-done.16) | copy-start | bytes 13828
  348.6 7.5 %copy-start.19 = (f32[729]{0:T(1024)S(1)}, f32[729]{0:T(1024)}, u32[]{:S(2)}) copy-start(f32[729]{0:T(1024)} %copy-done.18) | copy-start | bytes 8752
  348.6 7.5 %copy-start.23 = (f32[729]{0:T(1024)S(1)}, f32[729]{0:T(1024)}, u32[]{:S(2)}) copy-start(f32[729]{0:T(1024)} %copy-done.22) | copy-start | bytes 8752
  370.7 9.0 %copy-start.3 = (f32[729,1152]{1,0:T(8,128)S(1)}, f32[729,1152]{1,0:T(8,128)}, u32[]{:S(2)}) copy-start(f32[729,1152]{1,0:T(8,128)} %copy-done.2) | copy-start | bytes 10077700
  379.7 5.8 copy-start.7
  504.7 5.7 copy-start.21
  505.1 7.5 %copy-start.11 = (bf16[3,144,288]{2,1,0:T(8,128)(2,1)S(1)}, bf16[3,144,288]{2,1,0:T(8,128)(2,1)}, u32[]{:S(2)}) copy-start(bf16[3,144,288]{2,1,0:T(8,128)(2,1)} %param.20) | copy-start | bytes 746500
  505.1 8.3 %copy-start.25 = (bf16[288]{0:T(512)(128)(2,1)S(1)}, bf16[288]{0:T(512)(128)(2,1)}, u32[]{:S(2)}) copy-start(bf16[288]{0:T(512)(128)(2,1)} %param.21) | copy-start | bytes 1732
  505.1 8.9 %copy-start = (bf16[729,1152]{1,0:T(8,128)(2,1)S(1)}, bf16[729,1152]{1,0:T(8,128)(2,1)}, u32[]{:S(2)}) copy-start(bf16[729,1152]{1,0:T(8,128)(2,1)} %fusion.27.refs_2_) | copy-start | bytes 5038852
  526.2 84.0 %copy-start.8 = (bf16[729,1152]{1,0:T(8,128)(2,1)S(1)}, bf16[729,1152]{1,0:T(8,128)(2,1)}, u32[]{:S(2)}) copy-start(bf16[729,1152]{1,0:T(8,128)(2,1)} %fusion.30) | copy-start | bytes 5038852
  613.0 4.5 copy-start.12
  (7 other events, 19.7 us)
Sparse Core Ops, SparseCore 0:
  134.5 68.3 all-gather.1
  217.1 86.7 reduce-scatter.2
  307.5 79.5 reduce-scatter.4
